TPU v7x, 32 devices: a whole 2x2x4 slice. The times are simulated.
32 devices in a mesh: batch: 4 (over z), seq: 8 (over y, x, core).
Axes of the slice: x: 2, y: 2, z: 4, core: 2. Of those that a mesh axis runs over, the one named last changes fastest.
Arguments:
- inputs: bfloat16 [4, 1024, 1024], P('batch', 'seq'), may hold values from -6 to 6
- lengths: int32 [4], P('batch'), may hold values from 256 to 1024, as said below
- adapter_index: int32 [4], P('batch'), may hold values from 0 to 7
- memory_picks: int32 [4, 1024, 4, 32], P('batch', 'seq'), may hold values from 0 to 65535, as said below
- input_weights: bfloat16 [5, 1024, 1024], replicated, may hold values from -0.1875 to 0.1875
- output_weights: bfloat16 [2, 1024, 1024], replicated, may hold values from -0.75 to 0.75
- adapter_down: bfloat16 [7, 8, 1024, 16], replicated, may hold values from -0.1875 to 0.1875
- adapter_up: bfloat16 [7, 8, 16, 1024], replicated, may hold values from -0.75 to 0.75
- attention_gain: bfloat16 [1024], replicated, may hold values from 0.099609375 to 1.8984375
- memory_gain: bfloat16 [1024], replicated, may hold values from 0.099609375 to 1.8984375
- half_keys: bfloat16 [2, 4, 256, 128], replicated, may hold values from -0.5 to 0.5
- memory_values: bfloat16 [65536, 1024], P(('batch', 'seq')), may hold values from -6 to 6
- cotangent: bfloat16 [4, 1024, 1024], P('batch', 'seq'), may hold values from -6 to 6
Outputs:
- output: bfloat16 [4, 1024, 1024], P('batch', 'seq')
- grad_input: bfloat16 [4, 1024, 1024], P('batch', 'seq')
- grad_down: float32 [7, 8, 1024, 16], replicated
- grad_up: float32 [7, 8, 16, 1024], replicated
Inputs may be any that keep to these rules, and one draw needn't show every extreme that they name: The valid tokens of a sequence are its first lengths slots; some sequence fills all 1024 slots and some has exactly 256. `memory_picks`: the 32 picks of one token and memory head are distinct rows of one owner, owner k holding rows k * 2048 to (k + 1) * 2048 - 1 in the order of batch+seq. Among the 128 slots of one sequence on one device, at most 32 token-head pairs pick in the rows of any one owner, and in every draw some owner gets exactly 32 such pairs from every device.
All inputs are finite; a program needn't handle non-finite values.
Results may differ from a plain program's by a relative error of at most 0.022.
Values may be sent and summed in bfloat16 or wider, within the bound.
No kernel may reach another device: no remote copies, remote signals or barrier semaphores. Data moves between devices by JAX's collectives and lax.ppermute only.
A program may use at most 192 MiB of HBM per device.

v0:
```python
import functools

import jax
import jax.numpy as jnp
from jax import lax
from jax.experimental import pallas as pl
from jax.experimental.pallas import tpu as pltpu
from jax.sharding import PartitionSpec as P

HEAD_DIM = 64
MHEADS = 4
KHALF = 128
NSUB = 256
PICKS = 32
ADAPTERS = 8
RANK = 16
LANES = 128
ADAPTER_STEP = 4096
RECALL_ROWS = 128
EPS = 1e-06
NEG = -1e30
F32 = jnp.float32
BF16 = jnp.bfloat16
I32 = jnp.int32
HBM = pl.BlockSpec(memory_space=pltpu.HBM)
SMEM = pl.BlockSpec(memory_space=pltpu.SMEM)
VMEM = pl.BlockSpec(memory_space=pltpu.VMEM)
MIB = 1 << 20


def product(left, right):
    return lax.dot_general(left, right, (((1,), (0,)), ((), ())), preferred_element_type=F32)


def against(left, right):
    return lax.dot_general(left, right, (((1,), (1,)), ((), ())), preferred_element_type=F32)


def contract(left, right):
    return lax.dot_general(left, right, (((0,), (0,)), ((), ())), preferred_element_type=F32)


def iota(shape, axis):
    return lax.broadcasted_iota(I32, shape, axis)


def lane_pick(table, index):
    return jnp.take_along_axis(table, index, axis=1, mode="promise_in_bounds")


def shaped(shape, dtype):
    return jax.ShapeDtypeStruct(shape, dtype)


class Stage:
    def __init__(self, loads, stores):
        self.loads, self.stores = loads, stores
        self.waited, self.begun = set(), set()
        for _, copy in loads:
            copy.start()

    def __call__(self, *refs):
        for at, (ref, copy) in enumerate(self.loads):
            if at not in self.waited and (not refs or any(ref is one for one in refs)):
                self.waited.add(at)
                copy.wait()

    def send(self, *refs):
        for at, (ref, copy) in enumerate(self.stores):
            if at not in self.begun and (not refs or any(ref is one for one in refs)):
                self.begun.add(at)
                copy.start()

    def finish(self):
        self()
        self.send()
        for _, copy in self.stores:
            copy.wait()


def call(kernel, name, ins, outs, args, scratch=(), vmem=40, flops=1 << 28, moved=1 << 22, aliases=None):
    shapes = [(args[i].shape, args[i].dtype) for i, kind in enumerate(ins) if kind == "L"]
    stored = [(out.shape, out.dtype) for kind, out in outs if kind == "S"]
    count_in, count_out, count_user = len(ins), len(outs), len(scratch)

    def wrapped(*refs):
        given, results = list(refs[:count_in]), list(refs[count_in : count_in + count_out])
        rest = list(refs[count_in + count_out :])
        user, buffers = rest[:count_user], rest[count_user:]
        loads, stores = [], []
        for i, kind in enumerate(ins):
            if kind == "L":
                at = len(loads)
                loads.append((buffers[at], pltpu.make_async_copy(given[i], buffers[at], buffers[-1].at[at])))
                given[i] = buffers[at]
        for i, (kind, _) in enumerate(outs):
            if kind == "S":
                at = len(loads) + len(stores)
                stores.append((buffers[at], pltpu.make_async_copy(buffers[at], results[i], buffers[-1].at[at])))
                results[i] = buffers[at]
        stage = Stage(loads, stores)
        kernel(stage, *given, *results, *user)
        stage.finish()

    spaces = {"V": VMEM, "L": HBM, "S": HBM, "H": HBM, "M": SMEM}
    autos = [pltpu.VMEM(*one) for one in shapes + stored]
    args = [
        pltpu.with_memory_space_constraint(one, pltpu.HBM) if kind in "LH" else one
        for kind, one in zip(ins, args, strict=True)
    ]
    return pl.pallas_call(
        wrapped,
        name=name,
        out_shape=[pltpu.HBM(out.shape, out.dtype) if kind in "SH" else out for kind, out in outs],
        in_specs=[spaces[kind] for kind in ins],
        out_specs=[spaces[kind] for kind, _ in outs],
        input_output_aliases=aliases or {},
        scratch_shapes=list(scratch) + autos + ([sema(len(autos))] if autos else []),
        compiler_params=pltpu.CompilerParams(vmem_limit_bytes=vmem * MIB),
        cost_estimate=pl.CostEstimate(flops=flops, bytes_accessed=moved, transcendentals=0),
    )(*args)


def fetch(pairs, sems):
    copies = [
        pltpu.make_async_copy(source, target, sems.at[place])
        for place, (source, target) in enumerate(pairs)
    ]
    for copy in copies:
        copy.start()
    return copies


def sema(count):
    return pltpu.SemaphoreType.DMA((count,))


def gain_row(ref):
    return ref[...].astype(F32).reshape(1, ref.shape[0])


def inverse_norm(values):
    return lax.rsqrt(jnp.mean(values * values, axis=1, keepdims=True) + EPS)


def norm_back(values, inverse, scales, incoming):
    weighted = incoming * scales
    inner = jnp.mean(weighted * values, axis=1, keepdims=True)
    return weighted * inverse - values * inverse * inverse * inverse * inner


def qkv_kernel(ready, adapter, x_ref, gain_ref, w_any, dn_any, up_any, out_ref, norm_ref, rank_ref, w, dn, up, sems):
    groups, tokens, wide = out_ref.shape
    cols = wide // 3
    a = adapter[0]
    copies = fetch(
        [(dn_any.at[j, a], dn.at[pl.ds(RANK * j, RANK)]) for j in range(3)]
        + [(up_any.at[j, a], up.at[pl.ds(RANK * j, RANK)]) for j in range(3)]
        + [(w_any.at[j], w.at[j]) for j in range(3)],
        sems,
    )
    ready()
    x = x_ref[...].astype(F32)
    normed = (x * inverse_norm(x) * gain_row(gain_ref)).astype(BF16)
    norm_ref[...] = normed
    ready.send(norm_ref)
    for copy in copies[:6]:
        copy.wait()
    ranks = against(normed, dn[...]).astype(BF16)
    rank_ref[...] = ranks
    ready.send(rank_ref)
    place = iota((tokens, 3 * RANK), 1) // RANK
    for j in range(3):
        own = jnp.where(place == j, ranks.astype(F32), 0.0).astype(BF16)
        extra = product(own, up[...])
        copies[6 + j].wait()
        result = (product(normed, w[j]) + extra).astype(BF16)
        for s in range(groups):
            out_ref[s, :, j * cols : (j + 1) * cols] = result[:, s * cols : (s + 1) * cols]


def mix_back_kernel(ready, adapter, cot_ref, w_any, dn_any, up_any, grad_ref, rank_ref, w, dn, up, sems):
    a = adapter[0]
    copies = fetch([(up_any.at[6, a], up), (dn_any.at[6, a], dn), (w_any.at[1], w)], sems)
    ready()
    gy = cot_ref[...]
    copies[0].wait()
    ranks = against(gy, up[...]).astype(BF16)
    rank_ref[...] = ranks
    copies[1].wait()
    extra = product(ranks, dn[...])
    copies[2].wait()
    grad_ref[...] = (against(gy, w[...]) + extra).astype(BF16)


def route_kernel(rows_dev, owners, ready, adapter, picks_ref, slot_ref, slot_col_ref, pick_ref, *ids_refs):
    ready()
    heads, picks, tokens = picks_ref.shape
    capacity = 2 * heads * tokens // owners
    groups = capacity // 8
    visits = heads * tokens
    owner = jnp.concatenate([picks_ref[h, 0:1, :] for h in range(heads)], axis=1) // rows_dev
    hot = jnp.where(iota((owners, visits), 0) == owner, 1.0, 0.0)
    before = jnp.where(iota((visits, visits), 0) < iota((visits, visits), 1), 1.0, 0.0).astype(BF16)
    counts = product(hot.astype(BF16), before)
    within = jnp.sum(hot * counts, axis=0, keepdims=True).astype(I32)
    slot = owner * capacity + within
    rows = [slot[:, h * tokens : (h + 1) * tokens] for h in range(heads)]
    stacked = jnp.concatenate(rows + [jnp.full((8 - heads, tokens), -1, I32)], axis=0)
    slot_ref[...] = stacked
    tall = jnp.concatenate([stacked, jnp.full((tokens - 8, tokens), -1, I32)], axis=0)
    slot_col_ref[...] = jnp.transpose(tall)
    packed = jnp.concatenate([picks_ref[h] for h in range(heads)], axis=0)
    by_token = jnp.transpose(packed)
    pick_ref[...] = by_token
    local = by_token % rows_dev
    lanes = iota((tokens, LANES), 1)
    total = jnp.zeros((owners * 8, LANES), F32)
    out_lane = iota((owners * 8, LANES), 1) // PICKS
    place = iota((owners * 8, tokens), 0)
    base = (place // 8) * capacity + place % 8
    for g in range(groups):
        high = jnp.zeros((owners * 8, LANES), F32)
        low = jnp.zeros((owners * 8, LANES), F32)
        for h in range(heads):
            chosen = jnp.where(base + g * 8 == rows[h], 1.0, 0.0).astype(BF16)
            own = jnp.where(lanes // PICKS == h, local, 0)
            own = tile_groups(own.astype(F32), heads).astype(I32)
            high = high + product(chosen, (own // 256).astype(F32).astype(BF16))
            low = low + product(chosen, (own % 256).astype(F32).astype(BF16))
        total = jnp.where(out_lane == g, high * 256.0 + low, total)
    batches = len(ids_refs) - 1
    part = owners * 8 // batches
    ids_refs[-1][...] = total.astype(I32) + adapter[0] * ADAPTER_STEP
    for k in range(batches):
        target = lax.rem(lax.axis_index("batch") + k, batches)
        ids_refs[k][...] = ids_refs[-1][pl.ds(pl.multiple_of(target * part, part), part), :]


def tile_groups(values, count):
    total = values
    for turn in range(1, count):
        total = total + pltpu.roll(values, turn * PICKS, 1)
    return total


def prepare_kernel(groups, rows_dev, batches, ready, sent_ref, ids_ref, index_any, stage, turned, sems):
    ready()
    seq, _, cols = sent_ref.shape
    lanes = groups * PICKS
    chunks = 2 * lanes // cols
    for k in range(batches):
        source = lax.rem(lax.axis_index("batch") + (batches - k), batches)
        for s in range(seq):
            both = [
                sent_ref[s, (chunk * batches + k) * 8 : (chunk * batches + k + 1) * 8, :].astype(F32)
                for chunk in range(chunks)
            ]
            both = jnp.concatenate(both, axis=1).astype(I32)
            ids = widen(both[:, :lanes] * 256 + both[:, lanes:])
            ids_ref[pl.ds(pl.multiple_of((source * seq + s) * 8, 8), 8), :] = ids
    ready.send(ids_ref)
    places = ids_ref.shape[0]
    chunks = rows_dev // LANES
    high_rows = max(8, chunks)
    steps = groups * (places // LANES)
    for k in range(places // LANES):
        turned[k] = jnp.transpose(ids_ref[k * LANES : (k + 1) * LANES, :] & (ADAPTER_STEP - 1))

    def put(step, slot):
        target = index_any.at[pl.ds(pl.multiple_of(step * LANES, LANES), LANES)]
        return pltpu.make_async_copy(stage.at[slot], target, sems.at[slot])

    def one(step, carry):
        k, g = lax.rem(step, places // LANES), step // (places // LANES)
        slot = lax.rem(step, 2)
        mask = jnp.zeros((LANES, LANES), I32)
        highs = jnp.zeros((high_rows, LANES), I32)
        for r in range(PICKS):
            bit = (1 << r) if r < 31 else -(1 << 31)
            row = turned[k, pl.ds(g * PICKS + r, 1), :]
            mask = mask | jnp.where(row & 127 == iota((LANES, LANES), 0), bit, 0)
            highs = highs | jnp.where(row >> 7 == iota((high_rows, LANES), 0), bit, 0)

        @pl.when(step >= 2)
        def _():
            put(step - 2, slot).wait()

        for c in range(chunks):
            index = 31 - lax.clz(mask & highs[c : c + 1, :])
            stage[slot, :, c * LANES : (c + 1) * LANES] = jnp.transpose(index).astype(jnp.int16)
        put(step, slot).start()
        return carry

    lax.fori_loop(0, steps, one, 0)
    for step in range(max(0, steps - 2), steps):
        put(step, step % 2).wait()


def recall_kernel(groups, ready, weight_ref, index_any, mem_any, out_any, mem, index, dense, staged, sems):
    places = weight_ref.shape[0]
    rows_dev = mem.shape[0]
    chunks = rows_dev // LANES
    block = dense.shape[1]
    per_group = places // block
    blocks = groups * per_group
    seq = out_any.shape[0]
    planes = block // (8 * seq)

    def load(b, slot):
        source = index_any.at[pl.ds(pl.multiple_of(b * block, block), block)]
        return pltpu.make_async_copy(source, index.at[slot], sems.at[1 + slot])

    load(0, 0).start()
    copy = pltpu.make_async_copy(mem_any, mem, sems.at[0])
    copy.start()

    def gather(b, side):
        load(b, side).wait()

        @pl.when(b + 1 < blocks)
        def _():
            load(b + 1, 1 - side).start()

        pick(b, side)

    def pick(b, side):
        g, k = b // per_group, lax.rem(b, per_group)
        for start in range(0, block, 16):
            weights = weight_ref[pl.ds(pl.multiple_of(k * block + start, 16), 16), :].astype(F32)
            for c in range(chunks):
                at = index[side, start : start + 16, c * LANES : (c + 1) * LANES].astype(I32)
                value = lane_pick(weights, (at + g * PICKS) & 127)
                dense[side, start : start + 16, c * LANES : (c + 1) * LANES] = jnp.where(at >= 0, value, 0.0).astype(BF16)

    def save(b, side):
        g, k = b // per_group, lax.rem(b, per_group)
        return [
            pltpu.make_async_copy(
                staged.at[side, pl.ds(i * seq, seq)],
                out_any.at[:, k * planes + i, pl.ds(pl.multiple_of(g * 8, 8), 8), :],
                sems.at[3 + side * planes + i],
            )
            for i in range(planes)
        ]

    def multiply(b, side):
        result = product(dense[side], mem[...]).astype(BF16)

        @pl.when(b >= 2)
        def _():
            for one in save(b - 2, side):
                one.wait()

        staged[side] = result.reshape(block // 8, 8, result.shape[1])
        for one in save(b, side):
            one.start()

    gather(0, 0)
    copy.wait()

    def whole(i, carry):
        gather(2 * i + 1, 1)
        multiply(2 * i, 0)

        @pl.when(2 * i + 2 < blocks)
        def _():
            load(2 * i + 2, 0).wait()
            load(2 * i + 3, 1).start()

        pick(jnp.minimum(2 * i + 2, blocks - 1), 0)
        multiply(2 * i + 1, 1)
        return carry

    lax.fori_loop(0, blocks // 2, whole, 0)
    for b in range(blocks - 2, blocks):
        for one in save(b, b % 2):
            one.wait()


def recall_back_kernel(part, batches, groups, ready, ids_ref, *refs):
    before_ref = refs[0] if part else None
    grad_ref, mem_any, out_ref, mem, scores, sems = refs[part:]
    items, half = grad_ref.shape
    seq = items // (batches * groups * 8)
    rows_dev = mem.shape[0]
    capacity = groups * 8
    chunks = rows_dev // LANES
    block = scores.shape[0]
    per_block = block // capacity
    blocks = items // block
    copies = fetch([(mem_any.at[:, pl.ds(part * half, half)], mem)], sems)
    ready()
    copies[0].wait()

    def whole(b, outer):
        scores[...] = against(grad_ref[pl.ds(pl.multiple_of(b * block, block), block), :], mem[...])

        lane_group = iota((8, LANES), 1) // PICKS
        for local in range(per_block):
            sender = b * per_block + local
            spot = lax.rem(sender, batches) * seq + sender // batches
            start = pl.multiple_of(spot * 8, 8)
            ids = ids_ref[pl.ds(start, 8), :] & (ADAPTER_STEP - 1)
            low = ids & 127
            high = ids >> 7
            total = before_ref[pl.ds(start, 8), :] if part else jnp.zeros((8, LANES), F32)
            for g in range(groups):
                key = jnp.where(lane_group == g, high, -1)
                here = jnp.zeros((8, LANES), F32)
                row = local * capacity + g * 8
                for c in range(chunks):
                    found = scores[row : row + 8, c * LANES : (c + 1) * LANES]
                    here = jnp.where(key == c, lane_pick(found, low), here)
                total = total + here
            out_ref[pl.ds(start, 8), :] = total.astype(out_ref.dtype)
        return outer

    lax.fori_loop(0, blocks, whole, 0)


def head_parts(values, h, spare):
    lane = iota(values.shape, 1)
    return jnp.where(lane // HEAD_DIM == h, values, jnp.where(lane == (1 - h) * HEAD_DIM, spare, 0.0)).astype(BF16)


def widen(values):
    if values.shape[1] == LANES:
        return values
    return jnp.concatenate([values, jnp.zeros((values.shape[0], LANES - values.shape[1]), values.dtype)], axis=1)


def attend_kernel(groups, batches, ready, length, qkv_ref, *refs):
    o_ref, lse_ref, saved_any, parts, values_t, mixed, sems = refs[batches:]
    ready()
    saving = pltpu.make_async_copy(qkv_ref, saved_any, sems.at[0])
    saving.start()
    rows, wide = qkv_ref.shape
    cols = wide // 3
    seq = o_ref.shape[0]
    lanes = groups * PICKS
    for s in range(seq):
        ids = jnp.concatenate([refs[k][s * 8 : (s + 1) * 8, :lanes] for k in range(batches)], axis=0)
        both = jnp.concatenate([ids // 256, ids % 256], axis=1).astype(F32).astype(BF16)
        for chunk in range(2 * lanes // cols):
            start = rows // seq + chunk * batches * 8
            o_ref[s, start : start + batches * 8, :] = both[:, chunk * cols : (chunk + 1) * cols]
    heads = cols // HEAD_DIM
    size = min(256, rows)
    valid = length[0]
    bias = jnp.where(iota((rows, LANES), 0) < valid, 0.0, NEG)
    keys = widen(qkv_ref[:, cols : 2 * cols].astype(F32))
    values_t[...] = jnp.transpose(widen(qkv_ref[:, 2 * cols :].astype(F32))).astype(BF16)
    lse_ref[...] = jnp.zeros_like(lse_ref)

    def one(h, carry):
        parts[...] = head_parts(keys, h, bias)
        for i in range(rows // size):
            first, last = i * size, (i + 1) * size
            queries = widen(qkv_ref[first:last, 0:cols].astype(F32)) * (HEAD_DIM**-0.5)
            query = head_parts(queries, h, 1.0)
            near = against(parts[first:last], query)
            near = jnp.where(iota((size, size), 0) <= iota((size, size), 1), near, NEG)
            high = jnp.max(near, axis=0, keepdims=True)
            if i:
                far = against(parts[:first], query)
                high = jnp.maximum(high, jnp.max(far, axis=0, keepdims=True))
            near = jnp.exp(near - high)
            summed = jnp.sum(near, axis=0, keepdims=True)
            result = product(values_t[:, first:last], near.astype(BF16))
            if i:
                far = jnp.exp(far - high)
                summed = summed + jnp.sum(far, axis=0, keepdims=True)
                result = result + product(values_t[:, :first], far.astype(BF16))
            lse_ref[pl.ds(h, 1), first:last] = high + jnp.log(summed)
            own = iota((LANES, size), 0) // HEAD_DIM == h
            mixed[:, first:last] = jnp.where(own, result / summed, mixed[:, first:last])
        return carry

    mixed[...] = jnp.zeros_like(mixed)
    lax.fori_loop(0, heads, one, 0)
    ready.send(lse_ref)
    tokens = rows // seq
    for s in range(seq):
        first = s * tokens
        kept = jnp.where(first + iota((LANES, tokens), 1) < valid, mixed[:, first : first + tokens], 0.0)
        o_ref[s, 0:tokens, :] = jnp.transpose(kept)[:, :cols].astype(BF16)
    saving.wait()


def attend_back_kernel(ready, length, qkv_ref, go_ref, lse_ref, out_ref, dk, dv, dq, parts, keys_t, values):
    ready()
    rows, wide = qkv_ref.shape
    cols = wide // 3
    heads = cols // HEAD_DIM
    size = min(256, rows)
    valid = length[0]
    scaling = HEAD_DIM**-0.5
    bias = jnp.where(iota((rows, LANES), 0) < valid, 0.0, NEG)
    keys = widen(qkv_ref[:, cols : 2 * cols].astype(F32))
    keys_t[...] = jnp.transpose(keys).astype(BF16)
    values[...] = widen(qkv_ref[:, 2 * cols :])
    dk[...] = jnp.zeros_like(dk)
    dv[...] = jnp.zeros_like(dv)
    dq[...] = jnp.zeros_like(dq)

    def one(h, carry):
        parts[...] = head_parts(keys, h, bias)
        for i in range(rows // size):
            first, last = i * size, (i + 1) * size
            queries = widen(qkv_ref[first:last, 0:cols].astype(F32)) * scaling
            grads = widen(go_ref[first:last, :].astype(F32))
            query = head_parts(queries, h, 1.0)
            plain = head_parts(queries, h, 0.0)
            grad = head_parts(grads, h, 0.0)
            lse = lse_ref[pl.ds(h, 1), first:last]
            near = against(parts[first:last], query)
            near = jnp.where(iota((size, size), 0) <= iota((size, size), 1), near, NEG)
            near = jnp.exp(near - lse)
            near_gp = against(values[first:last], grad)
            delta = jnp.sum(near * near_gp, axis=0, keepdims=True)
            if i:
                far = jnp.exp(against(parts[:first], query) - lse)
                far_gp = against(values[:first], grad)
                delta = delta + jnp.sum(far * far_gp, axis=0, keepdims=True)
            near_gs = (near * (near_gp - delta)).astype(BF16)
            result = product(keys_t[:, first:last], near_gs)
            dk[first:last] += product(near_gs, plain)
            dv[first:last] += product(near.astype(BF16), grad)
            if i:
                far_gs = (far * (far_gp - delta)).astype(BF16)
                result = result + product(keys_t[:, :first], far_gs)
                dk[:first] += product(far_gs, plain)
                dv[:first] += product(far.astype(BF16), grad)
            own = iota((LANES, size), 0) // HEAD_DIM == h
            dq[:, first:last] = jnp.where(own, result, dq[:, first:last])
        return carry

    lax.fori_loop(0, heads, one, 0)
    out_ref[:, 0:cols] = (jnp.transpose(dq[...]) * scaling)[:, :cols].astype(BF16)
    out_ref[:, cols : 2 * cols] = dk[:, :cols].astype(BF16)
    out_ref[:, 2 * cols :] = dv[:, :cols].astype(BF16)


def pick_chosen(tables, index):
    tokens = index.shape[0]
    low = index & 127
    key = (index >> 7) + (iota((tokens, LANES), 1) // PICKS) * (NSUB // LANES)
    total = jnp.zeros((tokens, LANES), F32)
    for h in range(MHEADS):
        for c in range(NSUB // LANES):
            found = lane_pick(tables[h][:, c * LANES : (c + 1) * LANES], low)
            total = jnp.where(key == h * (NSUB // LANES) + c, found, total)
    return total


def group_reduce(values, reducer, fill):
    group = iota(values.shape, 1) // PICKS
    total = jnp.zeros(values.shape, F32)
    for h in range(MHEADS):
        one = reducer(jnp.where(group == h, values, fill), axis=1, keepdims=True)
        total = jnp.where(group == h, one, total)
    return total


def middle_kernel(
    ready, adapter, o_ref, x_ref, gain_ref, mix_ref, w_in_any, w_out_any, dn_any, up_any,
    left_ref, right_ref, same_ref, sent_ref, att_ref, rank_ref, mid_ref, norm_ref, gate_ref, w, dn, up, sems,
):
    groups = o_ref.shape[0]
    a = adapter[0]
    copies = fetch(
        [(dn_any.at[3, a], dn.at[0]), (dn_any.at[5, a], dn.at[1]), (up_any.at[3, a], up.at[0]), (up_any.at[5, a], up.at[1]),
         (w_out_any.at[0], w.at[0]), (w_in_any.at[4], w.at[1])],
        sems,
    )
    tokens = att_ref.shape[0]
    attended = jnp.concatenate([o_ref[s, 0:tokens, :] for s in range(groups)], axis=1)
    sent_ref[...] = o_ref[:, tokens:, :]
    ready.send(sent_ref)
    att_ref[...] = attended
    ready.send(att_ref)
    for copy in copies[:4]:
        copy.wait()
    rank_three = against(attended, dn[0]).astype(BF16)
    extra = product(rank_three, up[0])
    copies[4].wait()
    ready(x_ref, gain_ref)
    middle = x_ref[...].astype(F32) + (product(attended, w[0]) + extra)
    mid_ref[...] = middle
    normed = (middle * inverse_norm(middle) * gain_row(gain_ref)).astype(BF16)
    norm_ref[...] = normed
    same_ref[...] = normed
    ready.send(mid_ref, norm_ref)
    rank_five = against(normed, dn[1]).astype(BF16)
    rank_ref[0] = rank_three
    rank_ref[1] = rank_five
    extra = product(rank_five, up[1])
    copies[5].wait()
    gate = product(normed, w[1]) + extra
    gate_ref[...] = gate
    ready.send(rank_ref, gate_ref)
    ready(mix_ref)
    memory_grad = (mix_ref[...].astype(F32) * (gate * jax.nn.sigmoid(gate))).astype(BF16)
    half = left_ref.shape[1]
    left_ref[...] = memory_grad[:, :half]
    right_ref[...] = memory_grad[:, half:]


def scores_kernel(
    owners, ready, adapter, normed_ref, picks_ref, slot_ref, keys_ref, w_in_any, dn_any, up_any,
    send_ref, rank_ref, weight_ref, w, dn, up, sems,
):
    a = adapter[0]
    copies = fetch([(dn_any.at[4, a], dn), (up_any.at[4, a], up), (w_in_any.at[3], w)], sems)
    normed = normed_ref[...]
    copies[0].wait()
    ranks = against(normed, dn[...]).astype(BF16)
    rank_ref[...] = ranks
    copies[1].wait()
    extra = product(ranks, up[...])
    copies[2].wait()
    query = (product(normed, w[...]) + extra).astype(BF16)
    ready()
    ready.send(rank_ref)
    first, second = [], []
    for h in range(MHEADS):
        base = 2 * h * KHALF
        first.append(against(query[:, base : base + KHALF], keys_ref[0, h]))
        second.append(against(query[:, base + KHALF : base + 2 * KHALF], keys_ref[1, h]))
    picks = picks_ref[...]
    scores = pick_chosen(first, picks // NSUB) + pick_chosen(second, picks % NSUB)
    exponent = jnp.exp(scores - group_reduce(scores, jnp.max, NEG))
    weights = exponent / group_reduce(exponent, jnp.sum, 0.0)
    weight_ref[...] = weights
    ready.send(weight_ref)
    send_ref[...] = to_slots(weights, slot_ref, owners).astype(BF16)


def to_slots(weights, slot_ref, owners):
    tokens = weights.shape[0]
    capacity = 2 * MHEADS * tokens // owners
    lane_group = iota((tokens, LANES), 1) // PICKS
    tiled = [
        tile_groups(jnp.where(lane_group == h, weights, 0.0), MHEADS).astype(BF16) for h in range(MHEADS)
    ]
    place = iota((owners * 8, tokens), 0)
    base = (place // 8) * capacity + place % 8
    out_group = iota((owners * 8, LANES), 1) // PICKS
    total = jnp.zeros((owners * 8, LANES), F32)
    for g in range(capacity // 8):
        part = jnp.zeros((owners * 8, LANES), F32)
        for h in range(MHEADS):
            chosen = jnp.where(base + g * 8 == slot_ref[h : h + 1, :], 1.0, 0.0).astype(BF16)
            part = part + product(chosen, tiled[h])
        total = jnp.where(out_group == g, part, total)
    return total


def plane_hits(slot_ref, plane, seq, capacity):
    tokens = slot_ref.shape[1]
    place = plane * (seq * capacity) + iota((seq * capacity, tokens), 0)
    chosen = jnp.zeros((seq * capacity, tokens), F32)
    for h in range(MHEADS):
        chosen = jnp.where(place == slot_ref[h : h + 1, :], 1.0, chosen)
    return chosen.astype(BF16)


def scatter_kernel(ready, *refs):
    ready()
    out_ref = refs[-1]
    seq, batches, capacity, wide = out_ref.shape
    plane = lax.axis_index("batch")
    for k in range(batches):
        chosen = plane_hits(refs[k], plane, seq, capacity)
        rows = product(chosen, refs[batches + k][...]).astype(BF16)
        source = lax.rem(plane + (batches - k), batches)
        out_ref[:, pl.ds(source, 1)] = rows.reshape(seq, 1, capacity, wide)


def gather_kernel(ready, *refs):
    ready()
    batches = (len(refs) - 1) // 2
    back_ref = refs[batches]
    seq, _, capacity, wide = back_ref.shape
    plane = lax.axis_index("batch")
    for k in range(batches):
        chosen = plane_hits(refs[k], plane, seq, capacity)
        source = lax.rem(plane + (batches - k), batches)
        rows = back_ref[:, pl.ds(source, 1)].reshape(seq * capacity, wide)
        refs[batches + 1 + k][...] = contract(chosen, rows).astype(BF16)


def memory_kernel(batches, ready, adapter, gate_ref, mix_ref, *refs):
    w_in_any, dn_any, up_any, mixed_ref, grank_ref, ggate_ref, part_ref, w, dn, up, sems = refs[batches:]
    a = adapter[0]
    copies = fetch([(dn_any.at[5, a], dn), (up_any.at[5, a], up), (w_in_any.at[4], w)], sems)
    ready()
    memory = refs[0][...].astype(F32)
    for k in range(1, batches):
        memory = memory + refs[k][...].astype(F32)
    gate = gate_ref[...]
    sigmoid = jax.nn.sigmoid(gate)
    mixed_ref[...] = (memory * (gate * sigmoid)).astype(BF16)
    ggate = (mix_ref[...].astype(F32) * memory * sigmoid * (1.0 + gate * (1.0 - sigmoid))).astype(BF16)
    ggate_ref[...] = ggate
    for copy in copies[:2]:
        copy.wait()
    granks = against(ggate, up[...]).astype(BF16)
    grank_ref[...] = granks
    extra = product(granks, dn[...])
    copies[2].wait()
    ready.send(mixed_ref, ggate_ref, grank_ref)
    part_ref[...] = against(ggate, w[...]) + extra


def output_kernel(ready, adapter, mixed_ref, mid_ref, w_out_any, dn_any, up_any, out_ref, rank_ref, w, dn, up, sems):
    a = adapter[0]
    copies = fetch([(dn_any.at[6, a], dn), (up_any.at[6, a], up), (w_out_any.at[1], w)], sems)
    ready()
    mixed = mixed_ref[...]
    for copy in copies[:2]:
        copy.wait()
    ranks = against(mixed, dn[...]).astype(BF16)
    rank_ref[...] = ranks
    extra = product(ranks, up[...])
    copies[2].wait()
    out_ref[...] = (mid_ref[...] + (product(mixed, w[...]) + extra)).astype(BF16)


def query_kernel(
    owners, rows_dev, ready, length, adapter, back_ref, slot_ref, picks_ref, weight_ref, part_ref, mid_ref, cot_ref, gain_ref,
    keys_ref, w_in_any, w_out_any, dn_any, up_any,
    go_ref, gquery_ref, grank_ref, gmid_ref, w, dn, up, turned, sems,
):
    groups, tokens, cols = go_ref.shape
    a = adapter[0]
    copies = fetch(
        [(dn_any.at[3, a], dn.at[0]), (dn_any.at[4, a], dn.at[1]), (up_any.at[3, a], up.at[0]),
         (up_any.at[4, a], up.at[1]), (w_in_any.at[3], w.at[0]), (w_out_any.at[0], w.at[1])],
        sems,
    )
    ready(slot_ref, weight_ref)
    capacity = 2 * MHEADS * tokens // owners
    slots = iota((tokens, owners * 8), 1)
    base = (slots // 8) * capacity + slots % 8
    lane_group = iota((tokens, LANES), 1) // PICKS
    back = back_ref[...]
    gw = jnp.zeros((tokens, LANES), F32)
    for h in range(MHEADS):
        part = jnp.zeros((tokens, LANES), F32)
        for g in range(capacity // 8):
            chosen = jnp.where(base + g * 8 == slot_ref[:, h : h + 1], 1.0, 0.0).astype(BF16)
            part = jnp.where(lane_group == g, product(chosen, back), part)
        gw = jnp.where(lane_group == h, tile_groups(part, MHEADS), gw)
    weights = weight_ref[...]
    gscore = jnp.transpose(weights * (gw - group_reduce(weights * gw, jnp.sum, 0.0)))
    turned[...] = gscore
    ready(picks_ref, keys_ref)
    span = rows_dev // NSUB
    halves = []
    for h in range(MHEADS):

        def one(r, sums):
            pick = picks_ref[h, pl.ds(r, 1), :]
            value = turned[pl.ds(h * PICKS + r, 1), :]
            low = jnp.where((pick // NSUB) % span == iota((8, tokens), 0), value, 0.0)
            hit = (pick % NSUB).astype(jnp.int16) == lax.broadcasted_iota(jnp.int16, (NSUB, tokens), 0)
            return sums[0] + low, sums[1] + jnp.where(hit, value.astype(BF16), jnp.zeros((), BF16))

        start = (jnp.zeros((8, tokens), F32), jnp.zeros((NSUB, tokens), BF16))
        first, second = lax.fori_loop(0, PICKS, one, start, unroll=8)
        origin = picks_ref[h, 0:1, :] // rows_dev
        place = iota((NSUB, tokens), 0)
        wide = jnp.concatenate([first[:span]] * (NSUB // span), axis=0)
        wide = jnp.where(place // span == origin, wide, 0.0)
        halves.append(contract(wide.astype(BF16), keys_ref[0, h]))
        halves.append(contract(second, keys_ref[1, h]))
    gquery = jnp.concatenate(halves, axis=1).astype(BF16)
    gquery_ref[...] = gquery
    ready.send(gquery_ref)
    ready()
    for copy in copies[:4]:
        copy.wait()
    granks = against(gquery, up[1]).astype(BF16)
    grank_ref[1] = granks
    extra = product(granks, dn[1])
    copies[4].wait()
    gnormed = against(gquery, w[0]) + extra + part_ref[...]
    middle = mid_ref[...]
    gmid = cot_ref[...].astype(F32) + norm_back(middle, inverse_norm(middle), gain_row(gain_ref), gnormed)
    gmid_ref[...] = gmid
    ready.send(gmid_ref)
    low = gmid.astype(BF16)
    granks = against(low, up[0]).astype(BF16)
    grank_ref[0] = granks
    ready.send(grank_ref)
    extra = product(granks, dn[0])
    copies[5].wait()
    go = against(low, w[1]) + extra
    row = lax.axis_index("seq") * tokens + iota((tokens, 1), 0)
    go = jnp.where(row < length[0], go, 0.0).astype(BF16)
    for s in range(groups):
        go_ref[s] = go[:, s * cols : (s + 1) * cols]


def place_columns(out_ref, row, values):
    groups, _, cols = out_ref.shape
    low = values.astype(BF16)
    for s in range(groups):
        out_ref[s, row : row + values.shape[0], :] = low[:, s * cols : (s + 1) * cols]


def factor_kernel(ready, att_ref, norm_ref, mixed_ref, gmid_ref, gquery_ref, ggate_ref, cot_ref, r35, r4, r6, g34, g5, g6, out_ref):
    ready()
    half = 4 * RANK
    sides = (
        (att_ref[...], gmid_ref[...].astype(BF16), r35[0], g34[0]),
        (norm_ref[...], gquery_ref[...], r4[...], g34[1]),
        (norm_ref[...], ggate_ref[...], r35[1], g5[...]),
        (mixed_ref[...], cot_ref[...], r6[...], g6[...]),
    )
    for j, (value, gy, rank, grank) in enumerate(sides):
        place_columns(out_ref, j * RANK, contract(grank, value))
        place_columns(out_ref, half + j * RANK, contract(rank, gy))


def entry_factor_kernel(ready, adapter, grad_ref, norm_ref, ranks_ref, up_any, out_ref, gy_ref, grank_ref, up, sems):
    groups, tokens, wide = grad_ref.shape
    cols = wide // 3
    a = adapter[0]
    copies = fetch([(up_any.at[j, a], up.at[pl.ds(RANK * j, RANK)]) for j in range(3)], sems)
    gys = [
        jnp.concatenate([grad_ref[s, :, j * cols : (j + 1) * cols] for s in range(groups)], axis=1) for j in range(3)
    ]
    for j in range(3):
        gy_ref[j] = gys[j]
    ready.send(gy_ref)
    for copy in copies:
        copy.wait()
    ready()
    place = iota((tokens, 3 * RANK), 1) // RANK
    granks = jnp.zeros((tokens, 3 * RANK), F32)
    ranks = ranks_ref[...]
    for j in range(3):
        granks = jnp.where(place == j, against(gys[j], up[...]), granks)
        up_grad = contract(ranks, gys[j])
        place_columns(out_ref, (3 + j) * RANK, up_grad[j * RANK : (j + 1) * RANK, :])
    granks = granks.astype(BF16)
    grank_ref[...] = granks
    ready.send(grank_ref)
    place_columns(out_ref, 0, contract(granks, norm_ref[...]))


def entry_kernel(ready, adapter, gy_ref, grank_ref, x_ref, gain_ref, gmid_ref, w_any, dn_any, out_ref, w, dn, sems):
    a = adapter[0]
    copies = fetch(
        [(dn_any.at[j, a], dn.at[pl.ds(RANK * j, RANK)]) for j in range(3)] + [(w_any.at[j], w.at[j]) for j in range(3)],
        sems,
    )
    ready()
    x = x_ref[...].astype(F32)
    for copy in copies[:3]:
        copy.wait()
    total = product(grank_ref[...], dn[...])
    for j in range(3):
        copies[3 + j].wait()
        total = total + against(gy_ref[j], w[j])
    back = norm_back(x, inverse_norm(x), gain_row(gain_ref), total)
    out_ref[...] = (gmid_ref[...] + back).astype(BF16)


def sum_kernel(ready, parts_ref, out_ref):
    ready()
    total = parts_ref[0].astype(F32)
    for s in range(1, parts_ref.shape[0]):
        total = total + parts_ref[s].astype(F32)
    out_ref[...] = total.astype(BF16)


def stack_kernel(ready, *refs):
    for k in range(refs[-1].shape[0]):
        refs[-1][k] = refs[k][...]


def relative_marks(ids_ref, batches):
    plane = lax.axis_index("batch")
    absolute = adapter_marks(ids_ref, batches)
    marks = []
    for k in range(batches):
        source = lax.rem(plane + (batches - k), batches)
        mark = absolute[0]
        for b in range(1, batches):
            mark = jnp.where(source == b, absolute[b], mark)
        marks.append(mark)
    return marks


def adapter_marks(ids_ref, batches):
    step = ids_ref.shape[0] // batches
    return [ids_ref[b * step : b * step + 1, 0:1] // ADAPTER_STEP for b in range(batches)]


def spread_rows(parts, marks, runs, stage, sems):
    seq, batches = parts.shape[:2]
    for target, origin, base, count in runs:

        def put(i, target=target, origin=origin, base=base):
            return pltpu.make_async_copy(stage.at[base + i], target.at[origin + i], sems.at[base + i])

        def one(i, carry, put=put, base=base):
            start = pl.multiple_of((base + i) * RANK, RANK)
            rows = [
                jnp.concatenate([parts[s, k, pl.ds(start, RANK), :] for s in range(seq)], axis=1).astype(F32)
                for k in range(batches)
            ]
            for k in range(ADAPTERS):
                total = jnp.zeros(rows[0].shape, F32)
                for row, mark in zip(rows, marks, strict=True):
                    total = total + jnp.where(mark == k, row, 0.0)
                stage[base + i, k] = total
            put(i).start()
            return carry

        lax.fori_loop(0, count, one, 0)
    for target, origin, base, count in runs:
        for i in range(count):
            pltpu.make_async_copy(stage.at[base + i], target.at[origin + i], sems.at[base + i]).wait()


def spread_kernel(batches, ready, ids_ref, *refs):
    down_any, up_any, parts, stage, load_sems, sems = refs[-6:]
    seq = parts.shape[0]
    me = lax.axis_index("seq")
    copies = fetch([(refs[m % 2].at[m // 2], parts.at[me ^ m]) for m in range(seq)], load_sems)
    ready()
    marks = relative_marks(ids_ref, batches)
    for copy in copies:
        copy.wait()
    spread_rows(parts, marks, ((down_any, 3, 0, 4), (up_any, 3, 4, 4)), stage, sems)


def last_spread_kernel(batches, ready, ids_ref, down_in, up_in, *refs):
    down_any, up_any, parts, stage, load_sems, sems = refs[-6:]
    seq = parts.shape[0]
    me = lax.axis_index("seq")
    copies = fetch([(refs[m % 2].at[m // 2], parts.at[me ^ m]) for m in range(seq)], load_sems)
    ready()
    marks = relative_marks(ids_ref, batches)
    for copy in copies:
        copy.wait()
    spread_rows(parts, marks, ((down_any, 0, 0, 3), (up_any, 0, 3, 3)), stage, sems)


def along(values, axis, step, size):
    return lax.ppermute(values, axis, [(i, (i + step) % size) for i in range(size)])


def across(values, axis, mask, size):
    return lax.ppermute(values, axis, [(i, i ^ mask) for i in range(size)])


def to_pairs(values, axis, size):
    return [values] + [across(values, axis, m, size) for m in range(2, size, 2)]


def stacked(values, name):
    shape = shaped((len(values), *values[0].shape), values[0].dtype)
    return call(stack_kernel, name, "V" * len(values), [("V", shape)], values)[0]


def exchange(values, axes):
    return lax.all_to_all(values, axes, split_axis=0, concat_axis=0, tiled=True)


def body(
    inputs, lengths, adapter_index, memory_picks, input_weights, output_weights, adapter_down, adapter_up,
    attention_gain, memory_gain, half_keys, memory_values, cotangent,
):
    both = ("batch", "seq")
    batches, seq = lax.axis_size("batch"), lax.axis_size("seq")
    owners = batches * seq
    tokens, width = inputs.shape[1], inputs.shape[2]
    rows, cols, half = tokens * seq, width // seq, width // 2
    rows_dev = memory_values.shape[0]
    capacity = 2 * tokens * MHEADS // owners
    groups = capacity // 8
    items = owners * capacity
    block = min(owners * 8, 256)
    small_block = RECALL_ROWS
    carried = 2 * groups * PICKS // cols * batches * 8
    x, cot = inputs[0], cotangent[0]
    down = jnp.swapaxes(adapter_down, 2, 3)
    gain_one, gain_two = attention_gain, memory_gain
    picks = jnp.transpose(memory_picks[0], (1, 2, 0))
    matrix = pltpu.VMEM((width, width), BF16)
    pair = pltpu.VMEM((2, width, width), BF16)
    triple = pltpu.VMEM((3, width, width), BF16)
    small = pltpu.VMEM((RANK, width), BF16)
    two_small = pltpu.VMEM((2, RANK, width), BF16)
    three_small = pltpu.VMEM((3 * RANK, width), BF16)
    token_low, token_wide = shaped((tokens, width), BF16), shaped((tokens, width), F32)
    token_rank, token_lanes = shaped((tokens, RANK), BF16), shaped((tokens, LANES), F32)
    fixed = functools.partial

    qkv, normed, ranks = call(
        qkv_kernel, "qkv", "MLLHHH",
        [("V", shaped((seq, tokens, 3 * cols), BF16)), ("S", token_low), ("S", shaped((tokens, 3 * RANK), BF16))],
        (adapter_index, x, gain_one, input_weights, down, adapter_up), [triple, three_small, three_small, sema(9)],
    )
    qkv_all = exchange(qkv, "seq").reshape(rows, 3 * cols)

    slot, slot_col, pick, *ids_out = call(
        fixed(route_kernel, rows_dev, owners), "route", "ML",
        [("V", shaped((8, tokens), I32)), ("S", shaped((tokens, tokens), I32)), ("S", shaped((tokens, LANES), I32)),
         *[("V", shaped((seq * 8, LANES), I32)) for _ in range(batches)]],
        (adapter_index, picks), [pltpu.VMEM((owners * 8, LANES), I32)],
    )
    ids_out = [ids_out[0]] + [along(ids_out[k], "batch", k, batches) for k in range(1, batches)]
    qkv_all, ids_out = lax.optimization_barrier((qkv_all, ids_out))
    attended, lse, qkv_saved = call(
        fixed(attend_kernel, groups, batches), "attend", "MV" + "V" * batches,
        [("V", shaped((seq, tokens + carried, cols), BF16)), ("S", shaped((8, rows), F32)), ("H", shaped((rows, 3 * cols), BF16))],
        (lengths, qkv_all, *ids_out),
        [pltpu.VMEM((rows, LANES), BF16), pltpu.VMEM((LANES, rows), BF16), pltpu.VMEM((LANES, rows), F32), sema(1)],
    )
    o_all = exchange(attended, "seq")
    slot, late_cot, attended = lax.optimization_barrier((slot, cot, attended))
    slots = [slot] + [along(slot, "batch", k, batches) for k in range(1, batches)]
    mix_grad, grank_six = call(
        mix_back_kernel, "mixback", "MLHHH", [("S", token_low), ("S", token_rank)],
        (adapter_index, late_cot, output_weights, down, adapter_up), [matrix, small, small, sema(3)],
    )

    o_all, mix_grad, slots = lax.optimization_barrier((o_all, mix_grad, slots))
    left, right, same_two, sent, att, rank_pair, middle, normed_two, gate = call(
        middle_kernel, "middle", "MVLLLHHHH",
        [("V", shaped((tokens, half), BF16)), ("V", shaped((tokens, half), BF16)), ("V", token_low),
         ("S", shaped((seq, carried, cols), BF16)), ("S", token_low),
         ("S", shaped((2, tokens, RANK), BF16)), ("S", token_wide), ("S", token_low), ("S", token_wide)],
        (adapter_index, o_all, x, gain_two, mix_grad, input_weights, output_weights, down, adapter_up),
        [pair, two_small, two_small, sema(6)],
    )
    lefts = [left] + [along(left, "batch", k, batches) for k in range(1, batches)]
    weight_out, rank_four, weights = call(
        fixed(scores_kernel, owners), "scores", "MVLLLHHH",
        [("V", shaped((owners * 8, LANES), BF16)), ("S", token_rank), ("S", token_lanes)],
        (adapter_index, same_two, pick, slot, half_keys, input_weights, down, adapter_up), [matrix, small, small, sema(3)],
    )
    weight_in = exchange(weight_out.reshape(owners, 8, LANES), both).reshape(owners * 8, LANES)
    right, lefts = lax.optimization_barrier((right, lefts))
    rights = [right] + [along(right, "batch", k, batches) for k in range(1, batches)]

    def scatter(parts, name):
        out = [("V", shaped((seq, batches, capacity, half), BF16))]
        return call(scatter_kernel, name, "L" * batches + "V" * batches, out, (*slots, *parts))[0]

    left_out = scatter(lefts, "scatterleft")
    sent, left_out = lax.optimization_barrier((sent, left_out))
    ids, index = call(
        fixed(prepare_kernel, groups, rows_dev, batches), "prepare", "L",
        [("S", shaped((owners * 8, LANES), I32)), ("H", shaped((items, rows_dev), jnp.int16))], (sent,),
        [pltpu.VMEM((2, LANES, rows_dev), jnp.int16), pltpu.VMEM((owners * 8 // LANES, LANES, LANES), I32), sema(2)],
    )
    left_out, weight_in = lax.optimization_barrier((left_out, weight_in))
    left_in = exchange(left_out, "seq").reshape(items, half)

    (sums,) = call(
        fixed(recall_kernel, groups), "recall", "VHH", [("H", shaped((seq, batches, capacity, width), BF16))],
        (weight_in, index, memory_values),
        [pltpu.VMEM((rows_dev, width), BF16), pltpu.VMEM((2, small_block, rows_dev), jnp.int16), pltpu.VMEM((2, small_block, rows_dev), BF16),
         pltpu.VMEM((2, small_block // 8, 8, width), BF16), sema(3 + 2 * (small_block // (8 * seq)))],
        flops=1 << 32,
    )
    sums, left_in = lax.optimization_barrier((sums, left_in))
    back = exchange(sums, "seq")

    def recall_back(part, name, grads, kind, dtype, *before):
        return call(
            fixed(recall_back_kernel, part, batches, groups), name, "L" + "L" * part + "VH",
            [(kind, shaped((owners * 8, LANES), dtype))], (ids, *before, grads, memory_values),
            [pltpu.VMEM((rows_dev, half), BF16), pltpu.VMEM((block, rows_dev), F32), sema(1)], flops=1 << 31,
        )[0]

    right_out = scatter(rights, "scatterright")
    found_left = recall_back(0, "recallleft", left_in, "S", F32)
    right_out, back, found_left = lax.optimization_barrier((right_out, back, found_left))
    right_in = exchange(right_out, "seq").reshape(items, half)
    pieces = call(
        gather_kernel, "gather", "L" * batches + "V", [("V", token_low) for _ in range(batches)], (*slots, back),
    )
    pieces = [pieces[0]] + [along(pieces[k], "batch", batches - k, batches) for k in range(1, batches)]
    found = recall_back(1, "recallright", right_in, "V", BF16, found_left)
    found_back = exchange(found.reshape(owners, 8, LANES), both).reshape(owners * 8, LANES)

    mixed, grank_five, ggate, part = call(
        fixed(memory_kernel, batches), "memory", "MLL" + "V" * batches + "HHH",
        [("S", token_low), ("S", token_rank), ("S", token_low), ("S", token_wide)],
        (adapter_index, gate, mix_grad, *pieces, input_weights, down, adapter_up), [matrix, small, small, sema(3)],
    )

    go, gquery, grank_pair, gmid = call(
        fixed(query_kernel, owners, rows_dev), "query", "MMVLLLLLLLLHHHH",
        [("V", shaped((seq, tokens, cols), BF16)), ("S", token_low), ("S", shaped((2, tokens, RANK), BF16)), ("S", token_wide)],
        (lengths, adapter_index, found_back, slot_col, picks, weights, part, middle, cot, gain_two, half_keys,
         input_weights, output_weights, down, adapter_up),
        [pair, two_small, two_small, pltpu.VMEM((LANES, tokens), F32), sema(6)],
    )
    go_all = exchange(go, "seq").reshape(rows, cols)
    mixed, go = lax.optimization_barrier((mixed, go))
    output, rank_six = call(
        output_kernel, "output", "MLLHHH", [("S", token_low), ("S", token_rank)],
        (adapter_index, mixed, middle, output_weights, down, adapter_up), [matrix, small, small, sema(3)],
    )
    (factors,) = call(
        factor_kernel, "factors", "L" * 13, [("V", shaped((seq, 8 * RANK, cols), BF16))],
        (att, normed_two, mixed, gmid, gquery, ggate, cot, rank_pair, rank_four, rank_six, grank_pair, grank_five, grank_six),
    )
    factors, go_all = lax.optimization_barrier((factors, go_all))
    early_parts = exchange(factors, "seq")

    (grads,) = call(
        attend_back_kernel, "attendback", "MLVL", [("V", shaped((rows, 3 * cols), BF16))], (lengths, qkv_saved, go_all, lse),
        [pltpu.VMEM((rows, LANES), F32), pltpu.VMEM((rows, LANES), F32), pltpu.VMEM((LANES, rows), F32),
         pltpu.VMEM((rows, LANES), BF16), pltpu.VMEM((LANES, rows), BF16), pltpu.VMEM((rows, LANES), BF16)],
    )
    grads, early_parts = lax.optimization_barrier((grads, early_parts))
    grads_all = exchange(grads.reshape(seq, tokens, 3 * cols), "seq")
    (some,) = call(sum_kernel, "sumearly", "V", [("V", shaped((8 * RANK, cols), BF16))], (early_parts,))
    some = [some] + [along(some, "batch", k, batches) for k in range(1, batches)]
    some = stacked(some, "stackearly")
    late, gys, granks = call(
        entry_factor_kernel, "entryfactors", "MVLLH",
        [("V", shaped((seq, 6 * RANK, cols), BF16)), ("S", shaped((3, tokens, width), BF16)), ("S", shaped((tokens, 3 * RANK), BF16))],
        (adapter_index, grads_all, normed, ranks, adapter_up), [three_small, sema(3)],
    )
    late, some = lax.optimization_barrier((late, some))
    late_parts = exchange(late, "seq")
    some = to_pairs(some, "seq", seq)
    (grad_input,) = call(
        entry_kernel, "entry", "MLLLLLHH", [("S", token_low)],
        (adapter_index, gys, granks, x, gain_one, gmid, input_weights, down), [triple, three_small, sema(6)],
    )
    late_parts, some, grad_input = lax.optimization_barrier((late_parts, some, grad_input))
    (late_sum,) = call(sum_kernel, "sumlate", "V", [("V", shaped((6 * RANK, cols), BF16))], (late_parts,))
    late_sums = [late_sum] + [along(late_sum, "batch", k, batches) for k in range(1, batches)]
    some = stacked(some, "pairsearly")
    late_sums, some = lax.optimization_barrier((late_sums, some))
    late_all = to_pairs(stacked(late_sums, "stacklate"), "seq", seq)
    some = (some, across(some, "seq", 1, seq))
    full = shaped((7, ADAPTERS, RANK, width), F32)
    grad_down, grad_up = call(
        fixed(spread_kernel, batches), "spread", "LVV", [("H", full), ("H", full)], (ids, *some),
        [pltpu.VMEM((seq, batches, 8 * RANK, cols), BF16), pltpu.VMEM((8, ADAPTERS, RANK, width), F32), sema(seq), sema(8)],
    )
    late_all, grad_down, grad_up = lax.optimization_barrier((late_all, grad_down, grad_up))
    late_all = stacked(late_all, "pairslate")
    late_all = (late_all, across(late_all, "seq", 1, seq))
    grad_down, grad_up = call(
        fixed(last_spread_kernel, batches), "lastspread", "LHHVV", [("H", full), ("H", full)],
        (ids, grad_down, grad_up, *late_all),
        [pltpu.VMEM((seq, batches, 6 * RANK, cols), BF16), pltpu.VMEM((6, ADAPTERS, RANK, width), F32), sema(seq), sema(6)],
        aliases={1: 0, 2: 1},
    )
    return (output[None], grad_input[None], jnp.swapaxes(grad_down, 2, 3), grad_up)


def solution(mesh):
    split = P("batch", "seq", None)
    return jax.shard_map(
        body,
        mesh=mesh,
        in_specs=(
            split, P("batch"), P("batch"), P("batch", "seq", None, None), P(), P(), P(), P(), P(), P(), P(),
            P(("batch", "seq"), None), split,
        ),
        out_specs=(split, split, P(), P()),
        check_vma=False,
    )
```

profile of v0, /device:TPU:0, one launch (start us, length us, event | category | flops | bytes accessed | tf_op | source)
XLA Modules:
  0.0 243.5 jit_solution(14518613273532797967)
XLA Ops:
  1.3 5.7 %qkv.1 = (bf16[8,128,384]{2,1,0:T(8,128)(2,1)}, bf16[128,1024]{1,0:T(8,128)(2,1)}, bf16[128,48]{1,0:T(8,128)(2,1)}) custom-call(s32[1]{0:T(128)S(6)} %copy.22.refs_0_.refs_1_, bf16[128,1024]{1,0:T(8,128)(2,1)} %bitcast.33, bf16[1024]{0:T(1024)(128)(2,1)} %refs_4_.7, bf16[5,1024,1024]{2,1,0:T(8,128)(2,1)} %refs_6_.3, bf16[7,8,16,1024]{3,2,1,0:T(8,128)(2,1)} %bitcast.24, ...), custom_call_target="tpu_custom_call" | custom-call | flops 268435456 | bytes 4194304 | tf_op jit(solution)/shard_map/qkv/pallas_call | solution.py:111
  7.0 5.2 %all-to-all-start = ((bf16[8,128,384]{2,1,0:T(8,128)(2,1)}), bf16[8,128,384]{2,1,0:T(8,128)(2,1)S(1)}, u32[]{:S(2)}, u32[]{:S(2)}) async-start(bf16[8,128,384]{2,1,0:T(8,128)(2,1)} %get-tuple-element.105), calls=%async_computation | async-start | bytes 1572864 | tf_op jit(solution)/shard_map/all_to_all | solution.py:973
  24.8 5.0 %attend.1 = (bf16[8,192,128]{2,1,0:T(8,128)(2,1)}, f32[8,1024]{1,0:T(8,128)}, bf16[1024,384]{1,0:T(8,128)(2,1)}) custom-call(s32[1]{0:T(128)S(6)} %copy.21.refs_0_, bf16[1024,384]{1,0:T(8,128)(2,1)S(1)} %bitcast.21, s32[64,128]{1,0:T(8,128)S(1)} %get-tuple-element.111.refs_2_, s32[64,128]{1,0:T(8,128)S(1)} %collective-permute-done.refs_3_, ...), custom_call_target="tpu_custom_call" | custom-call | flops 268435456 | bytes 4194304 | tf_op jit(solution)/shard_map/attend/pallas_call | solution.py:111
  29.8 3.5 %all-to-all-start.1 = ((bf16[8,192,128]{2,1,0:T(8,128)(2,1)}), bf16[8,192,128]{2,1,0:T(8,128)(2,1)S(1)}, u32[]{:S(2)}, u32[]{:S(2)}) async-start(bf16[8,192,128]{2,1,0:T(8,128)(2,1)} %get-tuple-element.115), calls=%async_computation.1 | async-start | bytes 786432 | tf_op jit(solution)/shard_map/all_to_all | solution.py:973
  33.2 3.6 %collective-permute-start.5 = (s32[8,128]{1,0:T(8,128)S(1)}, s32[8,128]{1,0:T(8,128)S(1)}, u32[]{:S(2)}, u32[]{:S(2)}) collective-permute-start(s32[8,128]{1,0:T(8,128)S(1)} %get-tuple-element.123.refs_0_.refs_3_), channel_id=1, source_target_pairs={{0,24},{8,0},{16,8},{24,16},{1,25},{9,1},{17,9},{25,17},{2,26},{10... | collective-permute-start | bytes 12296 | tf_op jit(solution)/shard_map/ppermute | solution.py:956
  37.9 3.3 %mixback.1 = (bf16[128,1024]{1,0:T(8,128)(2,1)}, bf16[128,16]{1,0:T(8,128)(2,1)}) custom-call(s32[1]{0:T(128)S(6)} %copy.22.refs_0_.refs_1_, bf16[128,1024]{1,0:T(8,128)(2,1)} %bitcast.36, bf16[2,1024,1024]{2,1,0:T(8,128)(2,1)} %refs_3_.7, bf16[7,8,16,1024]{3,2,1,0:T(8,128)(2,1)} %bitcast.25, bf16[7,8,16,1024]{3,2,1,0:T(8,128)(2,1)} %refs_4_.6), custom_call_target="tpu_custom_call" | custom-call | flops 268435456 | bytes 4194304 | tf_op jit(solution)/shard_map/mixback/pallas_call | solution.py:111
  42.3 4.7 %middle.1 = (bf16[128,512]{1,0:T(8,128)(2,1)S(1)}, bf16[128,512]{1,0:T(8,128)(2,1)S(1)}, bf16[128,1024]{1,0:T(8,128)(2,1)S(1)}, bf16[8,64,128]{2,1,0:T(8,128)(2,...) custom-call(s32[1]{0:T(128)S(6)} %copy.22.refs_0_.refs_1_, ...), custom_call_target="tpu_custom_call" | custom-call | flops 268435456 | bytes 4194304 | tf_op jit(solution)/shard_map/middle/pallas_call | solution.py:111
  51.0 4.9 %scores.1 = (bf16[256,128]{1,0:T(8,128)(2,1)}, bf16[128,16]{1,0:T(8,128)(2,1)}, f32[128,128]{1,0:T(8,128)}) custom-call(s32[1]{0:T(128)S(6)} %copy.22.refs_0_.refs_1_, bf16[128,1024]{1,0:T(8,128)(2,1)S(1)} %get-tuple-element.136.refs_1_, s32[128,128]{1,0:T(8,128)} %get-tuple-element.137.refs_2_, s32[8,128]{1,0:T(8,128)} %copy-done, ...), custom_call_target="tpu_custom_call" | custom-call | flops 268435456 | bytes 4194304 | tf_op jit(solution)/shard_map/scores/pallas_call | solution.py:111
  55.9 5.5 %all-to-all-start.2 = ((bf16[32,8,128]{2,1,0:T(8,128)(2,1)}), bf16[32,8,128]{2,1,0:T(8,128)(2,1)S(1)}, u32[]{:S(2)}, u32[]{:S(2)}) async-start(bf16[32,8,128]{2,1,0:T(8,128)(2,1)} %bitcast.6), calls=%async_computation.2 | async-start | bytes 131072 | tf_op jit(solution)/shard_map/all_to_all | solution.py:973
  63.6 5.2 %all-to-all-done.2 = bf16[32,8,128]{2,1,0:T(8,128)(2,1)S(1)} async-done(((bf16[32,8,128]{2,1,0:T(8,128)(2,1)}), bf16[32,8,128]{2,1,0:T(8,128)(2,1)S(1)}, u32[]{:S(2)}, u32[]{:S(2)}) %all-to-all-start.2) | async-done | bytes 65568 | tf_op jit(solution)/shard_map/all_to_all | solution.py:973
  68.8 3.7 %all-to-all-start.3 = ((bf16[8,4,32,512]{3,2,1,0:T(8,128)(2,1)}), bf16[8,4,32,512]{3,2,1,0:T(8,128)(2,1)S(1)}, u32[]{:S(2)}, u32[]{:S(2)}) async-start(bf16[8,4,32,512]{3,2,1,0:T(8,128)(2,1)} %scatterleft.1), calls=%async_computation.3 | async-start | bytes 2097152 | tf_op jit(solution)/shard_map/all_to_all | solution.py:973
  72.6 6.6 %prepare.1 = (s32[256,128]{1,0:T(8,128)}, s16[1024,2048]{1,0:T(8,128)(2,1)}) custom-call(bf16[8,64,128]{2,1,0:T(8,128)(2,1)} %get-tuple-element.140.refs_0_), custom_call_target="tpu_custom_call" | custom-call | flops 268435456 | bytes 4194304 | tf_op jit(solution)/shard_map/prepare/pallas_call | solution.py:111
  79.2 11.4 %recall.1 = bf16[8,4,32,1024]{3,2,1,0:T(8,128)(2,1)} custom-call(bf16[256,128]{1,0:T(8,128)(2,1)S(1)} %bitcast.23, s16[1024,2048]{1,0:T(8,128)(2,1)} %get-tuple-element.141.refs_1_, bf16[2048,1024]{1,0:T(8,128)(2,1)} %refs_3_.6), custom_call_target="tpu_custom_call" | custom-call | flops 4294967296 | bytes 4194304 | tf_op jit(solution)/shard_map/recall/pallas_call | solution.py:111
  90.6 4.0 %all-to-all-start.4 = ((bf16[8,4,32,1024]{3,2,1,0:T(8,128)(2,1)}), bf16[8,4,32,1024]{3,2,1,0:T(8,128)(2,1)S(1)}, u32[]{:S(2)}, u32[]{:S(2)}) async-start(bf16[8,4,32,1024]{3,2,1,0:T(8,128)(2,1)} %recall.1), calls=%async_computation.4 | async-start | bytes 4194304 | tf_op jit(solution)/shard_map/all_to_all | solution.py:973
  97.3 3.3 %collective-permute-done.11.refs_7_ = bf16[128,512]{1,0:T(8,128)(2,1)S(1)} collective-permute-done((bf16[128,512]{1,0:T(8,128)(2,1)S(1)}, bf16[128,512]{1,0:T(8,128)(2,1)S(1)}, u32[]{:S(2)}, u32[]{:S(2)}) %collective-permute-start.11) | collective-permute-done | bytes 131104 | tf_op jit(solution)/shard_map/ppermute | solution.py:956
  100.6 8.3 %collective-permute-done.10.refs_6_ = bf16[128,512]{1,0:T(8,128)(2,1)S(1)} collective-permute-done((bf16[128,512]{1,0:T(8,128)(2,1)S(1)}, bf16[128,512]{1,0:T(8,128)(2,1)S(1)}, u32[]{:S(2)}, u32[]{:S(2)}) %collective-permute-start.10) | collective-permute-done | bytes 131104 | tf_op jit(solution)/shard_map/ppermute | solution.py:956
  111.2 6.2 %recallleft.1.refs_1_ = f32[256,128]{1,0:T(8,128)} custom-call(s32[256,128]{1,0:T(8,128)} %get-tuple-element.144.refs_0_, bf16[1024,512]{1,0:T(8,128)(2,1)S(1)} %bitcast.18, bf16[2048,1024]{1,0:T(8,128)(2,1)} %refs_3_.6), custom_call_target="tpu_custom_call" | custom-call | flops 2147483648 | bytes 4194304 | tf_op jit(solution)/shard_map/recallleft/pallas_call | solution.py:111
  117.3 3.9 %all-to-all-done.4.refs_4_ = bf16[8,4,32,1024]{3,2,1,0:T(8,128)(2,1)S(1)} async-done(((bf16[8,4,32,1024]{3,2,1,0:T(8,128)(2,1)}), bf16[8,4,32,1024]{3,2,1,0:T(8,128)(2,1)S(1)}, u32[]{:S(2)}, u32[]{:S(2)}) %all-to-all-start.4) | async-done | bytes 2097184 | tf_op jit(solution)/shard_map/all_to_all | solution.py:973
  121.2 3.6 %all-to-all-start.5 = ((bf16[8,4,32,512]{3,2,1,0:T(8,128)(2,1)}), bf16[8,4,32,512]{3,2,1,0:T(8,128)(2,1)S(1)}, u32[]{:S(2)}, u32[]{:S(2)}) async-start(bf16[8,4,32,512]{3,2,1,0:T(8,128)(2,1)} %scatterright.1), calls=%async_computation.5 | async-start | bytes 2097152 | tf_op jit(solution)/shard_map/all_to_all | solution.py:973
  129.6 10.5 %all-to-all-done.5 = bf16[8,4,32,512]{3,2,1,0:T(8,128)(2,1)S(1)} async-done(((bf16[8,4,32,512]{3,2,1,0:T(8,128)(2,1)}), bf16[8,4,32,512]{3,2,1,0:T(8,128)(2,1)S(1)}, u32[]{:S(2)}, u32[]{:S(2)}) %all-to-all-start.5) | async-done | bytes 1048608 | tf_op jit(solution)/shard_map/all_to_all | solution.py:973
  140.1 6.2 %recallright.1 = bf16[256,128]{1,0:T(8,128)(2,1)} custom-call(s32[256,128]{1,0:T(8,128)} %get-tuple-element.144.refs_0_, f32[256,128]{1,0:T(8,128)} %recallleft.1.refs_1_, bf16[1024,512]{1,0:T(8,128)(2,1)S(1)} %bitcast.19, bf16[2048,1024]{1,0:T(8,128)(2,1)} %refs_3_.6), custom_call_target="tpu_custom_call" | custom-call | flops 2147483648 | bytes 4194304 | tf_op jit(solution)/shard_map/recallright/pallas_call | solution.py:111
  149.0 3.8 %collective-permute-done.13.refs_5_ = bf16[128,1024]{1,0:T(8,128)(2,1)S(1)} collective-permute-done((bf16[128,1024]{1,0:T(8,128)(2,1)}, bf16[128,1024]{1,0:T(8,128)(2,1)S(1)}, u32[]{:S(2)}, u32[]{:S(2)}) %collective-permute-start.13) | collective-permute-done | bytes 262176 | tf_op jit(solution)/shard_map/ppermute | solution.py:956
  152.8 3.6 %memory.1 = (bf16[128,1024]{1,0:T(8,128)(2,1)}, bf16[128,16]{1,0:T(8,128)(2,1)}, bf16[128,1024]{1,0:T(8,128)(2,1)}, f32[128,1024]{1,0:T(8,128)}) custom-call(s32[1]{0:T(128)S(6)} %copy.22.refs_0_.refs_1_, f32[128,1024]{1,0:T(8,128)} %get-tuple-element.122.refs_1_, bf16[128,1024]{1,0:T(8,128)(2,1)} %get-tuple-element.121.refs_4_.refs_2_, ...), custom_call_target="tpu_custom_call" | custom-call | flops 268435456 | bytes 4194304 | tf_op jit(solution)/shard_map/memory/pallas_call | solution.py:111
  156.4 9.0 %query.1 = (bf16[8,128,128]{2,1,0:T(8,128)(2,1)}, bf16[128,1024]{1,0:T(8,128)(2,1)}, bf16[2,128,16]{2,1,0:T(8,128)(2,1)}, f32[128,1024]{1,0:T(8,128)}) custom-call(s32[1]{0:T(128)S(6)} %copy.21.refs_0_, s32[1]{0:T(128)S(6)} %copy.22.refs_0_.refs_1_, bf16[256,128]{1,0:T(8,128)(2,1)S(1)} %bitcast.22, s32[128,128]{1,0:T(8,128)} %get-tuple-element.154.refs_3_, ...), custom_call_target="tpu_custom_call" | custom-call | flops 268435456 | bytes 4194304 | tf_op jit(solution)/shard_map/query/pallas_call | solution.py:111
  165.4 3.9 %all-to-all-start.7 = ((bf16[8,128,128]{2,1,0:T(8,128)(2,1)}), bf16[8,128,128]{2,1,0:T(8,128)(2,1)S(1)}, u32[]{:S(2)}, u32[]{:S(2)}) async-start(bf16[8,128,128]{2,1,0:T(8,128)(2,1)} %get-tuple-element.158), calls=%async_computation.7 | async-start | bytes 524288 | tf_op jit(solution)/shard_map/all_to_all | solution.py:973
  176.2 3.4 %all-to-all-start.8 = ((bf16[8,128,128]{2,1,0:T(8,128)(2,1)}), bf16[8,128,128]{2,1,0:T(8,128)(2,1)S(1)}, u32[]{:S(2)}, u32[]{:S(2)}) async-start(bf16[8,128,128]{2,1,0:T(8,128)(2,1)} %factors.1), calls=%async_computation.8 | async-start | bytes 524288 | tf_op jit(solution)/shard_map/all_to_all | solution.py:973
  179.7 8.2 %attendback.1 = bf16[1024,384]{1,0:T(8,128)(2,1)} custom-call(s32[1]{0:T(128)S(6)} %copy.21.refs_0_, bf16[1024,384]{1,0:T(8,128)(2,1)} %get-tuple-element.161.refs_1_, bf16[1024,128]{1,0:T(8,128)(2,1)S(1)} %bitcast.20, f32[8,1024]{1,0:T(8,128)} %get-tuple-element.174.refs_3_), custom_call_target="tpu_custom_call" | custom-call | flops 268435456 | bytes 4194304 | tf_op jit(solution)/shard_map/attendback/pallas_call | solution.py:111
  187.8 4.1 %all-to-all-start.9 = ((bf16[8,128,384]{2,1,0:T(8,128)(2,1)}), bf16[8,128,384]{2,1,0:T(8,128)(2,1)S(1)}, u32[]{:S(2)}, u32[]{:S(2)}) async-start(bf16[8,128,384]{2,1,0:T(8,128)(2,1)} %bitcast.15), calls=%async_computation.9 | async-start | bytes 1572864 | tf_op jit(solution)/shard_map/all_to_all | solution.py:973
  200.3 4.2 %all-to-all-done.9.refs_1_ = bf16[8,128,384]{2,1,0:T(8,128)(2,1)S(1)} async-done(((bf16[8,128,384]{2,1,0:T(8,128)(2,1)}), bf16[8,128,384]{2,1,0:T(8,128)(2,1)S(1)}, u32[]{:S(2)}, u32[]{:S(2)}) %all-to-all-start.9) | async-done | bytes 786464 | tf_op jit(solution)/shard_map/all_to_all | solution.py:973
  207.4 3.4 %all-to-all-start.10 = ((bf16[8,96,128]{2,1,0:T(8,128)(2,1)}), bf16[8,96,128]{2,1,0:T(8,128)(2,1)S(1)}, u32[]{:S(2)}, u32[]{:S(2)}) async-start(bf16[8,96,128]{2,1,0:T(8,128)(2,1)} %get-tuple-element.181), calls=%async_computation.10 | async-start | bytes 393216 | tf_op jit(solution)/shard_map/all_to_all | solution.py:973
  214.3 6.0 %entry.1 = bf16[128,1024]{1,0:T(8,128)(2,1)} custom-call(s32[1]{0:T(128)S(6)} %copy.22.refs_0_.refs_1_, bf16[3,128,1024]{2,1,0:T(8,128)(2,1)} %get-tuple-element.183.refs_1_, bf16[128,48]{1,0:T(8,128)(2,1)} %get-tuple-element.184.refs_2_, bf16[128,1024]{1,0:T(8,128)(2,1)} %bitcast.35, bf16[1024]{0:T(1024)(128)(2,1)} %refs_4_.7, ...), custom_call_target="tpu_custom_call" | custom-call | flops 268435456 | bytes 4194304 | tf_op jit(solution)/shard_map/entry/pallas_call | solution.py:111
  234.1 3.7 %spread.1 = (f32[7,8,16,1024]{3,2,1,0:T(8,128)}, f32[7,8,16,1024]{3,2,1,0:T(8,128)}) custom-call(s32[256,128]{1,0:T(8,128)} %get-tuple-element.144.refs_0_, bf16[4,4,128,128]{3,2,1,0:T(8,128)(2,1)S(1)} %pairsearly.1.refs_1_, bf16[4,4,128,128]{3,2,1,0:T(8,128)(2,1)S(1)} %collective-permute-done.27.refs_2_), custom_call_target="tpu_custom_call" | custom-call | flops 268435456 | bytes 4194304 | tf_op jit(solution)/shard_map/spread/pallas_call | solution.py:111
  (84 shorter events, 73.2 us)
Async XLA Ops:
  7.0 17.8 %all-to-all-start = ((bf16[8,128,384]{2,1,0:T(8,128)(2,1)}), bf16[8,128,384]{2,1,0:T(8,128)(2,1)S(1)}, u32[]{:S(2)}, u32[]{:S(2)}) async-start(bf16[8,128,384]{2,1,0:T(8,128)(2,1)} %get-tuple-element.105), calls=%async_computation | async-start | bytes 1572864 | tf_op jit(solution)/shard_map/all_to_all | solution.py:973
  14.8 6.2 %collective-permute-start = (s32[64,128]{1,0:T(8,128)S(1)}, s32[64,128]{1,0:T(8,128)S(1)}, u32[]{:S(2)}, u32[]{:S(2)}) collective-permute-start(s32[64,128]{1,0:T(8,128)S(1)} %get-tuple-element.107), channel_id=1, source_target_pairs={{0,8},{8,16},{16,24},{24,0},{1,9},{9,17},{17,25},{25,1},{2,10},{10... | collective-permute-start | bytes 98312 | tf_op jit(solution)/shard_map/ppermute | solution.py:956
  29.8 12.5 %all-to-all-start.1 = ((bf16[8,192,128]{2,1,0:T(8,128)(2,1)}), bf16[8,192,128]{2,1,0:T(8,128)(2,1)S(1)}, u32[]{:S(2)}, u32[]{:S(2)}) async-start(bf16[8,192,128]{2,1,0:T(8,128)(2,1)} %get-tuple-element.115), calls=%async_computation.1 | async-start | bytes 786432 | tf_op jit(solution)/shard_map/all_to_all | solution.py:973
  33.2 8.0 %collective-permute-start.5 = (s32[8,128]{1,0:T(8,128)S(1)}, s32[8,128]{1,0:T(8,128)S(1)}, u32[]{:S(2)}, u32[]{:S(2)}) collective-permute-start(s32[8,128]{1,0:T(8,128)S(1)} %get-tuple-element.123.refs_0_.refs_3_), channel_id=1, source_target_pairs={{0,24},{8,0},{16,8},{24,16},{1,25},{9,1},{17,9},{25,17},{2,26},{10... | collective-permute-start | bytes 12296 | tf_op jit(solution)/shard_map/ppermute | solution.py:956
  36.9 5.4 %collective-permute-start.3 = (s32[8,128]{1,0:T(8,128)S(1)}, s32[8,128]{1,0:T(8,128)S(1)}, u32[]{:S(2)}, u32[]{:S(2)}) collective-permute-start(s32[8,128]{1,0:T(8,128)S(1)} %get-tuple-element.123.refs_0_.refs_3_), channel_id=1, source_target_pairs={{0,8},{8,16},{16,24},{24,0},{1,9},{9,17},{17,25},{25,1},{2,10},{10... | collective-permute-start | bytes 12296 | tf_op jit(solution)/shard_map/ppermute | solution.py:956
  47.1 14.3 %collective-permute-start.8 = (bf16[128,512]{1,0:T(8,128)(2,1)S(1)}, bf16[128,512]{1,0:T(8,128)(2,1)S(1)}, u32[]{:S(2)}, u32[]{:S(2)}) collective-permute-start(bf16[128,512]{1,0:T(8,128)(2,1)S(1)} %get-tuple-element.131.refs_4_), channel_id=1, source_target_pairs={{0,24},{8,0},{16,8},{24,16},{1,25},{9,1},{17,9},{25,17},{2,26},{10... | collective-permute-start | bytes 393224 | tf_op jit(solution)/shard_map/ppermute | solution.py:956
  49.9 11.5 %collective-permute-start.7 = (bf16[128,512]{1,0:T(8,128)(2,1)S(1)}, bf16[128,512]{1,0:T(8,128)(2,1)S(1)}, u32[]{:S(2)}, u32[]{:S(2)}) collective-permute-start(bf16[128,512]{1,0:T(8,128)(2,1)S(1)} %get-tuple-element.131.refs_4_), channel_id=1, source_target_pairs={{0,16},{8,24},{16,0},{24,8},{1,17},{9,25},{17,1},{25,9},{2,18},{10... | collective-permute-start | bytes 393224 | tf_op jit(solution)/shard_map/ppermute | solution.py:956
  50.1 11.4 %collective-permute-start.6 = (bf16[128,512]{1,0:T(8,128)(2,1)S(1)}, bf16[128,512]{1,0:T(8,128)(2,1)S(1)}, u32[]{:S(2)}, u32[]{:S(2)}) collective-permute-start(bf16[128,512]{1,0:T(8,128)(2,1)S(1)} %get-tuple-element.131.refs_4_), channel_id=1, source_target_pairs={{0,8},{8,16},{16,24},{24,0},{1,9},{9,17},{17,25},{25,1},{2,10},{10... | collective-permute-start | bytes 393224 | tf_op jit(solution)/shard_map/ppermute | solution.py:956
  55.9 12.9 %all-to-all-start.2 = ((bf16[32,8,128]{2,1,0:T(8,128)(2,1)}), bf16[32,8,128]{2,1,0:T(8,128)(2,1)S(1)}, u32[]{:S(2)}, u32[]{:S(2)}) async-start(bf16[32,8,128]{2,1,0:T(8,128)(2,1)} %bitcast.6), calls=%async_computation.2 | async-start | bytes 131072 | tf_op jit(solution)/shard_map/all_to_all | solution.py:973
  68.8 21.8 %all-to-all-start.3 = ((bf16[8,4,32,512]{3,2,1,0:T(8,128)(2,1)}), bf16[8,4,32,512]{3,2,1,0:T(8,128)(2,1)S(1)}, u32[]{:S(2)}, u32[]{:S(2)}) async-start(bf16[8,4,32,512]{3,2,1,0:T(8,128)(2,1)} %scatterleft.1), calls=%async_computation.3 | async-start | bytes 2097152 | tf_op jit(solution)/shard_map/all_to_all | solution.py:973
  90.6 30.6 %all-to-all-start.4 = ((bf16[8,4,32,1024]{3,2,1,0:T(8,128)(2,1)}), bf16[8,4,32,1024]{3,2,1,0:T(8,128)(2,1)S(1)}, u32[]{:S(2)}, u32[]{:S(2)}) async-start(bf16[8,4,32,1024]{3,2,1,0:T(8,128)(2,1)} %recall.1), calls=%async_computation.4 | async-start | bytes 4194304 | tf_op jit(solution)/shard_map/all_to_all | solution.py:973
  94.6 6.0 %collective-permute-start.11 = (bf16[128,512]{1,0:T(8,128)(2,1)S(1)}, bf16[128,512]{1,0:T(8,128)(2,1)S(1)}, u32[]{:S(2)}, u32[]{:S(2)}) collective-permute-start(bf16[128,512]{1,0:T(8,128)(2,1)S(1)} %get-tuple-element.129.refs_4_), channel_id=1, source_target_pairs={{0,24},{8,0},{16,8},{24,16},{1,25},{9,1},{17,9},{25,17},{2,26},{10... | collective-permute-start | bytes 393224 | tf_op jit(solution)/shard_map/ppermute | solution.py:956
  95.5 13.5 %collective-permute-start.10 = (bf16[128,512]{1,0:T(8,128)(2,1)S(1)}, bf16[128,512]{1,0:T(8,128)(2,1)S(1)}, u32[]{:S(2)}, u32[]{:S(2)}) collective-permute-start(bf16[128,512]{1,0:T(8,128)(2,1)S(1)} %get-tuple-element.129.refs_4_), channel_id=1, source_target_pairs={{0,16},{8,24},{16,0},{24,8},{1,17},{9,25},{17,1},{25,9},{2,18},{10... | collective-permute-start | bytes 393224 | tf_op jit(solution)/shard_map/ppermute | solution.py:956
  96.7 12.3 %collective-permute-start.9 = (bf16[128,512]{1,0:T(8,128)(2,1)S(1)}, bf16[128,512]{1,0:T(8,128)(2,1)S(1)}, u32[]{:S(2)}, u32[]{:S(2)}) collective-permute-start(bf16[128,512]{1,0:T(8,128)(2,1)S(1)} %get-tuple-element.129.refs_4_), channel_id=1, source_target_pairs={{0,8},{8,16},{16,24},{24,0},{1,9},{9,17},{17,25},{25,1},{2,10},{10... | collective-permute-start | bytes 393224 | tf_op jit(solution)/shard_map/ppermute | solution.py:956
  121.2 18.9 %all-to-all-start.5 = ((bf16[8,4,32,512]{3,2,1,0:T(8,128)(2,1)}), bf16[8,4,32,512]{3,2,1,0:T(8,128)(2,1)S(1)}, u32[]{:S(2)}, u32[]{:S(2)}) async-start(bf16[8,4,32,512]{3,2,1,0:T(8,128)(2,1)} %scatterright.1), calls=%async_computation.5 | async-start | bytes 2097152 | tf_op jit(solution)/shard_map/all_to_all | solution.py:973
  126.9 22.1 %collective-permute-start.12 = (bf16[128,1024]{1,0:T(8,128)(2,1)}, bf16[128,1024]{1,0:T(8,128)(2,1)S(1)}, u32[]{:S(2)}, u32[]{:S(2)}) collective-permute-start(bf16[128,1024]{1,0:T(8,128)(2,1)} %get-tuple-element.148), channel_id=1, source_target_pairs={{0,24},{8,0},{16,8},{24,16},{1,25},{9,1},{17,9},{25,17},{2,26},{10... | collective-permute-start | bytes 786440 | tf_op jit(solution)/shard_map/ppermute | solution.py:956
  127.8 24.9 %collective-permute-start.13 = (bf16[128,1024]{1,0:T(8,128)(2,1)}, bf16[128,1024]{1,0:T(8,128)(2,1)S(1)}, u32[]{:S(2)}, u32[]{:S(2)}) collective-permute-start(bf16[128,1024]{1,0:T(8,128)(2,1)} %get-tuple-element.149), channel_id=1, source_target_pairs={{0,16},{8,24},{16,0},{24,8},{1,17},{9,25},{17,1},{25,9},{2,18},{10... | collective-permute-start | bytes 786440 | tf_op jit(solution)/shard_map/ppermute | solution.py:956
  129.0 23.8 %collective-permute-start.14 = (bf16[128,1024]{1,0:T(8,128)(2,1)}, bf16[128,1024]{1,0:T(8,128)(2,1)S(1)}, u32[]{:S(2)}, u32[]{:S(2)}) collective-permute-start(bf16[128,1024]{1,0:T(8,128)(2,1)} %get-tuple-element.150), channel_id=1, source_target_pairs={{0,8},{8,16},{16,24},{24,0},{1,9},{9,17},{17,25},{25,1},{2,10},{10... | collective-permute-start | bytes 786440 | tf_op jit(solution)/shard_map/ppermute | solution.py:956
  146.4 10.0 %all-to-all-start.6 = ((bf16[32,8,128]{2,1,0:T(8,128)(2,1)}), bf16[32,8,128]{2,1,0:T(8,128)(2,1)S(1)}, u32[]{:S(2)}, u32[]{:S(2)}) async-start(bf16[32,8,128]{2,1,0:T(8,128)(2,1)} %bitcast.10), calls=%async_computation.6 | async-start | bytes 131072 | tf_op jit(solution)/shard_map/all_to_all | solution.py:973
  165.4 10.8 %all-to-all-start.7 = ((bf16[8,128,128]{2,1,0:T(8,128)(2,1)}), bf16[8,128,128]{2,1,0:T(8,128)(2,1)S(1)}, u32[]{:S(2)}, u32[]{:S(2)}) async-start(bf16[8,128,128]{2,1,0:T(8,128)(2,1)} %get-tuple-element.158), calls=%async_computation.7 | async-start | bytes 524288 | tf_op jit(solution)/shard_map/all_to_all | solution.py:973
  176.2 11.6 %all-to-all-start.8 = ((bf16[8,128,128]{2,1,0:T(8,128)(2,1)}), bf16[8,128,128]{2,1,0:T(8,128)(2,1)S(1)}, u32[]{:S(2)}, u32[]{:S(2)}) async-start(bf16[8,128,128]{2,1,0:T(8,128)(2,1)} %factors.1), calls=%async_computation.8 | async-start | bytes 524288 | tf_op jit(solution)/shard_map/all_to_all | solution.py:973
  187.8 16.7 %all-to-all-start.9 = ((bf16[8,128,384]{2,1,0:T(8,128)(2,1)}), bf16[8,128,384]{2,1,0:T(8,128)(2,1)S(1)}, u32[]{:S(2)}, u32[]{:S(2)}) async-start(bf16[8,128,384]{2,1,0:T(8,128)(2,1)} %bitcast.15), calls=%async_computation.9 | async-start | bytes 1572864 | tf_op jit(solution)/shard_map/all_to_all | solution.py:973
  193.8 5.0 %collective-permute-start.16 = (bf16[128,128]{1,0:T(8,128)(2,1)S(1)}, bf16[128,128]{1,0:T(8,128)(2,1)S(1)}, u32[]{:S(2)}, u32[]{:S(2)}) collective-permute-start(bf16[128,128]{1,0:T(8,128)(2,1)S(1)} %sumearly.1.refs_0_), channel_id=1, source_target_pairs={{0,16},{8,24},{16,0},{24,8},{1,17},{9,25},{17,1},{25,9},{2,18},{10... | collective-permute-start | bytes 98312 | tf_op jit(solution)/shard_map/ppermute | solution.py:956
  194.6 5.7 %collective-permute-start.15 = (bf16[128,128]{1,0:T(8,128)(2,1)S(1)}, bf16[128,128]{1,0:T(8,128)(2,1)S(1)}, u32[]{:S(2)}, u32[]{:S(2)}) collective-permute-start(bf16[128,128]{1,0:T(8,128)(2,1)S(1)} %sumearly.1.refs_0_), channel_id=1, source_target_pairs={{0,8},{8,16},{16,24},{24,0},{1,9},{9,17},{17,25},{25,1},{2,10},{10... | collective-permute-start | bytes 98312 | tf_op jit(solution)/shard_map/ppermute | solution.py:956
  207.4 14.9 %all-to-all-start.10 = ((bf16[8,96,128]{2,1,0:T(8,128)(2,1)}), bf16[8,96,128]{2,1,0:T(8,128)(2,1)S(1)}, u32[]{:S(2)}, u32[]{:S(2)}) async-start(bf16[8,96,128]{2,1,0:T(8,128)(2,1)} %get-tuple-element.181), calls=%async_computation.10 | async-start | bytes 393216 | tf_op jit(solution)/shard_map/all_to_all | solution.py:973
  210.8 9.5 %collective-permute-start.20 = (bf16[4,128,128]{2,1,0:T(8,128)(2,1)S(1)}, bf16[4,128,128]{2,1,0:T(8,128)(2,1)S(1)}, u32[]{:S(2)}, u32[]{:S(2)}) collective-permute-start(bf16[4,128,128]{2,1,0:T(8,128)(2,1)S(1)} %stackearly.1.refs_0_), channel_id=1, source_target_pairs={{0,6},{1,7},{2,4},{3,5},{4,2},{5,3},{6,0},{7,1},{8,14},{9,15},{10,... | collective-permute-start | bytes 393224 | tf_op jit(solution)/shard_map/ppermute | solution.py:960
  213.6 8.7 %collective-permute-start.19 = (bf16[4,128,128]{2,1,0:T(8,128)(2,1)S(1)}, bf16[4,128,128]{2,1,0:T(8,128)(2,1)S(1)}, u32[]{:S(2)}, u32[]{:S(2)}) collective-permute-start(bf16[4,128,128]{2,1,0:T(8,128)(2,1)S(1)} %stackearly.1.refs_0_), channel_id=1, source_target_pairs={{0,4},{1,5},{2,6},{3,7},{4,0},{5,1},{6,2},{7,3},{8,12},{9,13},{10,... | collective-permute-start | bytes 393224 | tf_op jit(solution)/shard_map/ppermute | solution.py:960
  214.2 8.1 %collective-permute-start.18 = (bf16[4,128,128]{2,1,0:T(8,128)(2,1)S(1)}, bf16[4,128,128]{2,1,0:T(8,128)(2,1)S(1)}, u32[]{:S(2)}, u32[]{:S(2)}) collective-permute-start(bf16[4,128,128]{2,1,0:T(8,128)(2,1)S(1)} %stackearly.1.refs_0_), channel_id=1, source_target_pairs={{0,2},{1,3},{2,0},{3,1},{4,6},{5,7},{6,4},{7,5},{8,10},{9,11},{10,... | collective-permute-start | bytes 393224 | tf_op jit(solution)/shard_map/ppermute | solution.py:960
  224.9 5.6 %collective-permute-start.21 = (bf16[96,128]{1,0:T(8,128)(2,1)S(1)}, bf16[96,128]{1,0:T(8,128)(2,1)S(1)}, u32[]{:S(2)}, u32[]{:S(2)}) collective-permute-start(bf16[96,128]{1,0:T(8,128)(2,1)S(1)} %sumlate.1.refs_0_), channel_id=1, source_target_pairs={{0,8},{8,16},{16,24},{24,0},{1,9},{9,17},{17,25},{25,1},{2,10},{10... | collective-permute-start | bytes 73736 | tf_op jit(solution)/shard_map/ppermute | solution.py:956
  230.6 7.3 %collective-permute-start.26 = (bf16[4,96,128]{2,1,0:T(8,128)(2,1)S(1)}, bf16[4,96,128]{2,1,0:T(8,128)(2,1)S(1)}, u32[]{:S(2)}, u32[]{:S(2)}) collective-permute-start(bf16[4,96,128]{2,1,0:T(8,128)(2,1)S(1)} %stacklate.1.refs_0_), channel_id=1, source_target_pairs={{0,6},{1,7},{2,4},{3,5},{4,2},{5,3},{6,0},{7,1},{8,14},{9,15},{10,... | collective-permute-start | bytes 294920 | tf_op jit(solution)/shard_map/ppermute | solution.py:960
  231.5 7.0 %collective-permute-start.25 = (bf16[4,96,128]{2,1,0:T(8,128)(2,1)S(1)}, bf16[4,96,128]{2,1,0:T(8,128)(2,1)S(1)}, u32[]{:S(2)}, u32[]{:S(2)}) collective-permute-start(bf16[4,96,128]{2,1,0:T(8,128)(2,1)S(1)} %stacklate.1.refs_0_), channel_id=1, source_target_pairs={{0,4},{1,5},{2,6},{3,7},{4,0},{5,1},{6,2},{7,3},{8,12},{9,13},{10,... | collective-permute-start | bytes 294920 | tf_op jit(solution)/shard_map/ppermute | solution.py:960
  232.9 5.6 %collective-permute-start.24 = (bf16[4,96,128]{2,1,0:T(8,128)(2,1)S(1)}, bf16[4,96,128]{2,1,0:T(8,128)(2,1)S(1)}, u32[]{:S(2)}, u32[]{:S(2)}) collective-permute-start(bf16[4,96,128]{2,1,0:T(8,128)(2,1)S(1)} %stacklate.1.refs_0_), channel_id=1, source_target_pairs={{0,2},{1,3},{2,0},{3,1},{4,6},{5,7},{6,4},{7,5},{8,10},{9,11},{10,... | collective-permute-start | bytes 294920 | tf_op jit(solution)/shard_map/ppermute | solution.py:960
  (12 other events, 75.2 us)
where the time goes:
time: 245 us; the launch traced here: 244 us
  Pallas kernels  105 us (43%)
  starting transfers between devices  78.7 us (32%)
  waiting for transfers between devices  56.9 us (23%)
  between operations  2.53 us (1%)
    pallas_call x28, Pallas kernels, call(): pl.pallas_call(wrapped, name=name, out_shape=[pltpu.HBM(out.shape, out.dt...  105 us
    all_to_all x11, starting transfers between devices, exchange(): return lax.all_to_all(values, axes, split_axis=0, concat_axis=0, tiled=True)  42.9 us
    ppermute x21, starting transfers between devices, along(): lax.ppermute(values, axis, [(i, (i + step) % size) for i in range(size)])  28.6 us
    all_to_all x11, waiting for transfers between devices, exchange(): return lax.all_to_all(values, axes, split_axis=0, concat_axis=0, tiled=True)  26.7 us
    ppermute x21, waiting for transfers between devices, along(): lax.ppermute(values, axis, [(i, (i + step) % size) for i in range(size)])  25.9 us
    ppermute x8, starting transfers between devices, across(): return lax.ppermute(values, axis, [(i, i ^ mask) for i in range(size)])  7.18 us
  transfers between devices with their start and end apart: 40, of which 20 were waited for; matrix products, arithmetic and copies ran while one was open for 0% of the time, Pallas kernels for 31%

commit v1 on v0

--- a/solution.py
+++ b/solution.py
@@ -78,7 +78,7 @@
             copy.wait()
 
 
-def call(kernel, name, ins, outs, args, scratch=(), vmem=40, flops=1 << 28, moved=1 << 22, aliases=None):
+def call(kernel, name, ins, outs, args, scratch=(), vmem=40, flops=1 << 12, moved=1 << 12, aliases=None):
     shapes = [(args[i].shape, args[i].dtype) for i, kind in enumerate(ins) if kind == "L"]
     stored = [(out.shape, out.dtype) for kind, out in outs if kind == "S"]
     count_in, count_out, count_user = len(ins), len(outs), len(scratch)
@@ -149,7 +149,7 @@
     return weighted * inverse - values * inverse * inverse * inverse * inner
 
 
-def qkv_kernel(ready, adapter, x_ref, gain_ref, w_any, dn_any, up_any, out_ref, norm_ref, rank_ref, w, dn, up, sems):
+def qkv_kernel(ready, adapter, x_ref, gain_ref, w_any, dn_any, up_any, out_ref, norm_ref, w, dn, up, sems):
     groups, tokens, wide = out_ref.shape
     cols = wide // 3
     a = adapter[0]
@@ -162,16 +162,16 @@
     ready()
     x = x_ref[...].astype(F32)
     normed = (x * inverse_norm(x) * gain_row(gain_ref)).astype(BF16)
-    norm_ref[...] = normed
-    ready.send(norm_ref)
+    width = normed.shape[1]
+    norm_ref[:, :width] = normed
     for copy in copies[:6]:
         copy.wait()
-    ranks = against(normed, dn[...]).astype(BF16)
-    rank_ref[...] = ranks
-    ready.send(rank_ref)
+    ranks = against(normed, dn[...])
+    norm_ref[:, width:] = widen(ranks).astype(BF16)
+    ready.send(norm_ref)
     place = iota((tokens, 3 * RANK), 1) // RANK
     for j in range(3):
-        own = jnp.where(place == j, ranks.astype(F32), 0.0).astype(BF16)
+        own = jnp.where(place == j, ranks, 0.0).astype(BF16)
         extra = product(own, up[...])
         copies[6 + j].wait()
         result = (product(normed, w[j]) + extra).astype(BF16)
@@ -234,7 +234,8 @@
     ids_refs[-1][...] = total.astype(I32) + adapter[0] * ADAPTER_STEP
     for k in range(batches):
         target = lax.rem(lax.axis_index("batch") + k, batches)
-        ids_refs[k][...] = ids_refs[-1][pl.ds(pl.multiple_of(target * part, part), part), :]
+        ids_refs[k][0:part, :] = ids_refs[-1][pl.ds(pl.multiple_of(target * part, part), part), :]
+        ids_refs[k][part:, :] = stacked
 
 
 def tile_groups(values, count):
@@ -431,7 +432,7 @@
 
 
 def attend_kernel(groups, batches, ready, length, qkv_ref, *refs):
-    o_ref, lse_ref, saved_any, parts, values_t, mixed, sems = refs[batches:]
+    o_ref, lse_ref, slots_ref, saved_any, parts, values_t, mixed, sems = refs[batches:]
     ready()
     saving = pltpu.make_async_copy(qkv_ref, saved_any, sems.at[0])
     saving.start()
@@ -439,6 +440,9 @@
     cols = wide // 3
     seq = o_ref.shape[0]
     lanes = groups * PICKS
+    for k in range(batches):
+        slots_ref[k] = refs[k][seq * 8 :, :]
+    ready.send(slots_ref)
     for s in range(seq):
         ids = jnp.concatenate([refs[k][s * 8 : (s + 1) * 8, :lanes] for k in range(batches)], axis=0)
         both = jnp.concatenate([ids // 256, ids % 256], axis=1).astype(F32).astype(BF16)
@@ -488,7 +492,22 @@
     saving.wait()
 
 
-def attend_back_kernel(ready, length, qkv_ref, go_ref, lse_ref, out_ref, dk, dv, dq, parts, keys_t, values):
+def attend_back_kernel(
+    ready, length, adapter, qkv_ref, go_ref, lse_ref, even_ref, odd_ref, up_any,
+    out_ref, upgrad_ref, dk, dv, dq, parts, keys_t, values, grads_all, norms, up, sems,
+):
+    a = adapter[0]
+    seq = out_ref.shape[0]
+    me = lax.axis_index("seq")
+    tokens = even_ref.shape[1]
+    copies = fetch(
+        [(up_any.at[j, a], up.at[pl.ds(RANK * j, RANK)]) for j in range(3)]
+        + [
+            ((even_ref, odd_ref)[m % 2].at[m // 2], norms.at[pl.ds(pl.multiple_of((me ^ m) * tokens, tokens), tokens)])
+            for m in range(seq)
+        ],
+        sems,
+    )
     ready()
     rows, wide = qkv_ref.shape
     cols = wide // 3
@@ -537,9 +556,29 @@
         return carry
 
     lax.fori_loop(0, heads, one, 0)
-    out_ref[:, 0:cols] = (jnp.transpose(dq[...]) * scaling)[:, :cols].astype(BF16)
-    out_ref[:, cols : 2 * cols] = dk[:, :cols].astype(BF16)
-    out_ref[:, 2 * cols :] = dv[:, :cols].astype(BF16)
+    grads_all[:, 0:cols] = (jnp.transpose(dq[...]) * scaling)[:, :cols].astype(BF16)
+    grads_all[:, cols : 2 * cols] = dk[:, :cols].astype(BF16)
+    grads_all[:, 2 * cols :] = dv[:, :cols].astype(BF16)
+    for s in range(seq):
+        out_ref[s, 0:tokens, :] = grads_all[s * tokens : (s + 1) * tokens, :]
+    for copy in copies:
+        copy.wait()
+    own = jnp.zeros((3 * RANK, cols), F32)
+    for s in range(seq):
+        own = jnp.where(me == s, up[:, s * cols : (s + 1) * cols].astype(F32), own)
+    own = own.astype(BF16)
+    place = iota((rows, 3 * RANK), 1) // RANK
+    granks = jnp.zeros((rows, 3 * RANK), F32)
+    for j in range(3):
+        granks = jnp.where(place == j, against(grads_all[:, j * cols : (j + 1) * cols], own), granks)
+    width = norms.shape[1] - LANES
+    down = contract(granks.astype(BF16), norms[:, :width]).astype(BF16)
+    both = contract(norms[:, width:], grads_all[...]).astype(BF16)
+    for j in range(3):
+        row = j * RANK
+        upgrad_ref[row : row + RANK, :] = both[row : row + RANK, j * cols : (j + 1) * cols]
+        for s in range(seq):
+            out_ref[s, tokens:, j * cols : (j + 1) * cols] = down[row : row + RANK, s * cols : (s + 1) * cols]
 
 
 def pick_chosen(tables, index):
@@ -657,38 +696,36 @@
     return total
 
 
-def plane_hits(slot_ref, plane, seq, capacity):
-    tokens = slot_ref.shape[1]
+def plane_hits(slots_ref, k, plane, seq, capacity):
+    tokens = slots_ref.shape[2]
     place = plane * (seq * capacity) + iota((seq * capacity, tokens), 0)
     chosen = jnp.zeros((seq * capacity, tokens), F32)
     for h in range(MHEADS):
-        chosen = jnp.where(place == slot_ref[h : h + 1, :], 1.0, chosen)
+        chosen = jnp.where(place == slots_ref[k, h : h + 1, :], 1.0, chosen)
     return chosen.astype(BF16)
 
 
-def scatter_kernel(ready, *refs):
+def scatter_kernel(ready, slots_ref, *refs):
     ready()
     out_ref = refs[-1]
     seq, batches, capacity, wide = out_ref.shape
     plane = lax.axis_index("batch")
     for k in range(batches):
-        chosen = plane_hits(refs[k], plane, seq, capacity)
-        rows = product(chosen, refs[batches + k][...]).astype(BF16)
+        chosen = plane_hits(slots_ref, k, plane, seq, capacity)
+        rows = product(chosen, refs[k][...]).astype(BF16)
         source = lax.rem(plane + (batches - k), batches)
         out_ref[:, pl.ds(source, 1)] = rows.reshape(seq, 1, capacity, wide)
 
 
-def gather_kernel(ready, *refs):
-    ready()
-    batches = (len(refs) - 1) // 2
-    back_ref = refs[batches]
-    seq, _, capacity, wide = back_ref.shape
+def gather_kernel(ready, slots_ref, back_ref, *refs):
+    ready()
+    seq, batches, capacity, wide = back_ref.shape
     plane = lax.axis_index("batch")
     for k in range(batches):
-        chosen = plane_hits(refs[k], plane, seq, capacity)
+        chosen = plane_hits(slots_ref, k, plane, seq, capacity)
         source = lax.rem(plane + (batches - k), batches)
         rows = back_ref[:, pl.ds(source, 1)].reshape(seq * capacity, wide)
-        refs[batches + 1 + k][...] = contract(chosen, rows).astype(BF16)
+        refs[k][...] = contract(chosen, rows).astype(BF16)
 
 
 def memory_kernel(batches, ready, adapter, gate_ref, mix_ref, *refs):
@@ -825,47 +862,46 @@
         place_columns(out_ref, half + j * RANK, contract(rank, gy))
 
 
-def entry_factor_kernel(ready, adapter, grad_ref, norm_ref, ranks_ref, up_any, out_ref, gy_ref, grank_ref, up, sems):
-    groups, tokens, wide = grad_ref.shape
+def late_kernel(ready, grads_ref, upgrad_ref, out_ref):
+    seq, _, wide = grads_ref.shape
     cols = wide // 3
+    tokens = grads_ref.shape[1] - RANK
+    total = grads_ref[0, tokens:, :].astype(F32)
+    for s in range(1, seq):
+        total = total + grads_ref[s, tokens:, :].astype(F32)
+    total = total.astype(BF16)
+    for j in range(3):
+        out_ref[j * RANK : (j + 1) * RANK, :] = total[:, j * cols : (j + 1) * cols]
+    ready()
+    out_ref[3 * RANK :, :] = upgrad_ref[...]
+
+
+def entry_kernel(ready, adapter, grads_ref, x_ref, gain_ref, gmid_ref, w_any, dn_any, up_any, out_ref, w, dn, up, sems):
     a = adapter[0]
-    copies = fetch([(up_any.at[j, a], up.at[pl.ds(RANK * j, RANK)]) for j in range(3)], sems)
+    seq, _, wide = grads_ref.shape
+    cols = wide // 3
+    tokens = out_ref.shape[0]
+    copies = fetch(
+        [(up_any.at[j, a], up.at[pl.ds(RANK * j, RANK)]) for j in range(3)]
+        + [(dn_any.at[j, a], dn.at[pl.ds(RANK * j, RANK)]) for j in range(3)]
+        + [(w_any.at[j], w.at[j]) for j in range(3)],
+        sems,
+    )
     gys = [
-        jnp.concatenate([grad_ref[s, :, j * cols : (j + 1) * cols] for s in range(groups)], axis=1) for j in range(3)
+        jnp.concatenate([grads_ref[s, 0:tokens, j * cols : (j + 1) * cols] for s in range(seq)], axis=1) for j in range(3)
     ]
-    for j in range(3):
-        gy_ref[j] = gys[j]
-    ready.send(gy_ref)
-    for copy in copies:
+    for copy in copies[:6]:
         copy.wait()
-    ready()
     place = iota((tokens, 3 * RANK), 1) // RANK
     granks = jnp.zeros((tokens, 3 * RANK), F32)
-    ranks = ranks_ref[...]
     for j in range(3):
         granks = jnp.where(place == j, against(gys[j], up[...]), granks)
-        up_grad = contract(ranks, gys[j])
-        place_columns(out_ref, (3 + j) * RANK, up_grad[j * RANK : (j + 1) * RANK, :])
-    granks = granks.astype(BF16)
-    grank_ref[...] = granks
-    ready.send(grank_ref)
-    place_columns(out_ref, 0, contract(granks, norm_ref[...]))
-
-
-def entry_kernel(ready, adapter, gy_ref, grank_ref, x_ref, gain_ref, gmid_ref, w_any, dn_any, out_ref, w, dn, sems):
-    a = adapter[0]
-    copies = fetch(
-        [(dn_any.at[j, a], dn.at[pl.ds(RANK * j, RANK)]) for j in range(3)] + [(w_any.at[j], w.at[j]) for j in range(3)],
-        sems,
-    )
+    total = product(granks.astype(BF16), dn[...])
+    for j in range(3):
+        copies[6 + j].wait()
+        total = total + against(gys[j], w[j])
     ready()
     x = x_ref[...].astype(F32)
-    for copy in copies[:3]:
-        copy.wait()
-    total = product(grank_ref[...], dn[...])
-    for j in range(3):
-        copies[3 + j].wait()
-        total = total + against(gy_ref[j], w[j])
     back = norm_back(x, inverse_norm(x), gain_row(gain_ref), total)
     out_ref[...] = (gmid_ref[...] + back).astype(BF16)
 
@@ -964,9 +1000,9 @@
     return [values] + [across(values, axis, m, size) for m in range(2, size, 2)]
 
 
-def stacked(values, name):
+def stacked(values, name, kind="V"):
     shape = shaped((len(values), *values[0].shape), values[0].dtype)
-    return call(stack_kernel, name, "V" * len(values), [("V", shape)], values)[0]
+    return call(stack_kernel, name, "V" * len(values), [(kind, shape)], values)[0]
 
 
 def exchange(values, axes):
@@ -1003,36 +1039,37 @@
     token_rank, token_lanes = shaped((tokens, RANK), BF16), shaped((tokens, LANES), F32)
     fixed = functools.partial
 
-    qkv, normed, ranks = call(
+    qkv, normed = call(
         qkv_kernel, "qkv", "MLLHHH",
-        [("V", shaped((seq, tokens, 3 * cols), BF16)), ("S", token_low), ("S", shaped((tokens, 3 * RANK), BF16))],
+        [("V", shaped((seq, tokens, 3 * cols), BF16)), ("S", shaped((tokens, width + LANES), BF16))],
         (adapter_index, x, gain_one, input_weights, down, adapter_up), [triple, three_small, three_small, sema(9)],
     )
     qkv_all = exchange(qkv, "seq").reshape(rows, 3 * cols)
 
     slot, slot_col, pick, *ids_out = call(
         fixed(route_kernel, rows_dev, owners), "route", "ML",
-        [("V", shaped((8, tokens), I32)), ("S", shaped((tokens, tokens), I32)), ("S", shaped((tokens, LANES), I32)),
-         *[("V", shaped((seq * 8, LANES), I32)) for _ in range(batches)]],
+        [("S", shaped((8, tokens), I32)), ("S", shaped((tokens, tokens), I32)), ("S", shaped((tokens, LANES), I32)),
+         *[("V", shaped((seq * 8 + 8, LANES), I32)) for _ in range(batches)]],
         (adapter_index, picks), [pltpu.VMEM((owners * 8, LANES), I32)],
     )
     ids_out = [ids_out[0]] + [along(ids_out[k], "batch", k, batches) for k in range(1, batches)]
-    qkv_all, ids_out = lax.optimization_barrier((qkv_all, ids_out))
-    attended, lse, qkv_saved = call(
+    mix_grad, grank_six = call(
+        mix_back_kernel, "mixback", "MLHHH", [("S", token_low), ("S", token_rank)],
+        (adapter_index, cot, output_weights, down, adapter_up), [matrix, small, small, sema(3)],
+    )
+
+    qkv_all, ids_out, mix_grad = lax.optimization_barrier((qkv_all, ids_out, mix_grad))
+    attended, lse, slots, qkv_saved = call(
         fixed(attend_kernel, groups, batches), "attend", "MV" + "V" * batches,
-        [("V", shaped((seq, tokens + carried, cols), BF16)), ("S", shaped((8, rows), F32)), ("H", shaped((rows, 3 * cols), BF16))],
+        [("V", shaped((seq, tokens + carried, cols), BF16)), ("S", shaped((8, rows), F32)),
+         ("S", shaped((batches, 8, LANES), I32)), ("H", shaped((rows, 3 * cols), BF16))],
         (lengths, qkv_all, *ids_out),
         [pltpu.VMEM((rows, LANES), BF16), pltpu.VMEM((LANES, rows), BF16), pltpu.VMEM((LANES, rows), F32), sema(1)],
     )
     o_all = exchange(attended, "seq")
-    slot, late_cot, attended = lax.optimization_barrier((slot, cot, attended))
-    slots = [slot] + [along(slot, "batch", k, batches) for k in range(1, batches)]
-    mix_grad, grank_six = call(
-        mix_back_kernel, "mixback", "MLHHH", [("S", token_low), ("S", token_rank)],
-        (adapter_index, late_cot, output_weights, down, adapter_up), [matrix, small, small, sema(3)],
-    )
-
-    o_all, mix_grad, slots = lax.optimization_barrier((o_all, mix_grad, slots))
+    normed, attended = lax.optimization_barrier((normed, attended))
+    normed_all = to_pairs(normed, "seq", seq)
+
     left, right, same_two, sent, att, rank_pair, middle, normed_two, gate = call(
         middle_kernel, "middle", "MVLLLHHHH",
         [("V", shaped((tokens, half), BF16)), ("V", shaped((tokens, half), BF16)), ("V", token_low),
@@ -1047,22 +1084,26 @@
         [("V", shaped((owners * 8, LANES), BF16)), ("S", token_rank), ("S", token_lanes)],
         (adapter_index, same_two, pick, slot, half_keys, input_weights, down, adapter_up), [matrix, small, small, sema(3)],
     )
+    weight_out, normed_all = lax.optimization_barrier((weight_out, normed_all))
     weight_in = exchange(weight_out.reshape(owners, 8, LANES), both).reshape(owners * 8, LANES)
     right, lefts = lax.optimization_barrier((right, lefts))
     rights = [right] + [along(right, "batch", k, batches) for k in range(1, batches)]
 
     def scatter(parts, name):
         out = [("V", shaped((seq, batches, capacity, half), BF16))]
-        return call(scatter_kernel, name, "L" * batches + "V" * batches, out, (*slots, *parts))[0]
+        return call(scatter_kernel, name, "L" + "V" * batches, out, (slots, *parts))[0]
 
     left_out = scatter(lefts, "scatterleft")
+    normed_all, left_out = lax.optimization_barrier((normed_all, left_out))
+    normed_all = stacked(normed_all, "pairsnorm", "S")
     sent, left_out = lax.optimization_barrier((sent, left_out))
     ids, index = call(
         fixed(prepare_kernel, groups, rows_dev, batches), "prepare", "L",
         [("S", shaped((owners * 8, LANES), I32)), ("H", shaped((items, rows_dev), jnp.int16))], (sent,),
         [pltpu.VMEM((2, LANES, rows_dev), jnp.int16), pltpu.VMEM((owners * 8 // LANES, LANES, LANES), I32), sema(2)],
     )
-    left_out, weight_in = lax.optimization_barrier((left_out, weight_in))
+    left_out, weight_in, normed_all = lax.optimization_barrier((left_out, weight_in, normed_all))
+    normed_all = (normed_all, across(normed_all, "seq", 1, seq))
     left_in = exchange(left_out, "seq").reshape(items, half)
 
     (sums,) = call(
@@ -1070,7 +1111,7 @@
         (weight_in, index, memory_values),
         [pltpu.VMEM((rows_dev, width), BF16), pltpu.VMEM((2, small_block, rows_dev), jnp.int16), pltpu.VMEM((2, small_block, rows_dev), BF16),
          pltpu.VMEM((2, small_block // 8, 8, width), BF16), sema(3 + 2 * (small_block // (8 * seq)))],
-        flops=1 << 32,
+        flops=1 << 12,
     )
     sums, left_in = lax.optimization_barrier((sums, left_in))
     back = exchange(sums, "seq")
@@ -1079,15 +1120,16 @@
         return call(
             fixed(recall_back_kernel, part, batches, groups), name, "L" + "L" * part + "VH",
             [(kind, shaped((owners * 8, LANES), dtype))], (ids, *before, grads, memory_values),
-            [pltpu.VMEM((rows_dev, half), BF16), pltpu.VMEM((block, rows_dev), F32), sema(1)], flops=1 << 31,
+            [pltpu.VMEM((rows_dev, half), BF16), pltpu.VMEM((block, rows_dev), F32), sema(1)],
         )[0]
 
+    rights, normed_all = lax.optimization_barrier((rights, normed_all))
     right_out = scatter(rights, "scatterright")
     found_left = recall_back(0, "recallleft", left_in, "S", F32)
     right_out, back, found_left = lax.optimization_barrier((right_out, back, found_left))
     right_in = exchange(right_out, "seq").reshape(items, half)
     pieces = call(
-        gather_kernel, "gather", "L" * batches + "V", [("V", token_low) for _ in range(batches)], (*slots, back),
+        gather_kernel, "gather", "LV", [("V", token_low) for _ in range(batches)], (slots, back),
     )
     pieces = [pieces[0]] + [along(pieces[k], "batch", batches - k, batches) for k in range(1, batches)]
     found = recall_back(1, "recallright", right_in, "V", BF16, found_left)
@@ -1119,33 +1161,29 @@
     factors, go_all = lax.optimization_barrier((factors, go_all))
     early_parts = exchange(factors, "seq")
 
-    (grads,) = call(
-        attend_back_kernel, "attendback", "MLVL", [("V", shaped((rows, 3 * cols), BF16))], (lengths, qkv_saved, go_all, lse),
+    grads, up_grads = call(
+        attend_back_kernel, "attendback", "MMLVLHHH",
+        [("V", shaped((seq, tokens + RANK, 3 * cols), BF16)), ("S", shaped((3 * RANK, cols), BF16))],
+        (lengths, adapter_index, qkv_saved, go_all, lse, *normed_all, adapter_up),
         [pltpu.VMEM((rows, LANES), F32), pltpu.VMEM((rows, LANES), F32), pltpu.VMEM((LANES, rows), F32),
-         pltpu.VMEM((rows, LANES), BF16), pltpu.VMEM((LANES, rows), BF16), pltpu.VMEM((rows, LANES), BF16)],
+         pltpu.VMEM((rows, LANES), BF16), pltpu.VMEM((LANES, rows), BF16), pltpu.VMEM((rows, LANES), BF16),
+         pltpu.VMEM((rows, 3 * cols), BF16), pltpu.VMEM((rows, width + LANES), BF16), three_small, sema(3 + seq)],
     )
     grads, early_parts = lax.optimization_barrier((grads, early_parts))
-    grads_all = exchange(grads.reshape(seq, tokens, 3 * cols), "seq")
+    grads_all = exchange(grads, "seq")
     (some,) = call(sum_kernel, "sumearly", "V", [("V", shaped((8 * RANK, cols), BF16))], (early_parts,))
     some = [some] + [along(some, "batch", k, batches) for k in range(1, batches)]
     some = stacked(some, "stackearly")
-    late, gys, granks = call(
-        entry_factor_kernel, "entryfactors", "MVLLH",
-        [("V", shaped((seq, 6 * RANK, cols), BF16)), ("S", shaped((3, tokens, width), BF16)), ("S", shaped((tokens, 3 * RANK), BF16))],
-        (adapter_index, grads_all, normed, ranks, adapter_up), [three_small, sema(3)],
-    )
-    late, some = lax.optimization_barrier((late, some))
-    late_parts = exchange(late, "seq")
     some = to_pairs(some, "seq", seq)
+    (late_sum,) = call(late_kernel, "late", "VL", [("V", shaped((6 * RANK, cols), BF16))], (grads_all, up_grads))
     (grad_input,) = call(
-        entry_kernel, "entry", "MLLLLLHH", [("S", token_low)],
-        (adapter_index, gys, granks, x, gain_one, gmid, input_weights, down), [triple, three_small, sema(6)],
-    )
-    late_parts, some, grad_input = lax.optimization_barrier((late_parts, some, grad_input))
-    (late_sum,) = call(sum_kernel, "sumlate", "V", [("V", shaped((6 * RANK, cols), BF16))], (late_parts,))
+        entry_kernel, "entry", "MVLLLHHH", [("S", token_low)],
+        (adapter_index, grads_all, x, gain_one, gmid, input_weights, down, adapter_up),
+        [triple, three_small, three_small, sema(9)],
+    )
     late_sums = [late_sum] + [along(late_sum, "batch", k, batches) for k in range(1, batches)]
     some = stacked(some, "pairsearly")
-    late_sums, some = lax.optimization_barrier((late_sums, some))
+    late_sums, some, grad_input = lax.optimization_barrier((late_sums, some, grad_input))
     late_all = to_pairs(stacked(late_sums, "stacklate"), "seq", seq)
     some = (some, across(some, "seq", 1, seq))
     full = shaped((7, ADAPTERS, RANK, width), F32)

time: 245 us -> 231 us (0.943)
  waiting for transfers between devices: 56.9 us -> 48.3 us
  starting transfers between devices: 78.7 us -> 73.5 us
    ppermute x21 -> x18, waiting for transfers between devices: 25.9 us -> 13 us  [along(): lax.ppermute(values, axis, [(i, (i + step) % size) for i in range(size)])]
    all_to_all x11 -> x10, waiting for transfers between devices: 26.7 us -> 33.3 us  [exchange(): return lax.all_to_all(values, axes, split_axis=0, concat_axis=0, tiled=True)]
    all_to_all x11 -> x10, starting transfers between devices: 42.9 us -> 37.8 us  [exchange(): return lax.all_to_all(values, axes, split_axis=0, concat_axis=0, tiled=True)]
    ppermute x21 -> x18, starting transfers between devices: 28.6 us -> 24.3 us  [along(): lax.ppermute(values, axis, [(i, (i + step) % size) for i in range(size)])]
    ppermute x8 -> x12, starting transfers between devices: 7.18 us -> 11.4 us  [across(): return lax.ppermute(values, axis, [(i, i ^ mask) for i in range(size)])]
  transfers between devices with their start and end apart: 40 -> 40, of which waited for: 20 -> 14; matrix products, arithmetic and copies ran while one was open for 0% -> 0% of each run, Pallas kernels for 31% -> 36%
where the time goes in v1:
time: 231 us; the launch traced here: 230 us
  Pallas kernels  106 us (46%)
  starting transfers between devices  73.5 us (32%)
  waiting for transfers between devices  48.3 us (21%)
  between operations  2.51 us (1%)
    pallas_call x28, Pallas kernels, call(): pl.pallas_call(wrapped, name=name, out_shape=[pltpu.HBM(out.shape, out.dt...  106 us
    all_to_all x10, starting transfers between devices, exchange(): return lax.all_to_all(values, axes, split_axis=0, concat_axis=0, tiled=True)  37.8 us
    all_to_all x10, waiting for transfers between devices, exchange(): return lax.all_to_all(values, axes, split_axis=0, concat_axis=0, tiled=True)  33.3 us
    ppermute x18, starting transfers between devices, along(): lax.ppermute(values, axis, [(i, (i + step) % size) for i in range(size)])  24.3 us
    ppermute x18, waiting for transfers between devices, along(): lax.ppermute(values, axis, [(i, (i + step) % size) for i in range(size)])  13 us
    ppermute x12, starting transfers between devices, across(): return lax.ppermute(values, axis, [(i, i ^ mask) for i in range(size)])  11.4 us
  transfers between devices with their start and end apart: 40, of which 14 were waited for; matrix products, arithmetic and copies ran while one was open for 0% of the time, Pallas kernels for 36%

profile of v1, /device:TPU:0, one launch (start us, length us, event | category | flops | bytes accessed | tf_op | source)
XLA Modules:
  0.0 229.9 jit_solution(8433738910878069168)
XLA Ops:
  1.3 5.7 %qkv.1 = (bf16[8,128,384]{2,1,0:T(8,128)(2,1)}, bf16[128,1152]{1,0:T(8,128)(2,1)}) custom-call(s32[1]{0:T(128)S(6)} %copy.22.refs_0_.refs_1_, bf16[128,1024]{1,0:T(8,128)(2,1)} %bitcast.32, bf16[1024]{0:T(1024)(128)(2,1)} %refs_3_.9, bf16[5,1024,1024]{2,1,0:T(8,128)(2,1)} %refs_5_.9, bf16[7,8,16,1024]{3,2,1,0:T(8,128)(2,1)} %bitcast.23, ...), custom_call_target="tpu_custom_call" | custom-call | flops 4096 | bytes 4096 | tf_op jit(solution)/shard_map/qkv/pallas_call | solution.py:111
  7.0 5.2 %all-to-all-start = ((bf16[8,128,384]{2,1,0:T(8,128)(2,1)}), bf16[8,128,384]{2,1,0:T(8,128)(2,1)S(1)}, u32[]{:S(2)}, u32[]{:S(2)}) async-start(bf16[8,128,384]{2,1,0:T(8,128)(2,1)} %get-tuple-element.108), calls=%async_computation | async-start | bytes 1572864 | tf_op jit(solution)/shard_map/all_to_all | solution.py:1009
  20.3 3.3 %mixback.1 = (bf16[128,1024]{1,0:T(8,128)(2,1)}, bf16[128,16]{1,0:T(8,128)(2,1)}) custom-call(s32[1]{0:T(128)S(6)} %copy.22.refs_0_.refs_1_, bf16[128,1024]{1,0:T(8,128)(2,1)} %bitcast.35, bf16[2,1024,1024]{2,1,0:T(8,128)(2,1)} %refs_3_.8, bf16[7,8,16,1024]{3,2,1,0:T(8,128)(2,1)} %bitcast.24, bf16[7,8,16,1024]{3,2,1,0:T(8,128)(2,1)} %refs_7_.7), custom_call_target="tpu_custom_call" | custom-call | flops 4096 | bytes 4096 | tf_op jit(solution)/shard_map/mixback/pallas_call | solution.py:111
  24.7 5.0 %attend.1 = (bf16[8,192,128]{2,1,0:T(8,128)(2,1)}, f32[8,1024]{1,0:T(8,128)}, s32[4,8,128]{2,1,0:T(8,128)}, bf16[1024,384]{1,0:T(8,128)(2,1)}) custom-call(s32[1]{0:T(128)S(6)} %copy.21.refs_0_, bf16[1024,384]{1,0:T(8,128)(2,1)S(1)} %bitcast.19, s32[72,128]{1,0:T(8,128)S(1)} %get-tuple-element.115.refs_2_, s32[72,128]{1,0:T(8,128)S(1)} %collective-permute-done.refs_3_, ...), custom_call_target="tpu_custom_call" | custom-call | flops 4096 | bytes 4096 | tf_op jit(solution)/shard_map/attend/pallas_call | solution.py:111
  29.8 3.8 %all-to-all-start.1 = ((bf16[8,192,128]{2,1,0:T(8,128)(2,1)}), bf16[8,192,128]{2,1,0:T(8,128)(2,1)S(1)}, u32[]{:S(2)}, u32[]{:S(2)}) async-start(bf16[8,192,128]{2,1,0:T(8,128)(2,1)} %get-tuple-element.119), calls=%async_computation.1 | async-start | bytes 786432 | tf_op jit(solution)/shard_map/all_to_all | solution.py:1009
  37.2 5.3 %all-to-all-done.1.refs_1_ = bf16[8,192,128]{2,1,0:T(8,128)(2,1)S(1)} async-done(((bf16[8,192,128]{2,1,0:T(8,128)(2,1)}), bf16[8,192,128]{2,1,0:T(8,128)(2,1)S(1)}, u32[]{:S(2)}, u32[]{:S(2)}) %all-to-all-start.1) | async-done | bytes 393248 | tf_op jit(solution)/shard_map/all_to_all | solution.py:1009
  42.5 4.8 %middle.1 = (bf16[128,512]{1,0:T(8,128)(2,1)S(1)}, bf16[128,512]{1,0:T(8,128)(2,1)S(1)}, bf16[128,1024]{1,0:T(8,128)(2,1)S(1)}, bf16[8,64,128]{2,1,0:T(8,128)(2,...) custom-call(s32[1]{0:T(128)S(6)} %copy.22.refs_0_.refs_1_, ...), custom_call_target="tpu_custom_call" | custom-call | flops 4096 | bytes 4096 | tf_op jit(solution)/shard_map/middle/pallas_call | solution.py:111
  47.2 3.2 %collective-permute-start.5 = (bf16[128,512]{1,0:T(8,128)(2,1)S(1)}, bf16[128,512]{1,0:T(8,128)(2,1)S(1)}, u32[]{:S(2)}, u32[]{:S(2)}) collective-permute-start(bf16[128,512]{1,0:T(8,128)(2,1)S(1)} %get-tuple-element.137.refs_1_), channel_id=1, source_target_pairs={{0,24},{8,0},{16,8},{24,16},{1,25},{9,1},{17,9},{25,17},{2,26},{10... | collective-permute-start | bytes 393224 | tf_op jit(solution)/shard_map/ppermute | solution.py:992
  51.5 4.9 %scores.1 = (bf16[256,128]{1,0:T(8,128)(2,1)}, bf16[128,16]{1,0:T(8,128)(2,1)}, f32[128,128]{1,0:T(8,128)}) custom-call(s32[1]{0:T(128)S(6)} %copy.22.refs_0_.refs_1_, bf16[128,1024]{1,0:T(8,128)(2,1)S(1)} %get-tuple-element.127.refs_1_, s32[128,128]{1,0:T(8,128)} %get-tuple-element.128.refs_2_, s32[8,128]{1,0:T(8,128)} %get-tuple-element.129.refs_3_, ...), custom_call_target="tpu_custom_call" | custom-call | flops 4096 | bytes 4096 | tf_op jit(solution)/shard_map/scores/pallas_call | solution.py:111
  56.4 3.6 %all-to-all-start.2 = ((bf16[32,8,128]{2,1,0:T(8,128)(2,1)}), bf16[32,8,128]{2,1,0:T(8,128)(2,1)S(1)}, u32[]{:S(2)}, u32[]{:S(2)}) async-start(bf16[32,8,128]{2,1,0:T(8,128)(2,1)} %bitcast.6), calls=%async_computation.2 | async-start | bytes 131072 | tf_op jit(solution)/shard_map/all_to_all | solution.py:1009
  63.7 3.7 %all-to-all-done.2 = bf16[32,8,128]{2,1,0:T(8,128)(2,1)S(1)} async-done(((bf16[32,8,128]{2,1,0:T(8,128)(2,1)}), bf16[32,8,128]{2,1,0:T(8,128)(2,1)S(1)}, u32[]{:S(2)}, u32[]{:S(2)}) %all-to-all-start.2) | async-done | bytes 65568 | tf_op jit(solution)/shard_map/all_to_all | solution.py:1009
  67.4 3.7 %all-to-all-start.3 = ((bf16[8,4,32,512]{3,2,1,0:T(8,128)(2,1)}), bf16[8,4,32,512]{3,2,1,0:T(8,128)(2,1)S(1)}, u32[]{:S(2)}, u32[]{:S(2)}) async-start(bf16[8,4,32,512]{3,2,1,0:T(8,128)(2,1)} %scatterleft.1), calls=%async_computation.3 | async-start | bytes 2097152 | tf_op jit(solution)/shard_map/all_to_all | solution.py:1009
  71.1 6.6 %prepare.1 = (s32[256,128]{1,0:T(8,128)}, s16[1024,2048]{1,0:T(8,128)(2,1)}) custom-call(bf16[8,64,128]{2,1,0:T(8,128)(2,1)} %get-tuple-element.154.refs_0_), custom_call_target="tpu_custom_call" | custom-call | flops 4096 | bytes 4096 | tf_op jit(solution)/shard_map/prepare/pallas_call | solution.py:111
  77.8 11.4 %recall.1 = bf16[8,4,32,1024]{3,2,1,0:T(8,128)(2,1)} custom-call(bf16[256,128]{1,0:T(8,128)(2,1)S(1)} %bitcast.22, s16[1024,2048]{1,0:T(8,128)(2,1)} %get-tuple-element.155.refs_1_, bf16[2048,1024]{1,0:T(8,128)(2,1)} %refs_3_.7), custom_call_target="tpu_custom_call" | custom-call | flops 4096 | bytes 4096 | tf_op jit(solution)/shard_map/recall/pallas_call | solution.py:111
  89.2 4.0 %all-to-all-start.4 = ((bf16[8,4,32,1024]{3,2,1,0:T(8,128)(2,1)}), bf16[8,4,32,1024]{3,2,1,0:T(8,128)(2,1)S(1)}, u32[]{:S(2)}, u32[]{:S(2)}) async-start(bf16[8,4,32,1024]{3,2,1,0:T(8,128)(2,1)} %recall.1), calls=%async_computation.4 | async-start | bytes 4194304 | tf_op jit(solution)/shard_map/all_to_all | solution.py:1009
  96.4 6.1 %recallleft.1.refs_1_ = f32[256,128]{1,0:T(8,128)} custom-call(s32[256,128]{1,0:T(8,128)} %get-tuple-element.158.refs_0_, bf16[1024,512]{1,0:T(8,128)(2,1)S(1)} %bitcast.17, bf16[2048,1024]{1,0:T(8,128)(2,1)} %refs_3_.7), custom_call_target="tpu_custom_call" | custom-call | flops 4096 | bytes 4096 | tf_op jit(solution)/shard_map/recallleft/pallas_call | solution.py:111
  102.5 5.0 %collective-permute-done.7.refs_3_ = bf16[128,512]{1,0:T(8,128)(2,1)S(1)} collective-permute-done((bf16[128,512]{1,0:T(8,128)(2,1)S(1)}, bf16[128,512]{1,0:T(8,128)(2,1)S(1)}, u32[]{:S(2)}, u32[]{:S(2)}) %collective-permute-start.7) | collective-permute-done | bytes 131104 | tf_op jit(solution)/shard_map/ppermute | solution.py:992
  109.7 10.1 %all-to-all-done.4.refs_1_ = bf16[8,4,32,1024]{3,2,1,0:T(8,128)(2,1)S(1)} async-done(((bf16[8,4,32,1024]{3,2,1,0:T(8,128)(2,1)}), bf16[8,4,32,1024]{3,2,1,0:T(8,128)(2,1)S(1)}, u32[]{:S(2)}, u32[]{:S(2)}) %all-to-all-start.4) | async-done | bytes 2097184 | tf_op jit(solution)/shard_map/all_to_all | solution.py:1009
  119.8 3.6 %all-to-all-start.5 = ((bf16[8,4,32,512]{3,2,1,0:T(8,128)(2,1)}), bf16[8,4,32,512]{3,2,1,0:T(8,128)(2,1)S(1)}, u32[]{:S(2)}, u32[]{:S(2)}) async-start(bf16[8,4,32,512]{3,2,1,0:T(8,128)(2,1)} %scatterright.1), calls=%async_computation.5 | async-start | bytes 2097152 | tf_op jit(solution)/shard_map/all_to_all | solution.py:1009
  128.1 10.6 %all-to-all-done.5 = bf16[8,4,32,512]{3,2,1,0:T(8,128)(2,1)S(1)} async-done(((bf16[8,4,32,512]{3,2,1,0:T(8,128)(2,1)}), bf16[8,4,32,512]{3,2,1,0:T(8,128)(2,1)S(1)}, u32[]{:S(2)}, u32[]{:S(2)}) %all-to-all-start.5) | async-done | bytes 1048608 | tf_op jit(solution)/shard_map/all_to_all | solution.py:1009
  138.7 6.2 %recallright.1 = bf16[256,128]{1,0:T(8,128)(2,1)} custom-call(s32[256,128]{1,0:T(8,128)} %get-tuple-element.158.refs_0_, f32[256,128]{1,0:T(8,128)} %recallleft.1.refs_1_, bf16[1024,512]{1,0:T(8,128)(2,1)S(1)} %bitcast.18, bf16[2048,1024]{1,0:T(8,128)(2,1)} %refs_3_.7), custom_call_target="tpu_custom_call" | custom-call | flops 4096 | bytes 4096 | tf_op jit(solution)/shard_map/recallright/pallas_call | solution.py:111
  147.5 3.8 %collective-permute-done.14.refs_5_ = bf16[128,1024]{1,0:T(8,128)(2,1)S(1)} collective-permute-done((bf16[128,1024]{1,0:T(8,128)(2,1)}, bf16[128,1024]{1,0:T(8,128)(2,1)S(1)}, u32[]{:S(2)}, u32[]{:S(2)}) %collective-permute-start.14) | collective-permute-done | bytes 262176 | tf_op jit(solution)/shard_map/ppermute | solution.py:992
  151.3 3.6 %memory.1 = (bf16[128,1024]{1,0:T(8,128)(2,1)}, bf16[128,16]{1,0:T(8,128)(2,1)}, bf16[128,1024]{1,0:T(8,128)(2,1)}, f32[128,1024]{1,0:T(8,128)}) custom-call(s32[1]{0:T(128)S(6)} %copy.22.refs_0_.refs_1_, f32[128,1024]{1,0:T(8,128)} %get-tuple-element.121.refs_1_, bf16[128,1024]{1,0:T(8,128)(2,1)} %get-tuple-element.120.refs_4_.refs_2_, ...), custom_call_target="tpu_custom_call" | custom-call | flops 4096 | bytes 4096 | tf_op jit(solution)/shard_map/memory/pallas_call | solution.py:111
  154.9 9.0 %query.1 = (bf16[8,128,128]{2,1,0:T(8,128)(2,1)}, bf16[128,1024]{1,0:T(8,128)(2,1)}, bf16[2,128,16]{2,1,0:T(8,128)(2,1)}, f32[128,1024]{1,0:T(8,128)}) custom-call(s32[1]{0:T(128)S(6)} %copy.21.refs_0_, s32[1]{0:T(128)S(6)} %copy.22.refs_0_.refs_1_, bf16[256,128]{1,0:T(8,128)(2,1)S(1)} %bitcast.21, s32[128,128]{1,0:T(8,128)} %get-tuple-element.168.refs_3_, ...), custom_call_target="tpu_custom_call" | custom-call | flops 4096 | bytes 4096 | tf_op jit(solution)/shard_map/query/pallas_call | solution.py:111
  163.9 3.9 %all-to-all-start.7 = ((bf16[8,128,128]{2,1,0:T(8,128)(2,1)}), bf16[8,128,128]{2,1,0:T(8,128)(2,1)S(1)}, u32[]{:S(2)}, u32[]{:S(2)}) async-start(bf16[8,128,128]{2,1,0:T(8,128)(2,1)} %get-tuple-element.172), calls=%async_computation.7 | async-start | bytes 524288 | tf_op jit(solution)/shard_map/all_to_all | solution.py:1009
  167.8 3.2 %output.1 = (bf16[128,1024]{1,0:T(8,128)(2,1)}, bf16[128,16]{1,0:T(8,128)(2,1)}) custom-call(s32[1]{0:T(128)S(6)} %copy.22.refs_0_.refs_1_, bf16[128,1024]{1,0:T(8,128)(2,1)} %get-tuple-element.173.refs_1_.refs_2_, f32[128,1024]{1,0:T(8,128)} %get-tuple-element.171.refs_7_.refs_2_, bf16[2,1024,1024]{2,1,0:T(8,128)(2,1)} %refs_3_.8, ...), custom_call_target="tpu_custom_call" | custom-call | flops 4096 | bytes 4096 | tf_op jit(solution)/shard_map/output/pallas_call | solution.py:111
  174.7 3.4 %all-to-all-start.8 = ((bf16[8,128,128]{2,1,0:T(8,128)(2,1)}), bf16[8,128,128]{2,1,0:T(8,128)(2,1)S(1)}, u32[]{:S(2)}, u32[]{:S(2)}) async-start(bf16[8,128,128]{2,1,0:T(8,128)(2,1)} %factors.1), calls=%async_computation.8 | async-start | bytes 524288 | tf_op jit(solution)/shard_map/all_to_all | solution.py:1009
  178.2 10.1 %attendback.1 = (bf16[8,144,384]{2,1,0:T(8,128)(2,1)}, bf16[48,128]{1,0:T(8,128)(2,1)}) custom-call(s32[1]{0:T(128)S(6)} %copy.21.refs_0_, s32[1]{0:T(128)S(6)} %copy.22.refs_0_.refs_1_, bf16[1024,384]{1,0:T(8,128)(2,1)} %get-tuple-element.175.refs_2_, bf16[1024,128]{1,0:T(8,128)(2,1)S(1)} %bitcast.20, f32[8,1024]{1,0:T(8,128)} %get-tuple-element.188.refs_4_, ...), custom_call_target="tpu_custom_call" | custom-call | flops 4096 | bytes 4096 | tf_op jit(solution)/shard_map/attendback/pallas_call | solution.py:111
  188.3 4.1 %all-to-all-start.9 = ((bf16[8,144,384]{2,1,0:T(8,128)(2,1)}), bf16[8,144,384]{2,1,0:T(8,128)(2,1)S(1)}, u32[]{:S(2)}, u32[]{:S(2)}) async-start(bf16[8,144,384]{2,1,0:T(8,128)(2,1)} %get-tuple-element.193), calls=%async_computation.9 | async-start | bytes 1769472 | tf_op jit(solution)/shard_map/all_to_all | solution.py:1009
  212.0 5.2 %entry.1 = bf16[128,1024]{1,0:T(8,128)(2,1)} custom-call(s32[1]{0:T(128)S(6)} %copy.22.refs_0_.refs_1_, bf16[8,144,384]{2,1,0:T(8,128)(2,1)S(1)} %all-to-all-done.9.refs_0_.refs_1_, bf16[128,1024]{1,0:T(8,128)(2,1)} %bitcast.34, bf16[1024]{0:T(1024)(128)(2,1)} %refs_3_.9, f32[128,1024]{1,0:T(8,128)} %get-tuple-element.178.refs_3_.refs_4_, ...), custom_call_target="tpu_custom_call" | custom-call | flops 4096 | bytes 4096 | tf_op jit(solution)/shard_map/entry/pallas_call | solution.py:111
  220.9 3.7 %spread.1 = (f32[7,8,16,1024]{3,2,1,0:T(8,128)}, f32[7,8,16,1024]{3,2,1,0:T(8,128)}) custom-call(s32[256,128]{1,0:T(8,128)} %get-tuple-element.158.refs_0_, bf16[4,4,128,128]{3,2,1,0:T(8,128)(2,1)S(1)} %pairsearly.1.refs_1_, bf16[4,4,128,128]{3,2,1,0:T(8,128)(2,1)S(1)} %collective-permute-done.28.refs_2_), custom_call_target="tpu_custom_call" | custom-call | flops 4096 | bytes 4096 | tf_op jit(solution)/shard_map/spread/pallas_call | solution.py:111
  226.7 3.0 %lastspread.1 = (f32[7,8,16,1024]{3,2,1,0:T(8,128)}, f32[7,8,16,1024]{3,2,1,0:T(8,128)}) custom-call(s32[256,128]{1,0:T(8,128)} %get-tuple-element.158.refs_0_, f32[7,8,16,1024]{3,2,1,0:T(8,128)} %get-tuple-element.204.refs_1_, f32[7,8,16,1024]{3,2,1,0:T(8,128)} %get-tuple-element.205.refs_2_, ...), custom_call_target="tpu_custom_call", output_to_operand_aliasing={{0}: (1, {}), {1}: (2, {})} | custom-call | flops 4096 | bytes 4096 | tf_op jit(solution)/shard_map/lastspread/pallas_call | solution.py:111
  (78 shorter events, 58.5 us)
Async XLA Ops:
  7.0 17.8 %all-to-all-start = ((bf16[8,128,384]{2,1,0:T(8,128)(2,1)}), bf16[8,128,384]{2,1,0:T(8,128)(2,1)S(1)}, u32[]{:S(2)}, u32[]{:S(2)}) async-start(bf16[8,128,384]{2,1,0:T(8,128)(2,1)} %get-tuple-element.108), calls=%async_computation | async-start | bytes 1572864 | tf_op jit(solution)/shard_map/all_to_all | solution.py:1009
  14.8 9.6 %collective-permute-start = (s32[72,128]{1,0:T(8,128)S(1)}, s32[72,128]{1,0:T(8,128)S(1)}, u32[]{:S(2)}, u32[]{:S(2)}) collective-permute-start(s32[72,128]{1,0:T(8,128)S(1)} %get-tuple-element.110), channel_id=1, source_target_pairs={{0,8},{8,16},{16,24},{24,0},{1,9},{9,17},{17,25},{25,1},{2,10},{10... | collective-permute-start | bytes 110600 | tf_op jit(solution)/shard_map/ppermute | solution.py:992
  16.4 7.9 %collective-permute-start.1 = (s32[72,128]{1,0:T(8,128)S(1)}, s32[72,128]{1,0:T(8,128)S(1)}, u32[]{:S(2)}, u32[]{:S(2)}) collective-permute-start(s32[72,128]{1,0:T(8,128)S(1)} %get-tuple-element.111), channel_id=1, source_target_pairs={{0,16},{8,24},{16,0},{24,8},{1,17},{9,25},{17,1},{25,9},{2,18},{10... | collective-permute-start | bytes 110600 | tf_op jit(solution)/shard_map/ppermute | solution.py:992
  29.8 12.7 %all-to-all-start.1 = ((bf16[8,192,128]{2,1,0:T(8,128)(2,1)}), bf16[8,192,128]{2,1,0:T(8,128)(2,1)S(1)}, u32[]{:S(2)}, u32[]{:S(2)}) async-start(bf16[8,192,128]{2,1,0:T(8,128)(2,1)} %get-tuple-element.119), calls=%async_computation.1 | async-start | bytes 786432 | tf_op jit(solution)/shard_map/all_to_all | solution.py:1009
  33.6 16.9 %collective-permute-start.11 = (bf16[128,1152]{1,0:T(8,128)(2,1)S(1)}, bf16[128,1152]{1,0:T(8,128)(2,1)S(1)}, u32[]{:S(2)}, u32[]{:S(2)}) collective-permute-start(bf16[128,1152]{1,0:T(8,128)(2,1)S(1)} %copy-done), channel_id=1, source_target_pairs={{0,6},{1,7},{2,4},{3,5},{4,2},{5,3},{6,0},{7,1},{8,14},{9,15},{10,... | collective-permute-start | bytes 884744 | tf_op jit(solution)/shard_map/ppermute | solution.py:996
  36.5 19.9 %collective-permute-start.10 = (bf16[128,1152]{1,0:T(8,128)(2,1)S(1)}, bf16[128,1152]{1,0:T(8,128)(2,1)S(1)}, u32[]{:S(2)}, u32[]{:S(2)}) collective-permute-start(bf16[128,1152]{1,0:T(8,128)(2,1)S(1)} %copy-done), channel_id=1, source_target_pairs={{0,4},{1,5},{2,6},{3,7},{4,0},{5,1},{6,2},{7,3},{8,12},{9,13},{10,... | collective-permute-start | bytes 884744 | tf_op jit(solution)/shard_map/ppermute | solution.py:996
  37.1 19.3 %collective-permute-start.9 = (bf16[128,1152]{1,0:T(8,128)(2,1)S(1)}, bf16[128,1152]{1,0:T(8,128)(2,1)S(1)}, u32[]{:S(2)}, u32[]{:S(2)}) collective-permute-start(bf16[128,1152]{1,0:T(8,128)(2,1)S(1)} %copy-done), channel_id=1, source_target_pairs={{0,2},{1,3},{2,0},{3,1},{4,6},{5,7},{6,4},{7,5},{8,10},{9,11},{10,... | collective-permute-start | bytes 884744 | tf_op jit(solution)/shard_map/ppermute | solution.py:996
  47.2 12.7 %collective-permute-start.5 = (bf16[128,512]{1,0:T(8,128)(2,1)S(1)}, bf16[128,512]{1,0:T(8,128)(2,1)S(1)}, u32[]{:S(2)}, u32[]{:S(2)}) collective-permute-start(bf16[128,512]{1,0:T(8,128)(2,1)S(1)} %get-tuple-element.137.refs_1_), channel_id=1, source_target_pairs={{0,24},{8,0},{16,8},{24,16},{1,25},{9,1},{17,9},{25,17},{2,26},{10... | collective-permute-start | bytes 393224 | tf_op jit(solution)/shard_map/ppermute | solution.py:992
  50.5 9.9 %collective-permute-start.4 = (bf16[128,512]{1,0:T(8,128)(2,1)S(1)}, bf16[128,512]{1,0:T(8,128)(2,1)S(1)}, u32[]{:S(2)}, u32[]{:S(2)}) collective-permute-start(bf16[128,512]{1,0:T(8,128)(2,1)S(1)} %get-tuple-element.137.refs_1_), channel_id=1, source_target_pairs={{0,16},{8,24},{16,0},{24,8},{1,17},{9,25},{17,1},{25,9},{2,18},{10... | collective-permute-start | bytes 393224 | tf_op jit(solution)/shard_map/ppermute | solution.py:992
  50.5 9.9 %collective-permute-start.3 = (bf16[128,512]{1,0:T(8,128)(2,1)S(1)}, bf16[128,512]{1,0:T(8,128)(2,1)S(1)}, u32[]{:S(2)}, u32[]{:S(2)}) collective-permute-start(bf16[128,512]{1,0:T(8,128)(2,1)S(1)} %get-tuple-element.137.refs_1_), channel_id=1, source_target_pairs={{0,8},{8,16},{16,24},{24,0},{1,9},{9,17},{17,25},{25,1},{2,10},{10... | collective-permute-start | bytes 393224 | tf_op jit(solution)/shard_map/ppermute | solution.py:992
  56.4 11.0 %all-to-all-start.2 = ((bf16[32,8,128]{2,1,0:T(8,128)(2,1)}), bf16[32,8,128]{2,1,0:T(8,128)(2,1)S(1)}, u32[]{:S(2)}, u32[]{:S(2)}) async-start(bf16[32,8,128]{2,1,0:T(8,128)(2,1)} %bitcast.6), calls=%async_computation.2 | async-start | bytes 131072 | tf_op jit(solution)/shard_map/all_to_all | solution.py:1009
  67.4 21.8 %all-to-all-start.3 = ((bf16[8,4,32,512]{3,2,1,0:T(8,128)(2,1)}), bf16[8,4,32,512]{3,2,1,0:T(8,128)(2,1)S(1)}, u32[]{:S(2)}, u32[]{:S(2)}) async-start(bf16[8,4,32,512]{3,2,1,0:T(8,128)(2,1)} %scatterleft.1), calls=%async_computation.3 | async-start | bytes 2097152 | tf_op jit(solution)/shard_map/all_to_all | solution.py:1009
  89.2 30.6 %all-to-all-start.4 = ((bf16[8,4,32,1024]{3,2,1,0:T(8,128)(2,1)}), bf16[8,4,32,1024]{3,2,1,0:T(8,128)(2,1)S(1)}, u32[]{:S(2)}, u32[]{:S(2)}) async-start(bf16[8,4,32,1024]{3,2,1,0:T(8,128)(2,1)} %recall.1), calls=%async_computation.4 | async-start | bytes 4194304 | tf_op jit(solution)/shard_map/all_to_all | solution.py:1009
  93.1 14.4 %collective-permute-start.12 = (bf16[4,128,1152]{2,1,0:T(8,128)(2,1)}, bf16[4,128,1152]{2,1,0:T(8,128)(2,1)}, u32[]{:S(2)}, u32[]{:S(2)}) collective-permute-start(bf16[4,128,1152]{2,1,0:T(8,128)(2,1)} %pairsnorm.1.refs_5_), channel_id=1, source_target_pairs={{0,1},{1,0},{2,3},{3,2},{4,5},{5,4},{6,7},{7,6},{8,9},{9,8},{10,11... | collective-permute-start | bytes 3538952 | tf_op jit(solution)/shard_map/ppermute | solution.py:996
  93.7 8.9 %collective-permute-start.8 = (bf16[128,512]{1,0:T(8,128)(2,1)S(1)}, bf16[128,512]{1,0:T(8,128)(2,1)S(1)}, u32[]{:S(2)}, u32[]{:S(2)}) collective-permute-start(bf16[128,512]{1,0:T(8,128)(2,1)S(1)} %get-tuple-element.149.refs_1_), channel_id=1, source_target_pairs={{0,24},{8,0},{16,8},{24,16},{1,25},{9,1},{17,9},{25,17},{2,26},{10... | collective-permute-start | bytes 393224 | tf_op jit(solution)/shard_map/ppermute | solution.py:992
  94.6 13.0 %collective-permute-start.7 = (bf16[128,512]{1,0:T(8,128)(2,1)S(1)}, bf16[128,512]{1,0:T(8,128)(2,1)S(1)}, u32[]{:S(2)}, u32[]{:S(2)}) collective-permute-start(bf16[128,512]{1,0:T(8,128)(2,1)S(1)} %get-tuple-element.149.refs_1_), channel_id=1, source_target_pairs={{0,16},{8,24},{16,0},{24,8},{1,17},{9,25},{17,1},{25,9},{2,18},{10... | collective-permute-start | bytes 393224 | tf_op jit(solution)/shard_map/ppermute | solution.py:992
  95.7 11.8 %collective-permute-start.6 = (bf16[128,512]{1,0:T(8,128)(2,1)S(1)}, bf16[128,512]{1,0:T(8,128)(2,1)S(1)}, u32[]{:S(2)}, u32[]{:S(2)}) collective-permute-start(bf16[128,512]{1,0:T(8,128)(2,1)S(1)} %get-tuple-element.149.refs_1_), channel_id=1, source_target_pairs={{0,8},{8,16},{16,24},{24,0},{1,9},{9,17},{17,25},{25,1},{2,10},{10... | collective-permute-start | bytes 393224 | tf_op jit(solution)/shard_map/ppermute | solution.py:992
  119.8 18.9 %all-to-all-start.5 = ((bf16[8,4,32,512]{3,2,1,0:T(8,128)(2,1)}), bf16[8,4,32,512]{3,2,1,0:T(8,128)(2,1)S(1)}, u32[]{:S(2)}, u32[]{:S(2)}) async-start(bf16[8,4,32,512]{3,2,1,0:T(8,128)(2,1)} %scatterright.1), calls=%async_computation.5 | async-start | bytes 2097152 | tf_op jit(solution)/shard_map/all_to_all | solution.py:1009
  125.4 22.1 %collective-permute-start.13 = (bf16[128,1024]{1,0:T(8,128)(2,1)}, bf16[128,1024]{1,0:T(8,128)(2,1)S(1)}, u32[]{:S(2)}, u32[]{:S(2)}) collective-permute-start(bf16[128,1024]{1,0:T(8,128)(2,1)} %get-tuple-element.162), channel_id=1, source_target_pairs={{0,24},{8,0},{16,8},{24,16},{1,25},{9,1},{17,9},{25,17},{2,26},{10... | collective-permute-start | bytes 786440 | tf_op jit(solution)/shard_map/ppermute | solution.py:992
  126.3 24.9 %collective-permute-start.14 = (bf16[128,1024]{1,0:T(8,128)(2,1)}, bf16[128,1024]{1,0:T(8,128)(2,1)S(1)}, u32[]{:S(2)}, u32[]{:S(2)}) collective-permute-start(bf16[128,1024]{1,0:T(8,128)(2,1)} %get-tuple-element.163), channel_id=1, source_target_pairs={{0,16},{8,24},{16,0},{24,8},{1,17},{9,25},{17,1},{25,9},{2,18},{10... | collective-permute-start | bytes 786440 | tf_op jit(solution)/shard_map/ppermute | solution.py:992
  127.5 23.8 %collective-permute-start.15 = (bf16[128,1024]{1,0:T(8,128)(2,1)}, bf16[128,1024]{1,0:T(8,128)(2,1)S(1)}, u32[]{:S(2)}, u32[]{:S(2)}) collective-permute-start(bf16[128,1024]{1,0:T(8,128)(2,1)} %get-tuple-element.164), channel_id=1, source_target_pairs={{0,8},{8,16},{16,24},{24,0},{1,9},{9,17},{17,25},{25,1},{2,10},{10... | collective-permute-start | bytes 786440 | tf_op jit(solution)/shard_map/ppermute | solution.py:992
  144.9 10.0 %all-to-all-start.6 = ((bf16[32,8,128]{2,1,0:T(8,128)(2,1)}), bf16[32,8,128]{2,1,0:T(8,128)(2,1)S(1)}, u32[]{:S(2)}, u32[]{:S(2)}) async-start(bf16[32,8,128]{2,1,0:T(8,128)(2,1)} %bitcast.10), calls=%async_computation.6 | async-start | bytes 131072 | tf_op jit(solution)/shard_map/all_to_all | solution.py:1009
  163.9 10.8 %all-to-all-start.7 = ((bf16[8,128,128]{2,1,0:T(8,128)(2,1)}), bf16[8,128,128]{2,1,0:T(8,128)(2,1)S(1)}, u32[]{:S(2)}, u32[]{:S(2)}) async-start(bf16[8,128,128]{2,1,0:T(8,128)(2,1)} %get-tuple-element.172), calls=%async_computation.7 | async-start | bytes 524288 | tf_op jit(solution)/shard_map/all_to_all | solution.py:1009
  174.7 13.5 %all-to-all-start.8 = ((bf16[8,128,128]{2,1,0:T(8,128)(2,1)}), bf16[8,128,128]{2,1,0:T(8,128)(2,1)S(1)}, u32[]{:S(2)}, u32[]{:S(2)}) async-start(bf16[8,128,128]{2,1,0:T(8,128)(2,1)} %factors.1), calls=%async_computation.8 | async-start | bytes 524288 | tf_op jit(solution)/shard_map/all_to_all | solution.py:1009
  188.3 18.3 %all-to-all-start.9 = ((bf16[8,144,384]{2,1,0:T(8,128)(2,1)}), bf16[8,144,384]{2,1,0:T(8,128)(2,1)S(1)}, u32[]{:S(2)}, u32[]{:S(2)}) async-start(bf16[8,144,384]{2,1,0:T(8,128)(2,1)} %get-tuple-element.193), calls=%async_computation.9 | async-start | bytes 1769472 | tf_op jit(solution)/shard_map/all_to_all | solution.py:1009
  200.8 9.2 %collective-permute-start.24 = (bf16[4,128,128]{2,1,0:T(8,128)(2,1)S(1)}, bf16[4,128,128]{2,1,0:T(8,128)(2,1)S(1)}, u32[]{:S(2)}, u32[]{:S(2)}) collective-permute-start(bf16[4,128,128]{2,1,0:T(8,128)(2,1)S(1)} %stackearly.1.refs_0_), channel_id=1, source_target_pairs={{0,6},{1,7},{2,4},{3,5},{4,2},{5,3},{6,0},{7,1},{8,14},{9,15},{10,... | collective-permute-start | bytes 393224 | tf_op jit(solution)/shard_map/ppermute | solution.py:996
  203.8 8.2 %collective-permute-start.23 = (bf16[4,128,128]{2,1,0:T(8,128)(2,1)S(1)}, bf16[4,128,128]{2,1,0:T(8,128)(2,1)S(1)}, u32[]{:S(2)}, u32[]{:S(2)}) collective-permute-start(bf16[4,128,128]{2,1,0:T(8,128)(2,1)S(1)} %stackearly.1.refs_0_), channel_id=1, source_target_pairs={{0,4},{1,5},{2,6},{3,7},{4,0},{5,1},{6,2},{7,3},{8,12},{9,13},{10,... | collective-permute-start | bytes 393224 | tf_op jit(solution)/shard_map/ppermute | solution.py:996
  204.3 7.6 %collective-permute-start.22 = (bf16[4,128,128]{2,1,0:T(8,128)(2,1)S(1)}, bf16[4,128,128]{2,1,0:T(8,128)(2,1)S(1)}, u32[]{:S(2)}, u32[]{:S(2)}) collective-permute-start(bf16[4,128,128]{2,1,0:T(8,128)(2,1)S(1)} %stackearly.1.refs_0_), channel_id=1, source_target_pairs={{0,2},{1,3},{2,0},{3,1},{4,6},{5,7},{6,4},{7,5},{8,10},{9,11},{10,... | collective-permute-start | bytes 393224 | tf_op jit(solution)/shard_map/ppermute | solution.py:996
  207.4 9.8 %collective-permute-start.18 = (bf16[96,128]{1,0:T(8,128)(2,1)S(1)}, bf16[96,128]{1,0:T(8,128)(2,1)S(1)}, u32[]{:S(2)}, u32[]{:S(2)}) collective-permute-start(bf16[96,128]{1,0:T(8,128)(2,1)S(1)} %late.1.refs_0_), channel_id=1, source_target_pairs={{0,24},{8,0},{16,8},{24,16},{1,25},{9,1},{17,9},{25,17},{2,26},{10... | collective-permute-start | bytes 73736 | tf_op jit(solution)/shard_map/ppermute | solution.py:992
  209.1 8.1 %collective-permute-start.17 = (bf16[96,128]{1,0:T(8,128)(2,1)S(1)}, bf16[96,128]{1,0:T(8,128)(2,1)S(1)}, u32[]{:S(2)}, u32[]{:S(2)}) collective-permute-start(bf16[96,128]{1,0:T(8,128)(2,1)S(1)} %late.1.refs_0_), channel_id=1, source_target_pairs={{0,16},{8,24},{16,0},{24,8},{1,17},{9,25},{17,1},{25,9},{2,18},{10... | collective-permute-start | bytes 73736 | tf_op jit(solution)/shard_map/ppermute | solution.py:992
  210.0 7.3 %collective-permute-start.16 = (bf16[96,128]{1,0:T(8,128)(2,1)S(1)}, bf16[96,128]{1,0:T(8,128)(2,1)S(1)}, u32[]{:S(2)}, u32[]{:S(2)}) collective-permute-start(bf16[96,128]{1,0:T(8,128)(2,1)S(1)} %late.1.refs_0_), channel_id=1, source_target_pairs={{0,8},{8,16},{16,24},{24,0},{1,9},{9,17},{17,25},{25,1},{2,10},{10... | collective-permute-start | bytes 73736 | tf_op jit(solution)/shard_map/ppermute | solution.py:992
  217.3 7.3 %collective-permute-start.27 = (bf16[4,96,128]{2,1,0:T(8,128)(2,1)S(1)}, bf16[4,96,128]{2,1,0:T(8,128)(2,1)S(1)}, u32[]{:S(2)}, u32[]{:S(2)}) collective-permute-start(bf16[4,96,128]{2,1,0:T(8,128)(2,1)S(1)} %stacklate.1.refs_0_), channel_id=1, source_target_pairs={{0,6},{1,7},{2,4},{3,5},{4,2},{5,3},{6,0},{7,1},{8,14},{9,15},{10,... | collective-permute-start | bytes 294920 | tf_op jit(solution)/shard_map/ppermute | solution.py:996
  (9 other events, 52.0 us)

commit v2 on v1

--- a/solution.py
+++ b/solution.py
@@ -16,7 +16,8 @@
 RANK = 16
 LANES = 128
 ADAPTER_STEP = 4096
-RECALL_ROWS = 128
+QUERY_UNROLL = 8
+RECALL_ROWS = 256
 EPS = 1e-06
 NEG = -1e30
 F32 = jnp.float32
@@ -42,6 +43,13 @@
 
 def iota(shape, axis):
     return lax.broadcasted_iota(I32, shape, axis)
+
+
+def short_pick(table, index):
+    numbers = lax.GatherDimensionNumbers(
+        offset_dims=(), collapsed_slice_dims=(1,), start_index_map=(1,), operand_batching_dims=(0,), start_indices_batching_dims=(0,)
+    )
+    return lax.gather(table, index[:, :, None], numbers, (1, 1), mode=lax.GatherScatterMode.PROMISE_IN_BOUNDS)
 
 
 def lane_pick(table, index):
@@ -289,7 +297,7 @@
 
         for c in range(chunks):
             index = 31 - lax.clz(mask & highs[c : c + 1, :])
-            stage[slot, :, c * LANES : (c + 1) * LANES] = jnp.transpose(index).astype(jnp.int16)
+            stage[slot, :, c * LANES : (c + 1) * LANES] = jnp.transpose(index.astype(jnp.int16))
         put(step, slot).start()
         return carry
 
@@ -328,11 +336,12 @@
     def pick(b, side):
         g, k = b // per_group, lax.rem(b, per_group)
         for start in range(0, block, 16):
-            weights = weight_ref[pl.ds(pl.multiple_of(k * block + start, 16), 16), :].astype(F32)
+            weights = weight_ref[pl.ds(pl.multiple_of(k * block + start, 16), 16), :]
+            shift = jnp.full((16, LANES), g * PICKS, I32).astype(jnp.int16)
             for c in range(chunks):
-                at = index[side, start : start + 16, c * LANES : (c + 1) * LANES].astype(I32)
-                value = lane_pick(weights, (at + g * PICKS) & 127)
-                dense[side, start : start + 16, c * LANES : (c + 1) * LANES] = jnp.where(at >= 0, value, 0.0).astype(BF16)
+                at = index[side, start : start + 16, c * LANES : (c + 1) * LANES]
+                value = short_pick(weights, (at + shift) & jnp.int16(127))
+                dense[side, start : start + 16, c * LANES : (c + 1) * LANES] = jnp.where(at >= 0, value, jnp.zeros((), BF16))
 
     def save(b, side):
         g, k = b // per_group, lax.rem(b, per_group)
@@ -604,13 +613,13 @@
 
 def middle_kernel(
     ready, adapter, o_ref, x_ref, gain_ref, mix_ref, w_in_any, w_out_any, dn_any, up_any,
-    left_ref, right_ref, same_ref, sent_ref, att_ref, rank_ref, mid_ref, norm_ref, gate_ref, w, dn, up, sems,
+    left_ref, right_ref, same_ref, ahead_ref, sent_ref, att_ref, rank_ref, mid_ref, norm_ref, gate_ref, w, dn, up, sems,
 ):
     groups = o_ref.shape[0]
     a = adapter[0]
     copies = fetch(
         [(dn_any.at[3, a], dn.at[0]), (dn_any.at[5, a], dn.at[1]), (up_any.at[3, a], up.at[0]), (up_any.at[5, a], up.at[1]),
-         (w_out_any.at[0], w.at[0]), (w_in_any.at[4], w.at[1])],
+         (w_out_any.at[0], w.at[0]), (w_in_any.at[4], w.at[1]), (w_in_any.at[3], ahead_ref)],
         sems,
     )
     tokens = att_ref.shape[0]
@@ -644,22 +653,22 @@
     half = left_ref.shape[1]
     left_ref[...] = memory_grad[:, :half]
     right_ref[...] = memory_grad[:, half:]
+    copies[6].wait()
 
 
 def scores_kernel(
-    owners, ready, adapter, normed_ref, picks_ref, slot_ref, keys_ref, w_in_any, dn_any, up_any,
-    send_ref, rank_ref, weight_ref, w, dn, up, sems,
+    owners, ready, adapter, normed_ref, w_ref, picks_ref, slot_ref, keys_ref, dn_any, up_any,
+    send_ref, rank_ref, weight_ref, dn, up, sems,
 ):
     a = adapter[0]
-    copies = fetch([(dn_any.at[4, a], dn), (up_any.at[4, a], up), (w_in_any.at[3], w)], sems)
+    copies = fetch([(dn_any.at[4, a], dn), (up_any.at[4, a], up)], sems)
     normed = normed_ref[...]
     copies[0].wait()
     ranks = against(normed, dn[...]).astype(BF16)
     rank_ref[...] = ranks
     copies[1].wait()
     extra = product(ranks, up[...])
-    copies[2].wait()
-    query = (product(normed, w[...]) + extra).astype(BF16)
+    query = (product(normed, w_ref[...]) + extra).astype(BF16)
     ready()
     ready.send(rank_ref)
     first, second = [], []
@@ -795,9 +804,8 @@
     turned[...] = gscore
     ready(picks_ref, keys_ref)
     span = rows_dev // NSUB
-    halves = []
-    for h in range(MHEADS):
-
+
+    def head(h, carry):
         def one(r, sums):
             pick = picks_ref[h, pl.ds(r, 1), :]
             value = turned[pl.ds(h * PICKS + r, 1), :]
@@ -806,15 +814,18 @@
             return sums[0] + low, sums[1] + jnp.where(hit, value.astype(BF16), jnp.zeros((), BF16))
 
         start = (jnp.zeros((8, tokens), F32), jnp.zeros((NSUB, tokens), BF16))
-        first, second = lax.fori_loop(0, PICKS, one, start, unroll=8)
+        first, second = lax.fori_loop(0, PICKS, one, start, unroll=QUERY_UNROLL)
         origin = picks_ref[h, 0:1, :] // rows_dev
         place = iota((NSUB, tokens), 0)
         wide = jnp.concatenate([first[:span]] * (NSUB // span), axis=0)
         wide = jnp.where(place // span == origin, wide, 0.0)
-        halves.append(contract(wide.astype(BF16), keys_ref[0, h]))
-        halves.append(contract(second, keys_ref[1, h]))
-    gquery = jnp.concatenate(halves, axis=1).astype(BF16)
-    gquery_ref[...] = gquery
+        at = pl.multiple_of(h * 2 * KHALF, 2 * KHALF)
+        gquery_ref[:, pl.ds(at, KHALF)] = contract(wide.astype(BF16), keys_ref[0, h]).astype(BF16)
+        gquery_ref[:, pl.ds(at + KHALF, KHALF)] = contract(second, keys_ref[1, h]).astype(BF16)
+        return carry
+
+    lax.fori_loop(0, MHEADS, head, 0)
+    gquery = gquery_ref[...]
     ready.send(gquery_ref)
     ready()
     for copy in copies[:4]:
@@ -876,7 +887,7 @@
     out_ref[3 * RANK :, :] = upgrad_ref[...]
 
 
-def entry_kernel(ready, adapter, grads_ref, x_ref, gain_ref, gmid_ref, w_any, dn_any, up_any, out_ref, w, dn, up, sems):
+def entry_kernel(ready, adapter, grads_ref, x_ref, gain_ref, gmid_ref, w_any, dn_any, up_any, out_ref, w, gy, total, dn, up, sems):
     a = adapter[0]
     seq, _, wide = grads_ref.shape
     cols = wide // 3
@@ -887,22 +898,26 @@
         + [(w_any.at[j], w.at[j]) for j in range(3)],
         sems,
     )
-    gys = [
-        jnp.concatenate([grads_ref[s, 0:tokens, j * cols : (j + 1) * cols] for s in range(seq)], axis=1) for j in range(3)
-    ]
+    for j in range(3):
+        for s in range(seq):
+            gy[j, :, s * cols : (s + 1) * cols] = grads_ref[s, 0:tokens, j * cols : (j + 1) * cols]
     for copy in copies[:6]:
         copy.wait()
     place = iota((tokens, 3 * RANK), 1) // RANK
     granks = jnp.zeros((tokens, 3 * RANK), F32)
     for j in range(3):
-        granks = jnp.where(place == j, against(gys[j], up[...]), granks)
-    total = product(granks.astype(BF16), dn[...])
-    for j in range(3):
-        copies[6 + j].wait()
-        total = total + against(gys[j], w[j])
+        granks = jnp.where(place == j, against(gy[j], up[...]), granks)
+    total[...] = product(granks.astype(BF16), dn[...])
+
+    def one(j, carry):
+        pltpu.make_async_copy(w_any.at[j], w.at[j], sems.at[6 + j]).wait()
+        total[...] += against(gy[j], w[j])
+        return carry
+
+    lax.fori_loop(0, 3, one, 0)
     ready()
     x = x_ref[...].astype(F32)
-    back = norm_back(x, inverse_norm(x), gain_row(gain_ref), total)
+    back = norm_back(x, inverse_norm(x), gain_row(gain_ref), total[...])
     out_ref[...] = (gmid_ref[...] + back).astype(BF16)
 
 
@@ -1070,19 +1085,19 @@
     normed, attended = lax.optimization_barrier((normed, attended))
     normed_all = to_pairs(normed, "seq", seq)
 
-    left, right, same_two, sent, att, rank_pair, middle, normed_two, gate = call(
+    left, right, same_two, ahead, sent, att, rank_pair, middle, normed_two, gate = call(
         middle_kernel, "middle", "MVLLLHHHH",
         [("V", shaped((tokens, half), BF16)), ("V", shaped((tokens, half), BF16)), ("V", token_low),
-         ("S", shaped((seq, carried, cols), BF16)), ("S", token_low),
+         ("V", shaped((width, width), BF16)), ("S", shaped((seq, carried, cols), BF16)), ("S", token_low),
          ("S", shaped((2, tokens, RANK), BF16)), ("S", token_wide), ("S", token_low), ("S", token_wide)],
         (adapter_index, o_all, x, gain_two, mix_grad, input_weights, output_weights, down, adapter_up),
-        [pair, two_small, two_small, sema(6)],
+        [pair, two_small, two_small, sema(7)],
     )
     lefts = [left] + [along(left, "batch", k, batches) for k in range(1, batches)]
     weight_out, rank_four, weights = call(
-        fixed(scores_kernel, owners), "scores", "MVLLLHHH",
+        fixed(scores_kernel, owners), "scores", "MVVLLLHH",
         [("V", shaped((owners * 8, LANES), BF16)), ("S", token_rank), ("S", token_lanes)],
-        (adapter_index, same_two, pick, slot, half_keys, input_weights, down, adapter_up), [matrix, small, small, sema(3)],
+        (adapter_index, same_two, ahead, pick, slot, half_keys, down, adapter_up), [small, small, sema(2)],
     )
     weight_out, normed_all = lax.optimization_barrier((weight_out, normed_all))
     weight_in = exchange(weight_out.reshape(owners, 8, LANES), both).reshape(owners * 8, LANES)
@@ -1179,7 +1194,7 @@
     (grad_input,) = call(
         entry_kernel, "entry", "MVLLLHHH", [("S", token_low)],
         (adapter_index, grads_all, x, gain_one, gmid, input_weights, down, adapter_up),
-        [triple, three_small, three_small, sema(9)],
+        [triple, pltpu.VMEM((3, tokens, width), BF16), pltpu.VMEM((tokens, width), F32), three_small, three_small, sema(9)],
     )
     late_sums = [late_sum] + [along(late_sum, "batch", k, batches) for k in range(1, batches)]
     some = stacked(some, "pairsearly")

time: 231 us -> 228 us (0.987)
  Pallas kernels: 106 us -> 102 us
    pallas_call x28, Pallas kernels: 106 us -> 102 us  [call(): pl.pallas_call(wrapped, name=name, out_shape=[pltpu.HBM(out.shape, out.dt...]
  transfers between devices with their start and end apart: 40 -> 40, of which waited for: 14 -> 15; matrix products, arithmetic and copies ran while one was open for 0% -> 0% of each run, Pallas kernels for 36% -> 35%
where the time goes in v2:
time: 228 us; the launch traced here: 226 us
  Pallas kernels  102 us (45%)
  starting transfers between devices  73.4 us (32%)
  waiting for transfers between devices  48.4 us (21%)
  between operations  2.5 us (1%)
    pallas_call x28, Pallas kernels, call(): pl.pallas_call(wrapped, name=name, out_shape=[pltpu.HBM(out.shape, out.dt...  102 us
    all_to_all x10, starting transfers between devices, exchange(): return lax.all_to_all(values, axes, split_axis=0, concat_axis=0, tiled=True)  37.7 us
    all_to_all x10, waiting for transfers between devices, exchange(): return lax.all_to_all(values, axes, split_axis=0, concat_axis=0, tiled=True)  32.7 us
    ppermute x18, starting transfers between devices, along(): lax.ppermute(values, axis, [(i, (i + step) % size) for i in range(size)])  24.3 us
    ppermute x18, waiting for transfers between devices, along(): lax.ppermute(values, axis, [(i, (i + step) % size) for i in range(size)])  13.7 us
    ppermute x12, starting transfers between devices, across(): return lax.ppermute(values, axis, [(i, i ^ mask) for i in range(size)])  11.4 us
  transfers between devices with their start and end apart: 40, of which 15 were waited for; matrix products, arithmetic and copies ran while one was open for 0% of the time, Pallas kernels for 35%

profile of v2, /device:TPU:0, one launch (start us, length us, event | category | flops | bytes accessed | tf_op | source)
XLA Modules:
  0.0 226.4 jit_solution(5524027016404250997)
XLA Ops:
  1.3 5.7 %qkv.1 = (bf16[8,128,384]{2,1,0:T(8,128)(2,1)}, bf16[128,1152]{1,0:T(8,128)(2,1)}) custom-call(s32[1]{0:T(128)S(6)} %copy.22.refs_0_.refs_1_, bf16[128,1024]{1,0:T(8,128)(2,1)} %bitcast.32, bf16[1024]{0:T(1024)(128)(2,1)} %refs_3_.9, bf16[5,1024,1024]{2,1,0:T(8,128)(2,1)} %refs_5_.9, bf16[7,8,16,1024]{3,2,1,0:T(8,128)(2,1)} %bitcast.23, ...), custom_call_target="tpu_custom_call" | custom-call | flops 4096 | bytes 4096 | tf_op jit(solution)/shard_map/qkv/pallas_call | solution.py:119
  7.0 5.2 %all-to-all-start = ((bf16[8,128,384]{2,1,0:T(8,128)(2,1)}), bf16[8,128,384]{2,1,0:T(8,128)(2,1)S(1)}, u32[]{:S(2)}, u32[]{:S(2)}) async-start(bf16[8,128,384]{2,1,0:T(8,128)(2,1)} %get-tuple-element.109), calls=%async_computation | async-start | bytes 1572864 | tf_op jit(solution)/shard_map/all_to_all | solution.py:1024
  20.3 3.3 %mixback.1 = (bf16[128,1024]{1,0:T(8,128)(2,1)}, bf16[128,16]{1,0:T(8,128)(2,1)}) custom-call(s32[1]{0:T(128)S(6)} %copy.22.refs_0_.refs_1_, bf16[128,1024]{1,0:T(8,128)(2,1)} %bitcast.35, bf16[2,1024,1024]{2,1,0:T(8,128)(2,1)} %refs_3_.8, bf16[7,8,16,1024]{3,2,1,0:T(8,128)(2,1)} %bitcast.24, bf16[7,8,16,1024]{3,2,1,0:T(8,128)(2,1)} %refs_7_.7), custom_call_target="tpu_custom_call" | custom-call | flops 4096 | bytes 4096 | tf_op jit(solution)/shard_map/mixback/pallas_call | solution.py:119
  24.7 5.0 %attend.1 = (bf16[8,192,128]{2,1,0:T(8,128)(2,1)}, f32[8,1024]{1,0:T(8,128)}, s32[4,8,128]{2,1,0:T(8,128)}, bf16[1024,384]{1,0:T(8,128)(2,1)}) custom-call(s32[1]{0:T(128)S(6)} %copy.21.refs_0_, bf16[1024,384]{1,0:T(8,128)(2,1)S(1)} %bitcast.19, s32[72,128]{1,0:T(8,128)S(1)} %get-tuple-element.116.refs_2_, s32[72,128]{1,0:T(8,128)S(1)} %collective-permute-done.refs_3_, ...), custom_call_target="tpu_custom_call" | custom-call | flops 4096 | bytes 4096 | tf_op jit(solution)/shard_map/attend/pallas_call | solution.py:119
  29.8 3.8 %all-to-all-start.1 = ((bf16[8,192,128]{2,1,0:T(8,128)(2,1)}), bf16[8,192,128]{2,1,0:T(8,128)(2,1)S(1)}, u32[]{:S(2)}, u32[]{:S(2)}) async-start(bf16[8,192,128]{2,1,0:T(8,128)(2,1)} %get-tuple-element.120), calls=%async_computation.1 | async-start | bytes 786432 | tf_op jit(solution)/shard_map/all_to_all | solution.py:1024
  37.2 5.3 %all-to-all-done.1.refs_1_ = bf16[8,192,128]{2,1,0:T(8,128)(2,1)S(1)} async-done(((bf16[8,192,128]{2,1,0:T(8,128)(2,1)}), bf16[8,192,128]{2,1,0:T(8,128)(2,1)S(1)}, u32[]{:S(2)}, u32[]{:S(2)}) %all-to-all-start.1) | async-done | bytes 393248 | tf_op jit(solution)/shard_map/all_to_all | solution.py:1024
  42.5 4.8 %middle.1 = (bf16[128,512]{1,0:T(8,128)(2,1)S(1)}, bf16[128,512]{1,0:T(8,128)(2,1)S(1)}, bf16[128,1024]{1,0:T(8,128)(2,1)S(1)}, bf16[1024,1024]{1,0:T(8,128)(2,1...) custom-call(s32[1]{0:T(128)S(6)} %copy.22.refs_0_.refs_1_, ...), custom_call_target="tpu_custom_call" | custom-call | flops 4096 | bytes 4096 | tf_op jit(solution)/shard_map/middle/pallas_call | solution.py:119
  47.2 3.2 %collective-permute-start.5 = (bf16[128,512]{1,0:T(8,128)(2,1)S(1)}, bf16[128,512]{1,0:T(8,128)(2,1)S(1)}, u32[]{:S(2)}, u32[]{:S(2)}) collective-permute-start(bf16[128,512]{1,0:T(8,128)(2,1)S(1)} %get-tuple-element.139.refs_1_), channel_id=1, source_target_pairs={{0,24},{8,0},{16,8},{24,16},{1,25},{9,1},{17,9},{25,17},{2,26},{10... | collective-permute-start | bytes 393224 | tf_op jit(solution)/shard_map/ppermute | solution.py:1007
  51.5 4.2 %scores.1 = (bf16[256,128]{1,0:T(8,128)(2,1)}, bf16[128,16]{1,0:T(8,128)(2,1)}, f32[128,128]{1,0:T(8,128)}) custom-call(s32[1]{0:T(128)S(6)} %copy.22.refs_0_.refs_1_, bf16[128,1024]{1,0:T(8,128)(2,1)S(1)} %get-tuple-element.128.refs_1_, bf16[1024,1024]{1,0:T(8,128)(2,1)S(1)} %get-tuple-element.129.refs_2_, s32[128,128]{1,0:T(8,128)} %get-tuple-element.130.refs_3_, ...), custom_call_target="tpu_custom_call" | custom-call | flops 4096 | bytes 4096 | tf_op jit(solution)/shard_map/scores/pallas_call | solution.py:119
  55.7 3.6 %all-to-all-start.2 = ((bf16[32,8,128]{2,1,0:T(8,128)(2,1)}), bf16[32,8,128]{2,1,0:T(8,128)(2,1)S(1)}, u32[]{:S(2)}, u32[]{:S(2)}) async-start(bf16[32,8,128]{2,1,0:T(8,128)(2,1)} %bitcast.6), calls=%async_computation.2 | async-start | bytes 131072 | tf_op jit(solution)/shard_map/all_to_all | solution.py:1024
  63.7 3.0 %all-to-all-done.2 = bf16[32,8,128]{2,1,0:T(8,128)(2,1)S(1)} async-done(((bf16[32,8,128]{2,1,0:T(8,128)(2,1)}), bf16[32,8,128]{2,1,0:T(8,128)(2,1)S(1)}, u32[]{:S(2)}, u32[]{:S(2)}) %all-to-all-start.2) | async-done | bytes 65568 | tf_op jit(solution)/shard_map/all_to_all | solution.py:1024
  66.7 3.7 %all-to-all-start.3 = ((bf16[8,4,32,512]{3,2,1,0:T(8,128)(2,1)}), bf16[8,4,32,512]{3,2,1,0:T(8,128)(2,1)S(1)}, u32[]{:S(2)}, u32[]{:S(2)}) async-start(bf16[8,4,32,512]{3,2,1,0:T(8,128)(2,1)} %scatterleft.1), calls=%async_computation.3 | async-start | bytes 2097152 | tf_op jit(solution)/shard_map/all_to_all | solution.py:1024
  70.5 5.8 %prepare.1 = (s32[256,128]{1,0:T(8,128)}, s16[1024,2048]{1,0:T(8,128)(2,1)}) custom-call(bf16[8,64,128]{2,1,0:T(8,128)(2,1)} %get-tuple-element.156.refs_0_), custom_call_target="tpu_custom_call" | custom-call | flops 4096 | bytes 4096 | tf_op jit(solution)/shard_map/prepare/pallas_call | solution.py:119
  76.3 9.2 %recall.1 = bf16[8,4,32,1024]{3,2,1,0:T(8,128)(2,1)} custom-call(bf16[256,128]{1,0:T(8,128)(2,1)S(1)} %bitcast.22, s16[1024,2048]{1,0:T(8,128)(2,1)} %get-tuple-element.157.refs_1_, bf16[2048,1024]{1,0:T(8,128)(2,1)} %refs_3_.7), custom_call_target="tpu_custom_call" | custom-call | flops 4096 | bytes 4096 | tf_op jit(solution)/shard_map/recall/pallas_call | solution.py:119
  85.6 3.8 %all-to-all-start.4 = ((bf16[8,4,32,1024]{3,2,1,0:T(8,128)(2,1)}), bf16[8,4,32,1024]{3,2,1,0:T(8,128)(2,1)S(1)}, u32[]{:S(2)}, u32[]{:S(2)}) async-start(bf16[8,4,32,1024]{3,2,1,0:T(8,128)(2,1)} %recall.1), calls=%async_computation.4 | async-start | bytes 4194304 | tf_op jit(solution)/shard_map/all_to_all | solution.py:1024
  92.7 6.1 %recallleft.1.refs_1_ = f32[256,128]{1,0:T(8,128)} custom-call(s32[256,128]{1,0:T(8,128)} %get-tuple-element.160.refs_0_, bf16[1024,512]{1,0:T(8,128)(2,1)S(1)} %bitcast.17, bf16[2048,1024]{1,0:T(8,128)(2,1)} %refs_3_.7), custom_call_target="tpu_custom_call" | custom-call | flops 4096 | bytes 4096 | tf_op jit(solution)/shard_map/recallleft/pallas_call | solution.py:119
  98.8 5.0 %collective-permute-done.7.refs_3_ = bf16[128,512]{1,0:T(8,128)(2,1)S(1)} collective-permute-done((bf16[128,512]{1,0:T(8,128)(2,1)S(1)}, bf16[128,512]{1,0:T(8,128)(2,1)S(1)}, u32[]{:S(2)}, u32[]{:S(2)}) %collective-permute-start.7) | collective-permute-done | bytes 131104 | tf_op jit(solution)/shard_map/ppermute | solution.py:1007
  106.0 10.1 %all-to-all-done.4.refs_1_ = bf16[8,4,32,1024]{3,2,1,0:T(8,128)(2,1)S(1)} async-done(((bf16[8,4,32,1024]{3,2,1,0:T(8,128)(2,1)}), bf16[8,4,32,1024]{3,2,1,0:T(8,128)(2,1)S(1)}, u32[]{:S(2)}, u32[]{:S(2)}) %all-to-all-start.4) | async-done | bytes 2097184 | tf_op jit(solution)/shard_map/all_to_all | solution.py:1024
  116.1 3.6 %all-to-all-start.5 = ((bf16[8,4,32,512]{3,2,1,0:T(8,128)(2,1)}), bf16[8,4,32,512]{3,2,1,0:T(8,128)(2,1)S(1)}, u32[]{:S(2)}, u32[]{:S(2)}) async-start(bf16[8,4,32,512]{3,2,1,0:T(8,128)(2,1)} %scatterright.1), calls=%async_computation.5 | async-start | bytes 2097152 | tf_op jit(solution)/shard_map/all_to_all | solution.py:1024
  124.4 10.6 %all-to-all-done.5 = bf16[8,4,32,512]{3,2,1,0:T(8,128)(2,1)S(1)} async-done(((bf16[8,4,32,512]{3,2,1,0:T(8,128)(2,1)}), bf16[8,4,32,512]{3,2,1,0:T(8,128)(2,1)S(1)}, u32[]{:S(2)}, u32[]{:S(2)}) %all-to-all-start.5) | async-done | bytes 1048608 | tf_op jit(solution)/shard_map/all_to_all | solution.py:1024
  135.0 6.2 %recallright.1 = bf16[256,128]{1,0:T(8,128)(2,1)} custom-call(s32[256,128]{1,0:T(8,128)} %get-tuple-element.160.refs_0_, f32[256,128]{1,0:T(8,128)} %recallleft.1.refs_1_, bf16[1024,512]{1,0:T(8,128)(2,1)S(1)} %bitcast.18, bf16[2048,1024]{1,0:T(8,128)(2,1)} %refs_3_.7), custom_call_target="tpu_custom_call" | custom-call | flops 4096 | bytes 4096 | tf_op jit(solution)/shard_map/recallright/pallas_call | solution.py:119
  143.8 3.8 %collective-permute-done.14.refs_5_ = bf16[128,1024]{1,0:T(8,128)(2,1)S(1)} collective-permute-done((bf16[128,1024]{1,0:T(8,128)(2,1)}, bf16[128,1024]{1,0:T(8,128)(2,1)S(1)}, u32[]{:S(2)}, u32[]{:S(2)}) %collective-permute-start.14) | collective-permute-done | bytes 262176 | tf_op jit(solution)/shard_map/ppermute | solution.py:1007
  147.6 3.6 %memory.1 = (bf16[128,1024]{1,0:T(8,128)(2,1)}, bf16[128,16]{1,0:T(8,128)(2,1)}, bf16[128,1024]{1,0:T(8,128)(2,1)}, f32[128,1024]{1,0:T(8,128)}) custom-call(s32[1]{0:T(128)S(6)} %copy.22.refs_0_.refs_1_, f32[128,1024]{1,0:T(8,128)} %get-tuple-element.122.refs_1_, bf16[128,1024]{1,0:T(8,128)(2,1)} %get-tuple-element.121.refs_4_.refs_2_, ...), custom_call_target="tpu_custom_call" | custom-call | flops 4096 | bytes 4096 | tf_op jit(solution)/shard_map/memory/pallas_call | solution.py:119
  151.2 9.1 %query.1 = (bf16[8,128,128]{2,1,0:T(8,128)(2,1)}, bf16[128,1024]{1,0:T(8,128)(2,1)}, bf16[2,128,16]{2,1,0:T(8,128)(2,1)}, f32[128,1024]{1,0:T(8,128)}) custom-call(s32[1]{0:T(128)S(6)} %copy.21.refs_0_, s32[1]{0:T(128)S(6)} %copy.22.refs_0_.refs_1_, bf16[256,128]{1,0:T(8,128)(2,1)S(1)} %bitcast.21, s32[128,128]{1,0:T(8,128)} %get-tuple-element.170.refs_3_, ...), custom_call_target="tpu_custom_call" | custom-call | flops 4096 | bytes 4096 | tf_op jit(solution)/shard_map/query/pallas_call | solution.py:119
  160.3 3.9 %all-to-all-start.7 = ((bf16[8,128,128]{2,1,0:T(8,128)(2,1)}), bf16[8,128,128]{2,1,0:T(8,128)(2,1)S(1)}, u32[]{:S(2)}, u32[]{:S(2)}) async-start(bf16[8,128,128]{2,1,0:T(8,128)(2,1)} %get-tuple-element.174), calls=%async_computation.7 | async-start | bytes 524288 | tf_op jit(solution)/shard_map/all_to_all | solution.py:1024
  164.2 3.2 %output.1 = (bf16[128,1024]{1,0:T(8,128)(2,1)}, bf16[128,16]{1,0:T(8,128)(2,1)}) custom-call(s32[1]{0:T(128)S(6)} %copy.22.refs_0_.refs_1_, bf16[128,1024]{1,0:T(8,128)(2,1)} %get-tuple-element.175.refs_1_.refs_2_, f32[128,1024]{1,0:T(8,128)} %get-tuple-element.173.refs_7_.refs_2_, bf16[2,1024,1024]{2,1,0:T(8,128)(2,1)} %refs_3_.8, ...), custom_call_target="tpu_custom_call" | custom-call | flops 4096 | bytes 4096 | tf_op jit(solution)/shard_map/output/pallas_call | solution.py:119
  171.2 3.4 %all-to-all-start.8 = ((bf16[8,128,128]{2,1,0:T(8,128)(2,1)}), bf16[8,128,128]{2,1,0:T(8,128)(2,1)S(1)}, u32[]{:S(2)}, u32[]{:S(2)}) async-start(bf16[8,128,128]{2,1,0:T(8,128)(2,1)} %factors.1), calls=%async_computation.8 | async-start | bytes 524288 | tf_op jit(solution)/shard_map/all_to_all | solution.py:1024
  174.6 10.1 %attendback.1 = (bf16[8,144,384]{2,1,0:T(8,128)(2,1)}, bf16[48,128]{1,0:T(8,128)(2,1)}) custom-call(s32[1]{0:T(128)S(6)} %copy.21.refs_0_, s32[1]{0:T(128)S(6)} %copy.22.refs_0_.refs_1_, bf16[1024,384]{1,0:T(8,128)(2,1)} %get-tuple-element.177.refs_2_, bf16[1024,128]{1,0:T(8,128)(2,1)S(1)} %bitcast.20, f32[8,1024]{1,0:T(8,128)} %get-tuple-element.190.refs_4_, ...), custom_call_target="tpu_custom_call" | custom-call | flops 4096 | bytes 4096 | tf_op jit(solution)/shard_map/attendback/pallas_call | solution.py:119
  184.7 4.1 %all-to-all-start.9 = ((bf16[8,144,384]{2,1,0:T(8,128)(2,1)}), bf16[8,144,384]{2,1,0:T(8,128)(2,1)S(1)}, u32[]{:S(2)}, u32[]{:S(2)}) async-start(bf16[8,144,384]{2,1,0:T(8,128)(2,1)} %get-tuple-element.195), calls=%async_computation.9 | async-start | bytes 1769472 | tf_op jit(solution)/shard_map/all_to_all | solution.py:1024
  208.4 5.3 %entry.1 = bf16[128,1024]{1,0:T(8,128)(2,1)} custom-call(s32[1]{0:T(128)S(6)} %copy.22.refs_0_.refs_1_, bf16[8,144,384]{2,1,0:T(8,128)(2,1)S(1)} %all-to-all-done.9.refs_0_.refs_1_, bf16[128,1024]{1,0:T(8,128)(2,1)} %bitcast.34, bf16[1024]{0:T(1024)(128)(2,1)} %refs_3_.9, f32[128,1024]{1,0:T(8,128)} %get-tuple-element.180.refs_3_.refs_4_, ...), custom_call_target="tpu_custom_call" | custom-call | flops 4096 | bytes 4096 | tf_op jit(solution)/shard_map/entry/pallas_call | solution.py:119
  217.4 3.7 %spread.1 = (f32[7,8,16,1024]{3,2,1,0:T(8,128)}, f32[7,8,16,1024]{3,2,1,0:T(8,128)}) custom-call(s32[256,128]{1,0:T(8,128)} %get-tuple-element.160.refs_0_, bf16[4,4,128,128]{3,2,1,0:T(8,128)(2,1)S(1)} %pairsearly.1.refs_1_, bf16[4,4,128,128]{3,2,1,0:T(8,128)(2,1)S(1)} %collective-permute-done.28.refs_2_), custom_call_target="tpu_custom_call" | custom-call | flops 4096 | bytes 4096 | tf_op jit(solution)/shard_map/spread/pallas_call | solution.py:119
  223.3 3.0 %lastspread.1 = (f32[7,8,16,1024]{3,2,1,0:T(8,128)}, f32[7,8,16,1024]{3,2,1,0:T(8,128)}) custom-call(s32[256,128]{1,0:T(8,128)} %get-tuple-element.160.refs_0_, f32[7,8,16,1024]{3,2,1,0:T(8,128)} %get-tuple-element.206.refs_1_, f32[7,8,16,1024]{3,2,1,0:T(8,128)} %get-tuple-element.207.refs_2_, ...), custom_call_target="tpu_custom_call", output_to_operand_aliasing={{0}: (1, {}), {1}: (2, {})} | custom-call | flops 4096 | bytes 4096 | tf_op jit(solution)/shard_map/lastspread/pallas_call | solution.py:119
  (78 shorter events, 59.3 us)
Async XLA Ops:
  7.0 17.8 %all-to-all-start = ((bf16[8,128,384]{2,1,0:T(8,128)(2,1)}), bf16[8,128,384]{2,1,0:T(8,128)(2,1)S(1)}, u32[]{:S(2)}, u32[]{:S(2)}) async-start(bf16[8,128,384]{2,1,0:T(8,128)(2,1)} %get-tuple-element.109), calls=%async_computation | async-start | bytes 1572864 | tf_op jit(solution)/shard_map/all_to_all | solution.py:1024
  14.8 9.6 %collective-permute-start = (s32[72,128]{1,0:T(8,128)S(1)}, s32[72,128]{1,0:T(8,128)S(1)}, u32[]{:S(2)}, u32[]{:S(2)}) collective-permute-start(s32[72,128]{1,0:T(8,128)S(1)} %get-tuple-element.111), channel_id=1, source_target_pairs={{0,8},{8,16},{16,24},{24,0},{1,9},{9,17},{17,25},{25,1},{2,10},{10... | collective-permute-start | bytes 110600 | tf_op jit(solution)/shard_map/ppermute | solution.py:1007
  16.4 7.9 %collective-permute-start.1 = (s32[72,128]{1,0:T(8,128)S(1)}, s32[72,128]{1,0:T(8,128)S(1)}, u32[]{:S(2)}, u32[]{:S(2)}) collective-permute-start(s32[72,128]{1,0:T(8,128)S(1)} %get-tuple-element.112), channel_id=1, source_target_pairs={{0,16},{8,24},{16,0},{24,8},{1,17},{9,25},{17,1},{25,9},{2,18},{10... | collective-permute-start | bytes 110600 | tf_op jit(solution)/shard_map/ppermute | solution.py:1007
  29.8 12.7 %all-to-all-start.1 = ((bf16[8,192,128]{2,1,0:T(8,128)(2,1)}), bf16[8,192,128]{2,1,0:T(8,128)(2,1)S(1)}, u32[]{:S(2)}, u32[]{:S(2)}) async-start(bf16[8,192,128]{2,1,0:T(8,128)(2,1)} %get-tuple-element.120), calls=%async_computation.1 | async-start | bytes 786432 | tf_op jit(solution)/shard_map/all_to_all | solution.py:1024
  33.6 16.9 %collective-permute-start.11 = (bf16[128,1152]{1,0:T(8,128)(2,1)S(1)}, bf16[128,1152]{1,0:T(8,128)(2,1)S(1)}, u32[]{:S(2)}, u32[]{:S(2)}) collective-permute-start(bf16[128,1152]{1,0:T(8,128)(2,1)S(1)} %copy-done), channel_id=1, source_target_pairs={{0,6},{1,7},{2,4},{3,5},{4,2},{5,3},{6,0},{7,1},{8,14},{9,15},{10,... | collective-permute-start | bytes 884744 | tf_op jit(solution)/shard_map/ppermute | solution.py:1011
  36.5 19.2 %collective-permute-start.10 = (bf16[128,1152]{1,0:T(8,128)(2,1)S(1)}, bf16[128,1152]{1,0:T(8,128)(2,1)S(1)}, u32[]{:S(2)}, u32[]{:S(2)}) collective-permute-start(bf16[128,1152]{1,0:T(8,128)(2,1)S(1)} %copy-done), channel_id=1, source_target_pairs={{0,4},{1,5},{2,6},{3,7},{4,0},{5,1},{6,2},{7,3},{8,12},{9,13},{10,... | collective-permute-start | bytes 884744 | tf_op jit(solution)/shard_map/ppermute | solution.py:1011
  37.1 18.6 %collective-permute-start.9 = (bf16[128,1152]{1,0:T(8,128)(2,1)S(1)}, bf16[128,1152]{1,0:T(8,128)(2,1)S(1)}, u32[]{:S(2)}, u32[]{:S(2)}) collective-permute-start(bf16[128,1152]{1,0:T(8,128)(2,1)S(1)} %copy-done), channel_id=1, source_target_pairs={{0,2},{1,3},{2,0},{3,1},{4,6},{5,7},{6,4},{7,5},{8,10},{9,11},{10,... | collective-permute-start | bytes 884744 | tf_op jit(solution)/shard_map/ppermute | solution.py:1011
  47.2 12.1 %collective-permute-start.5 = (bf16[128,512]{1,0:T(8,128)(2,1)S(1)}, bf16[128,512]{1,0:T(8,128)(2,1)S(1)}, u32[]{:S(2)}, u32[]{:S(2)}) collective-permute-start(bf16[128,512]{1,0:T(8,128)(2,1)S(1)} %get-tuple-element.139.refs_1_), channel_id=1, source_target_pairs={{0,24},{8,0},{16,8},{24,16},{1,25},{9,1},{17,9},{25,17},{2,26},{10... | collective-permute-start | bytes 393224 | tf_op jit(solution)/shard_map/ppermute | solution.py:1007
  50.5 9.9 %collective-permute-start.4 = (bf16[128,512]{1,0:T(8,128)(2,1)S(1)}, bf16[128,512]{1,0:T(8,128)(2,1)S(1)}, u32[]{:S(2)}, u32[]{:S(2)}) collective-permute-start(bf16[128,512]{1,0:T(8,128)(2,1)S(1)} %get-tuple-element.139.refs_1_), channel_id=1, source_target_pairs={{0,16},{8,24},{16,0},{24,8},{1,17},{9,25},{17,1},{25,9},{2,18},{10... | collective-permute-start | bytes 393224 | tf_op jit(solution)/shard_map/ppermute | solution.py:1007
  50.5 9.9 %collective-permute-start.3 = (bf16[128,512]{1,0:T(8,128)(2,1)S(1)}, bf16[128,512]{1,0:T(8,128)(2,1)S(1)}, u32[]{:S(2)}, u32[]{:S(2)}) collective-permute-start(bf16[128,512]{1,0:T(8,128)(2,1)S(1)} %get-tuple-element.139.refs_1_), channel_id=1, source_target_pairs={{0,8},{8,16},{16,24},{24,0},{1,9},{9,17},{17,25},{25,1},{2,10},{10... | collective-permute-start | bytes 393224 | tf_op jit(solution)/shard_map/ppermute | solution.py:1007
  55.7 11.0 %all-to-all-start.2 = ((bf16[32,8,128]{2,1,0:T(8,128)(2,1)}), bf16[32,8,128]{2,1,0:T(8,128)(2,1)S(1)}, u32[]{:S(2)}, u32[]{:S(2)}) async-start(bf16[32,8,128]{2,1,0:T(8,128)(2,1)} %bitcast.6), calls=%async_computation.2 | async-start | bytes 131072 | tf_op jit(solution)/shard_map/all_to_all | solution.py:1024
  66.7 18.9 %all-to-all-start.3 = ((bf16[8,4,32,512]{3,2,1,0:T(8,128)(2,1)}), bf16[8,4,32,512]{3,2,1,0:T(8,128)(2,1)S(1)}, u32[]{:S(2)}, u32[]{:S(2)}) async-start(bf16[8,4,32,512]{3,2,1,0:T(8,128)(2,1)} %scatterleft.1), calls=%async_computation.3 | async-start | bytes 2097152 | tf_op jit(solution)/shard_map/all_to_all | solution.py:1024
  85.6 30.5 %all-to-all-start.4 = ((bf16[8,4,32,1024]{3,2,1,0:T(8,128)(2,1)}), bf16[8,4,32,1024]{3,2,1,0:T(8,128)(2,1)S(1)}, u32[]{:S(2)}, u32[]{:S(2)}) async-start(bf16[8,4,32,1024]{3,2,1,0:T(8,128)(2,1)} %recall.1), calls=%async_computation.4 | async-start | bytes 4194304 | tf_op jit(solution)/shard_map/all_to_all | solution.py:1024
  89.4 14.4 %collective-permute-start.12 = (bf16[4,128,1152]{2,1,0:T(8,128)(2,1)}, bf16[4,128,1152]{2,1,0:T(8,128)(2,1)}, u32[]{:S(2)}, u32[]{:S(2)}) collective-permute-start(bf16[4,128,1152]{2,1,0:T(8,128)(2,1)} %pairsnorm.1.refs_5_), channel_id=1, source_target_pairs={{0,1},{1,0},{2,3},{3,2},{4,5},{5,4},{6,7},{7,6},{8,9},{9,8},{10,11... | collective-permute-start | bytes 3538952 | tf_op jit(solution)/shard_map/ppermute | solution.py:1011
  90.0 8.9 %collective-permute-start.8 = (bf16[128,512]{1,0:T(8,128)(2,1)S(1)}, bf16[128,512]{1,0:T(8,128)(2,1)S(1)}, u32[]{:S(2)}, u32[]{:S(2)}) collective-permute-start(bf16[128,512]{1,0:T(8,128)(2,1)S(1)} %get-tuple-element.151.refs_1_), channel_id=1, source_target_pairs={{0,24},{8,0},{16,8},{24,16},{1,25},{9,1},{17,9},{25,17},{2,26},{10... | collective-permute-start | bytes 393224 | tf_op jit(solution)/shard_map/ppermute | solution.py:1007
  90.9 13.0 %collective-permute-start.7 = (bf16[128,512]{1,0:T(8,128)(2,1)S(1)}, bf16[128,512]{1,0:T(8,128)(2,1)S(1)}, u32[]{:S(2)}, u32[]{:S(2)}) collective-permute-start(bf16[128,512]{1,0:T(8,128)(2,1)S(1)} %get-tuple-element.151.refs_1_), channel_id=1, source_target_pairs={{0,16},{8,24},{16,0},{24,8},{1,17},{9,25},{17,1},{25,9},{2,18},{10... | collective-permute-start | bytes 393224 | tf_op jit(solution)/shard_map/ppermute | solution.py:1007
  92.0 11.8 %collective-permute-start.6 = (bf16[128,512]{1,0:T(8,128)(2,1)S(1)}, bf16[128,512]{1,0:T(8,128)(2,1)S(1)}, u32[]{:S(2)}, u32[]{:S(2)}) collective-permute-start(bf16[128,512]{1,0:T(8,128)(2,1)S(1)} %get-tuple-element.151.refs_1_), channel_id=1, source_target_pairs={{0,8},{8,16},{16,24},{24,0},{1,9},{9,17},{17,25},{25,1},{2,10},{10... | collective-permute-start | bytes 393224 | tf_op jit(solution)/shard_map/ppermute | solution.py:1007
  116.1 18.9 %all-to-all-start.5 = ((bf16[8,4,32,512]{3,2,1,0:T(8,128)(2,1)}), bf16[8,4,32,512]{3,2,1,0:T(8,128)(2,1)S(1)}, u32[]{:S(2)}, u32[]{:S(2)}) async-start(bf16[8,4,32,512]{3,2,1,0:T(8,128)(2,1)} %scatterright.1), calls=%async_computation.5 | async-start | bytes 2097152 | tf_op jit(solution)/shard_map/all_to_all | solution.py:1024
  121.7 22.1 %collective-permute-start.13 = (bf16[128,1024]{1,0:T(8,128)(2,1)}, bf16[128,1024]{1,0:T(8,128)(2,1)S(1)}, u32[]{:S(2)}, u32[]{:S(2)}) collective-permute-start(bf16[128,1024]{1,0:T(8,128)(2,1)} %get-tuple-element.164), channel_id=1, source_target_pairs={{0,24},{8,0},{16,8},{24,16},{1,25},{9,1},{17,9},{25,17},{2,26},{10... | collective-permute-start | bytes 786440 | tf_op jit(solution)/shard_map/ppermute | solution.py:1007
  122.6 24.9 %collective-permute-start.14 = (bf16[128,1024]{1,0:T(8,128)(2,1)}, bf16[128,1024]{1,0:T(8,128)(2,1)S(1)}, u32[]{:S(2)}, u32[]{:S(2)}) collective-permute-start(bf16[128,1024]{1,0:T(8,128)(2,1)} %get-tuple-element.165), channel_id=1, source_target_pairs={{0,16},{8,24},{16,0},{24,8},{1,17},{9,25},{17,1},{25,9},{2,18},{10... | collective-permute-start | bytes 786440 | tf_op jit(solution)/shard_map/ppermute | solution.py:1007
  123.8 23.8 %collective-permute-start.15 = (bf16[128,1024]{1,0:T(8,128)(2,1)}, bf16[128,1024]{1,0:T(8,128)(2,1)S(1)}, u32[]{:S(2)}, u32[]{:S(2)}) collective-permute-start(bf16[128,1024]{1,0:T(8,128)(2,1)} %get-tuple-element.166), channel_id=1, source_target_pairs={{0,8},{8,16},{16,24},{24,0},{1,9},{9,17},{17,25},{25,1},{2,10},{10... | collective-permute-start | bytes 786440 | tf_op jit(solution)/shard_map/ppermute | solution.py:1007
  141.2 10.0 %all-to-all-start.6 = ((bf16[32,8,128]{2,1,0:T(8,128)(2,1)}), bf16[32,8,128]{2,1,0:T(8,128)(2,1)S(1)}, u32[]{:S(2)}, u32[]{:S(2)}) async-start(bf16[32,8,128]{2,1,0:T(8,128)(2,1)} %bitcast.10), calls=%async_computation.6 | async-start | bytes 131072 | tf_op jit(solution)/shard_map/all_to_all | solution.py:1024
  160.3 10.8 %all-to-all-start.7 = ((bf16[8,128,128]{2,1,0:T(8,128)(2,1)}), bf16[8,128,128]{2,1,0:T(8,128)(2,1)S(1)}, u32[]{:S(2)}, u32[]{:S(2)}) async-start(bf16[8,128,128]{2,1,0:T(8,128)(2,1)} %get-tuple-element.174), calls=%async_computation.7 | async-start | bytes 524288 | tf_op jit(solution)/shard_map/all_to_all | solution.py:1024
  171.2 13.5 %all-to-all-start.8 = ((bf16[8,128,128]{2,1,0:T(8,128)(2,1)}), bf16[8,128,128]{2,1,0:T(8,128)(2,1)S(1)}, u32[]{:S(2)}, u32[]{:S(2)}) async-start(bf16[8,128,128]{2,1,0:T(8,128)(2,1)} %factors.1), calls=%async_computation.8 | async-start | bytes 524288 | tf_op jit(solution)/shard_map/all_to_all | solution.py:1024
  184.7 18.4 %all-to-all-start.9 = ((bf16[8,144,384]{2,1,0:T(8,128)(2,1)}), bf16[8,144,384]{2,1,0:T(8,128)(2,1)S(1)}, u32[]{:S(2)}, u32[]{:S(2)}) async-start(bf16[8,144,384]{2,1,0:T(8,128)(2,1)} %get-tuple-element.195), calls=%async_computation.9 | async-start | bytes 1769472 | tf_op jit(solution)/shard_map/all_to_all | solution.py:1024
  197.2 9.2 %collective-permute-start.24 = (bf16[4,128,128]{2,1,0:T(8,128)(2,1)S(1)}, bf16[4,128,128]{2,1,0:T(8,128)(2,1)S(1)}, u32[]{:S(2)}, u32[]{:S(2)}) collective-permute-start(bf16[4,128,128]{2,1,0:T(8,128)(2,1)S(1)} %stackearly.1.refs_0_), channel_id=1, source_target_pairs={{0,6},{1,7},{2,4},{3,5},{4,2},{5,3},{6,0},{7,1},{8,14},{9,15},{10,... | collective-permute-start | bytes 393224 | tf_op jit(solution)/shard_map/ppermute | solution.py:1011
  200.2 8.2 %collective-permute-start.23 = (bf16[4,128,128]{2,1,0:T(8,128)(2,1)S(1)}, bf16[4,128,128]{2,1,0:T(8,128)(2,1)S(1)}, u32[]{:S(2)}, u32[]{:S(2)}) collective-permute-start(bf16[4,128,128]{2,1,0:T(8,128)(2,1)S(1)} %stackearly.1.refs_0_), channel_id=1, source_target_pairs={{0,4},{1,5},{2,6},{3,7},{4,0},{5,1},{6,2},{7,3},{8,12},{9,13},{10,... | collective-permute-start | bytes 393224 | tf_op jit(solution)/shard_map/ppermute | solution.py:1011
  200.8 7.6 %collective-permute-start.22 = (bf16[4,128,128]{2,1,0:T(8,128)(2,1)S(1)}, bf16[4,128,128]{2,1,0:T(8,128)(2,1)S(1)}, u32[]{:S(2)}, u32[]{:S(2)}) collective-permute-start(bf16[4,128,128]{2,1,0:T(8,128)(2,1)S(1)} %stackearly.1.refs_0_), channel_id=1, source_target_pairs={{0,2},{1,3},{2,0},{3,1},{4,6},{5,7},{6,4},{7,5},{8,10},{9,11},{10,... | collective-permute-start | bytes 393224 | tf_op jit(solution)/shard_map/ppermute | solution.py:1011
  203.8 9.9 %collective-permute-start.18 = (bf16[96,128]{1,0:T(8,128)(2,1)S(1)}, bf16[96,128]{1,0:T(8,128)(2,1)S(1)}, u32[]{:S(2)}, u32[]{:S(2)}) collective-permute-start(bf16[96,128]{1,0:T(8,128)(2,1)S(1)} %late.1.refs_0_), channel_id=1, source_target_pairs={{0,24},{8,0},{16,8},{24,16},{1,25},{9,1},{17,9},{25,17},{2,26},{10... | collective-permute-start | bytes 73736 | tf_op jit(solution)/shard_map/ppermute | solution.py:1007
  205.6 8.2 %collective-permute-start.17 = (bf16[96,128]{1,0:T(8,128)(2,1)S(1)}, bf16[96,128]{1,0:T(8,128)(2,1)S(1)}, u32[]{:S(2)}, u32[]{:S(2)}) collective-permute-start(bf16[96,128]{1,0:T(8,128)(2,1)S(1)} %late.1.refs_0_), channel_id=1, source_target_pairs={{0,16},{8,24},{16,0},{24,8},{1,17},{9,25},{17,1},{25,9},{2,18},{10... | collective-permute-start | bytes 73736 | tf_op jit(solution)/shard_map/ppermute | solution.py:1007
  206.4 7.4 %collective-permute-start.16 = (bf16[96,128]{1,0:T(8,128)(2,1)S(1)}, bf16[96,128]{1,0:T(8,128)(2,1)S(1)}, u32[]{:S(2)}, u32[]{:S(2)}) collective-permute-start(bf16[96,128]{1,0:T(8,128)(2,1)S(1)} %late.1.refs_0_), channel_id=1, source_target_pairs={{0,8},{8,16},{16,24},{24,0},{1,9},{9,17},{17,25},{25,1},{2,10},{10... | collective-permute-start | bytes 73736 | tf_op jit(solution)/shard_map/ppermute | solution.py:1007
  213.9 7.3 %collective-permute-start.27 = (bf16[4,96,128]{2,1,0:T(8,128)(2,1)S(1)}, bf16[4,96,128]{2,1,0:T(8,128)(2,1)S(1)}, u32[]{:S(2)}, u32[]{:S(2)}) collective-permute-start(bf16[4,96,128]{2,1,0:T(8,128)(2,1)S(1)} %stacklate.1.refs_0_), channel_id=1, source_target_pairs={{0,6},{1,7},{2,4},{3,5},{4,2},{5,3},{6,0},{7,1},{8,14},{9,15},{10,... | collective-permute-start | bytes 294920 | tf_op jit(solution)/shard_map/ppermute | solution.py:1011
  (9 other events, 52.0 us)

commit v3 on v2

--- a/solution.py
+++ b/solution.py
@@ -64,11 +64,17 @@
     def __init__(self, loads, stores):
         self.loads, self.stores = loads, stores
         self.waited, self.begun = set(), set()
-        for _, copy in loads:
-            copy.start()
+        for _, copy, later in loads:
+            if not later:
+                copy.start()
+
+    def begin(self):
+        for _, copy, later in self.loads:
+            if later:
+                copy.start()
 
     def __call__(self, *refs):
-        for at, (ref, copy) in enumerate(self.loads):
+        for at, (ref, copy, _) in enumerate(self.loads):
             if at not in self.waited and (not refs or any(ref is one for one in refs)):
                 self.waited.add(at)
                 copy.wait()
@@ -87,7 +93,7 @@
 
 
 def call(kernel, name, ins, outs, args, scratch=(), vmem=40, flops=1 << 12, moved=1 << 12, aliases=None):
-    shapes = [(args[i].shape, args[i].dtype) for i, kind in enumerate(ins) if kind == "L"]
+    shapes = [(args[i].shape, args[i].dtype) for i, kind in enumerate(ins) if kind in "LD"]
     stored = [(out.shape, out.dtype) for kind, out in outs if kind == "S"]
     count_in, count_out, count_user = len(ins), len(outs), len(scratch)
 
@@ -97,9 +103,10 @@
         user, buffers = rest[:count_user], rest[count_user:]
         loads, stores = [], []
         for i, kind in enumerate(ins):
-            if kind == "L":
+            if kind in "LD":
                 at = len(loads)
-                loads.append((buffers[at], pltpu.make_async_copy(given[i], buffers[at], buffers[-1].at[at])))
+                copy = pltpu.make_async_copy(given[i], buffers[at], buffers[-1].at[at])
+                loads.append((buffers[at], copy, kind == "D"))
                 given[i] = buffers[at]
         for i, (kind, _) in enumerate(outs):
             if kind == "S":
@@ -110,10 +117,10 @@
         kernel(stage, *given, *results, *user)
         stage.finish()
 
-    spaces = {"V": VMEM, "L": HBM, "S": HBM, "H": HBM, "M": SMEM}
+    spaces = {"V": VMEM, "L": HBM, "D": HBM, "S": HBM, "H": HBM, "M": SMEM}
     autos = [pltpu.VMEM(*one) for one in shapes + stored]
     args = [
-        pltpu.with_memory_space_constraint(one, pltpu.HBM) if kind in "LH" else one
+        pltpu.with_memory_space_constraint(one, pltpu.HBM) if kind in "LDH" else one
         for kind, one in zip(ins, args, strict=True)
     ]
     return pl.pallas_call(
@@ -777,15 +784,10 @@
 def query_kernel(
     owners, rows_dev, ready, length, adapter, back_ref, slot_ref, picks_ref, weight_ref, part_ref, mid_ref, cot_ref, gain_ref,
     keys_ref, w_in_any, w_out_any, dn_any, up_any,
-    go_ref, gquery_ref, grank_ref, gmid_ref, w, dn, up, turned, sems,
+    go_ref, gquery_ref, grank_ref, gmid_ref, w, dn, up, turned, spots, sems,
 ):
     groups, tokens, cols = go_ref.shape
     a = adapter[0]
-    copies = fetch(
-        [(dn_any.at[3, a], dn.at[0]), (dn_any.at[4, a], dn.at[1]), (up_any.at[3, a], up.at[0]),
-         (up_any.at[4, a], up.at[1]), (w_in_any.at[3], w.at[0]), (w_out_any.at[0], w.at[1])],
-        sems,
-    )
     ready(slot_ref, weight_ref)
     capacity = 2 * MHEADS * tokens // owners
     slots = iota((tokens, owners * 8), 1)
@@ -803,6 +805,12 @@
     gscore = jnp.transpose(weights * (gw - group_reduce(weights * gw, jnp.sum, 0.0)))
     turned[...] = gscore
     ready(picks_ref, keys_ref)
+    ready.begin()
+    copies = fetch(
+        [(dn_any.at[3, a], dn.at[0]), (dn_any.at[4, a], dn.at[1]), (up_any.at[3, a], up.at[0]),
+         (up_any.at[4, a], up.at[1]), (w_in_any.at[3], w.at[0]), (w_out_any.at[0], w.at[1])],
+        sems,
+    )
     span = rows_dev // NSUB
 
     def head(h, carry):
@@ -819,13 +827,14 @@
         place = iota((NSUB, tokens), 0)
         wide = jnp.concatenate([first[:span]] * (NSUB // span), axis=0)
         wide = jnp.where(place // span == origin, wide, 0.0)
-        at = pl.multiple_of(h * 2 * KHALF, 2 * KHALF)
-        gquery_ref[:, pl.ds(at, KHALF)] = contract(wide.astype(BF16), keys_ref[0, h]).astype(BF16)
-        gquery_ref[:, pl.ds(at + KHALF, KHALF)] = contract(second, keys_ref[1, h]).astype(BF16)
+        spots[h, 0] = wide.astype(BF16)
+        spots[h, 1] = second
         return carry
 
     lax.fori_loop(0, MHEADS, head, 0)
-    gquery = gquery_ref[...]
+    halves = [contract(spots[h, half], keys_ref[half, h]) for h in range(MHEADS) for half in range(2)]
+    gquery = jnp.concatenate(halves, axis=1).astype(BF16)
+    gquery_ref[...] = gquery
     ready.send(gquery_ref)
     ready()
     for copy in copies[:4]:
@@ -1152,16 +1161,16 @@
 
     mixed, grank_five, ggate, part = call(
         fixed(memory_kernel, batches), "memory", "MLL" + "V" * batches + "HHH",
-        [("S", token_low), ("S", token_rank), ("S", token_low), ("S", token_wide)],
+        [("S", token_low), ("S", token_rank), ("S", token_low), ("V", token_wide)],
         (adapter_index, gate, mix_grad, *pieces, input_weights, down, adapter_up), [matrix, small, small, sema(3)],
     )
 
     go, gquery, grank_pair, gmid = call(
-        fixed(query_kernel, owners, rows_dev), "query", "MMVLLLLLLLLHHHH",
+        fixed(query_kernel, owners, rows_dev), "query", "MMVLLLVDDDLHHHH",
         [("V", shaped((seq, tokens, cols), BF16)), ("S", token_low), ("S", shaped((2, tokens, RANK), BF16)), ("S", token_wide)],
         (lengths, adapter_index, found_back, slot_col, picks, weights, part, middle, cot, gain_two, half_keys,
          input_weights, output_weights, down, adapter_up),
-        [pair, two_small, two_small, pltpu.VMEM((LANES, tokens), F32), sema(6)],
+        [pair, two_small, two_small, pltpu.VMEM((LANES, tokens), F32), pltpu.VMEM((MHEADS, 2, NSUB, tokens), BF16), sema(6)],
     )
     go_all = exchange(go, "seq").reshape(rows, cols)
     mixed, go = lax.optimization_barrier((mixed, go))

time: 228 us -> 226 us (level)
  transfers between devices with their start and end apart: 40 -> 40, of which waited for: 15 -> 16; matrix products, arithmetic and copies ran while one was open for 0% -> 0% of each run, Pallas kernels for 35% -> 35%
where the time goes in v3:
time: 226 us; the launch traced here: 225 us
  Pallas kernels  100 us (44%)
  starting transfers between devices  72.7 us (32%)
  waiting for transfers between devices  49.3 us (22%)
  between operations  2.49 us (1%)
    pallas_call x28, Pallas kernels, call(): pl.pallas_call(wrapped, name=name, out_shape=[pltpu.HBM(out.shape, out.dt...  100 us
    all_to_all x10, starting transfers between devices, exchange(): return lax.all_to_all(values, axes, split_axis=0, concat_axis=0, tiled=True)  37.4 us
    all_to_all x10, waiting for transfers between devices, exchange(): return lax.all_to_all(values, axes, split_axis=0, concat_axis=0, tiled=True)  33.4 us
    ppermute x18, starting transfers between devices, along(): lax.ppermute(values, axis, [(i, (i + step) % size) for i in range(size)])  23.8 us
    ppermute x18, waiting for transfers between devices, along(): lax.ppermute(values, axis, [(i, (i + step) % size) for i in range(size)])  13.7 us
    ppermute x12, starting transfers between devices, across(): return lax.ppermute(values, axis, [(i, i ^ mask) for i in range(size)])  11.4 us
  transfers between devices with their start and end apart: 40, of which 16 were waited for; matrix products, arithmetic and copies ran while one was open for 0% of the time, Pallas kernels for 35%

profile of v3, /device:TPU:0, one launch (start us, length us, event | category | flops | bytes accessed | tf_op | source)
XLA Modules:
  0.0 224.7 jit_solution(3407997348548067280)
XLA Ops:
  1.3 5.7 %qkv.1 = (bf16[8,128,384]{2,1,0:T(8,128)(2,1)}, bf16[128,1152]{1,0:T(8,128)(2,1)}) custom-call(s32[1]{0:T(128)S(6)} %copy.22.refs_0_.refs_1_, bf16[128,1024]{1,0:T(8,128)(2,1)} %bitcast.32, bf16[1024]{0:T(1024)(128)(2,1)} %refs_3_.9, bf16[5,1024,1024]{2,1,0:T(8,128)(2,1)} %refs_5_.9, bf16[7,8,16,1024]{3,2,1,0:T(8,128)(2,1)} %bitcast.23, ...), custom_call_target="tpu_custom_call" | custom-call | flops 4096 | bytes 4096 | tf_op jit(solution)/shard_map/qkv/pallas_call | solution.py:126
  7.0 5.2 %all-to-all-start = ((bf16[8,128,384]{2,1,0:T(8,128)(2,1)}), bf16[8,128,384]{2,1,0:T(8,128)(2,1)S(1)}, u32[]{:S(2)}, u32[]{:S(2)}) async-start(bf16[8,128,384]{2,1,0:T(8,128)(2,1)} %get-tuple-element.109), calls=%async_computation | async-start | bytes 1572864 | tf_op jit(solution)/shard_map/all_to_all | solution.py:1033
  20.3 3.3 %mixback.1 = (bf16[128,1024]{1,0:T(8,128)(2,1)}, bf16[128,16]{1,0:T(8,128)(2,1)}) custom-call(s32[1]{0:T(128)S(6)} %copy.22.refs_0_.refs_1_, bf16[128,1024]{1,0:T(8,128)(2,1)} %bitcast.35, bf16[2,1024,1024]{2,1,0:T(8,128)(2,1)} %refs_3_.8, bf16[7,8,16,1024]{3,2,1,0:T(8,128)(2,1)} %bitcast.24, bf16[7,8,16,1024]{3,2,1,0:T(8,128)(2,1)} %refs_7_.7), custom_call_target="tpu_custom_call" | custom-call | flops 4096 | bytes 4096 | tf_op jit(solution)/shard_map/mixback/pallas_call | solution.py:126
  24.7 5.0 %attend.1 = (bf16[8,192,128]{2,1,0:T(8,128)(2,1)}, f32[8,1024]{1,0:T(8,128)}, s32[4,8,128]{2,1,0:T(8,128)}, bf16[1024,384]{1,0:T(8,128)(2,1)}) custom-call(s32[1]{0:T(128)S(6)} %copy.21.refs_0_, bf16[1024,384]{1,0:T(8,128)(2,1)S(1)} %bitcast.19, s32[72,128]{1,0:T(8,128)S(1)} %get-tuple-element.116.refs_2_, s32[72,128]{1,0:T(8,128)S(1)} %collective-permute-done.refs_3_, ...), custom_call_target="tpu_custom_call" | custom-call | flops 4096 | bytes 4096 | tf_op jit(solution)/shard_map/attend/pallas_call | solution.py:126
  29.8 3.8 %all-to-all-start.1 = ((bf16[8,192,128]{2,1,0:T(8,128)(2,1)}), bf16[8,192,128]{2,1,0:T(8,128)(2,1)S(1)}, u32[]{:S(2)}, u32[]{:S(2)}) async-start(bf16[8,192,128]{2,1,0:T(8,128)(2,1)} %get-tuple-element.120), calls=%async_computation.1 | async-start | bytes 786432 | tf_op jit(solution)/shard_map/all_to_all | solution.py:1033
  37.2 5.3 %all-to-all-done.1.refs_1_ = bf16[8,192,128]{2,1,0:T(8,128)(2,1)S(1)} async-done(((bf16[8,192,128]{2,1,0:T(8,128)(2,1)}), bf16[8,192,128]{2,1,0:T(8,128)(2,1)S(1)}, u32[]{:S(2)}, u32[]{:S(2)}) %all-to-all-start.1) | async-done | bytes 393248 | tf_op jit(solution)/shard_map/all_to_all | solution.py:1033
  42.5 4.8 %middle.1 = (bf16[128,512]{1,0:T(8,128)(2,1)S(1)}, bf16[128,512]{1,0:T(8,128)(2,1)S(1)}, bf16[128,1024]{1,0:T(8,128)(2,1)S(1)}, bf16[1024,1024]{1,0:T(8,128)(2,1...) custom-call(s32[1]{0:T(128)S(6)} %copy.22.refs_0_.refs_1_, ...), custom_call_target="tpu_custom_call" | custom-call | flops 4096 | bytes 4096 | tf_op jit(solution)/shard_map/middle/pallas_call | solution.py:126
  47.2 3.2 %collective-permute-start.5 = (bf16[128,512]{1,0:T(8,128)(2,1)S(1)}, bf16[128,512]{1,0:T(8,128)(2,1)S(1)}, u32[]{:S(2)}, u32[]{:S(2)}) collective-permute-start(bf16[128,512]{1,0:T(8,128)(2,1)S(1)} %get-tuple-element.139.refs_1_), channel_id=1, source_target_pairs={{0,24},{8,0},{16,8},{24,16},{1,25},{9,1},{17,9},{25,17},{2,26},{10... | collective-permute-start | bytes 393224 | tf_op jit(solution)/shard_map/ppermute | solution.py:1016
  51.5 4.2 %scores.1 = (bf16[256,128]{1,0:T(8,128)(2,1)}, bf16[128,16]{1,0:T(8,128)(2,1)}, f32[128,128]{1,0:T(8,128)}) custom-call(s32[1]{0:T(128)S(6)} %copy.22.refs_0_.refs_1_, bf16[128,1024]{1,0:T(8,128)(2,1)S(1)} %get-tuple-element.128.refs_1_, bf16[1024,1024]{1,0:T(8,128)(2,1)S(1)} %get-tuple-element.129.refs_2_, s32[128,128]{1,0:T(8,128)} %get-tuple-element.130.refs_3_, ...), custom_call_target="tpu_custom_call" | custom-call | flops 4096 | bytes 4096 | tf_op jit(solution)/shard_map/scores/pallas_call | solution.py:126
  55.7 3.6 %all-to-all-start.2 = ((bf16[32,8,128]{2,1,0:T(8,128)(2,1)}), bf16[32,8,128]{2,1,0:T(8,128)(2,1)S(1)}, u32[]{:S(2)}, u32[]{:S(2)}) async-start(bf16[32,8,128]{2,1,0:T(8,128)(2,1)} %bitcast.6), calls=%async_computation.2 | async-start | bytes 131072 | tf_op jit(solution)/shard_map/all_to_all | solution.py:1033
  63.7 3.0 %all-to-all-done.2 = bf16[32,8,128]{2,1,0:T(8,128)(2,1)S(1)} async-done(((bf16[32,8,128]{2,1,0:T(8,128)(2,1)}), bf16[32,8,128]{2,1,0:T(8,128)(2,1)S(1)}, u32[]{:S(2)}, u32[]{:S(2)}) %all-to-all-start.2) | async-done | bytes 65568 | tf_op jit(solution)/shard_map/all_to_all | solution.py:1033
  66.7 3.7 %all-to-all-start.3 = ((bf16[8,4,32,512]{3,2,1,0:T(8,128)(2,1)}), bf16[8,4,32,512]{3,2,1,0:T(8,128)(2,1)S(1)}, u32[]{:S(2)}, u32[]{:S(2)}) async-start(bf16[8,4,32,512]{3,2,1,0:T(8,128)(2,1)} %scatterleft.1), calls=%async_computation.3 | async-start | bytes 2097152 | tf_op jit(solution)/shard_map/all_to_all | solution.py:1033
  70.5 5.8 %prepare.1 = (s32[256,128]{1,0:T(8,128)}, s16[1024,2048]{1,0:T(8,128)(2,1)}) custom-call(bf16[8,64,128]{2,1,0:T(8,128)(2,1)} %get-tuple-element.156.refs_0_), custom_call_target="tpu_custom_call" | custom-call | flops 4096 | bytes 4096 | tf_op jit(solution)/shard_map/prepare/pallas_call | solution.py:126
  76.3 9.2 %recall.1 = bf16[8,4,32,1024]{3,2,1,0:T(8,128)(2,1)} custom-call(bf16[256,128]{1,0:T(8,128)(2,1)S(1)} %bitcast.22, s16[1024,2048]{1,0:T(8,128)(2,1)} %get-tuple-element.157.refs_1_, bf16[2048,1024]{1,0:T(8,128)(2,1)} %refs_3_.7), custom_call_target="tpu_custom_call" | custom-call | flops 4096 | bytes 4096 | tf_op jit(solution)/shard_map/recall/pallas_call | solution.py:126
  85.6 3.8 %all-to-all-start.4 = ((bf16[8,4,32,1024]{3,2,1,0:T(8,128)(2,1)}), bf16[8,4,32,1024]{3,2,1,0:T(8,128)(2,1)S(1)}, u32[]{:S(2)}, u32[]{:S(2)}) async-start(bf16[8,4,32,1024]{3,2,1,0:T(8,128)(2,1)} %recall.1), calls=%async_computation.4 | async-start | bytes 4194304 | tf_op jit(solution)/shard_map/all_to_all | solution.py:1033
  92.7 6.1 %recallleft.1.refs_1_ = f32[256,128]{1,0:T(8,128)} custom-call(s32[256,128]{1,0:T(8,128)} %get-tuple-element.160.refs_0_, bf16[1024,512]{1,0:T(8,128)(2,1)S(1)} %bitcast.17, bf16[2048,1024]{1,0:T(8,128)(2,1)} %refs_3_.7), custom_call_target="tpu_custom_call" | custom-call | flops 4096 | bytes 4096 | tf_op jit(solution)/shard_map/recallleft/pallas_call | solution.py:126
  98.8 5.0 %collective-permute-done.7.refs_3_ = bf16[128,512]{1,0:T(8,128)(2,1)S(1)} collective-permute-done((bf16[128,512]{1,0:T(8,128)(2,1)S(1)}, bf16[128,512]{1,0:T(8,128)(2,1)S(1)}, u32[]{:S(2)}, u32[]{:S(2)}) %collective-permute-start.7) | collective-permute-done | bytes 131104 | tf_op jit(solution)/shard_map/ppermute | solution.py:1016
  106.0 10.1 %all-to-all-done.4.refs_1_ = bf16[8,4,32,1024]{3,2,1,0:T(8,128)(2,1)S(1)} async-done(((bf16[8,4,32,1024]{3,2,1,0:T(8,128)(2,1)}), bf16[8,4,32,1024]{3,2,1,0:T(8,128)(2,1)S(1)}, u32[]{:S(2)}, u32[]{:S(2)}) %all-to-all-start.4) | async-done | bytes 2097184 | tf_op jit(solution)/shard_map/all_to_all | solution.py:1033
  116.1 3.6 %all-to-all-start.5 = ((bf16[8,4,32,512]{3,2,1,0:T(8,128)(2,1)}), bf16[8,4,32,512]{3,2,1,0:T(8,128)(2,1)S(1)}, u32[]{:S(2)}, u32[]{:S(2)}) async-start(bf16[8,4,32,512]{3,2,1,0:T(8,128)(2,1)} %scatterright.1), calls=%async_computation.5 | async-start | bytes 2097152 | tf_op jit(solution)/shard_map/all_to_all | solution.py:1033
  124.4 10.6 %all-to-all-done.5 = bf16[8,4,32,512]{3,2,1,0:T(8,128)(2,1)S(1)} async-done(((bf16[8,4,32,512]{3,2,1,0:T(8,128)(2,1)}), bf16[8,4,32,512]{3,2,1,0:T(8,128)(2,1)S(1)}, u32[]{:S(2)}, u32[]{:S(2)}) %all-to-all-start.5) | async-done | bytes 1048608 | tf_op jit(solution)/shard_map/all_to_all | solution.py:1033
  135.0 6.2 %recallright.1 = bf16[256,128]{1,0:T(8,128)(2,1)} custom-call(s32[256,128]{1,0:T(8,128)} %get-tuple-element.160.refs_0_, f32[256,128]{1,0:T(8,128)} %recallleft.1.refs_1_, bf16[1024,512]{1,0:T(8,128)(2,1)S(1)} %bitcast.18, bf16[2048,1024]{1,0:T(8,128)(2,1)} %refs_3_.7), custom_call_target="tpu_custom_call" | custom-call | flops 4096 | bytes 4096 | tf_op jit(solution)/shard_map/recallright/pallas_call | solution.py:126
  143.8 3.8 %collective-permute-done.14.refs_5_ = bf16[128,1024]{1,0:T(8,128)(2,1)S(1)} collective-permute-done((bf16[128,1024]{1,0:T(8,128)(2,1)}, bf16[128,1024]{1,0:T(8,128)(2,1)S(1)}, u32[]{:S(2)}, u32[]{:S(2)}) %collective-permute-start.14) | collective-permute-done | bytes 262176 | tf_op jit(solution)/shard_map/ppermute | solution.py:1016
  151.2 8.0 %query.1 = (bf16[8,128,128]{2,1,0:T(8,128)(2,1)}, bf16[128,1024]{1,0:T(8,128)(2,1)}, bf16[2,128,16]{2,1,0:T(8,128)(2,1)}, f32[128,1024]{1,0:T(8,128)}) custom-call(s32[1]{0:T(128)S(6)} %copy.21.refs_0_, s32[1]{0:T(128)S(6)} %copy.22.refs_0_.refs_1_, bf16[256,128]{1,0:T(8,128)(2,1)S(1)} %bitcast.21, s32[128,128]{1,0:T(8,128)} %get-tuple-element.170.refs_3_, ...), custom_call_target="tpu_custom_call" | custom-call | flops 4096 | bytes 4096 | tf_op jit(solution)/shard_map/query/pallas_call | solution.py:126
  159.2 3.6 %all-to-all-start.7 = ((bf16[8,128,128]{2,1,0:T(8,128)(2,1)}), bf16[8,128,128]{2,1,0:T(8,128)(2,1)S(1)}, u32[]{:S(2)}, u32[]{:S(2)}) async-start(bf16[8,128,128]{2,1,0:T(8,128)(2,1)} %get-tuple-element.174), calls=%async_computation.7 | async-start | bytes 524288 | tf_op jit(solution)/shard_map/all_to_all | solution.py:1033
  162.8 3.2 %output.1 = (bf16[128,1024]{1,0:T(8,128)(2,1)}, bf16[128,16]{1,0:T(8,128)(2,1)}) custom-call(s32[1]{0:T(128)S(6)} %copy.22.refs_0_.refs_1_, bf16[128,1024]{1,0:T(8,128)(2,1)} %get-tuple-element.175.refs_1_.refs_2_, f32[128,1024]{1,0:T(8,128)} %get-tuple-element.173.refs_7_.refs_2_, bf16[2,1024,1024]{2,1,0:T(8,128)(2,1)} %refs_3_.8, ...), custom_call_target="tpu_custom_call" | custom-call | flops 4096 | bytes 4096 | tf_op jit(solution)/shard_map/output/pallas_call | solution.py:126
  169.5 3.4 %all-to-all-start.8 = ((bf16[8,128,128]{2,1,0:T(8,128)(2,1)}), bf16[8,128,128]{2,1,0:T(8,128)(2,1)S(1)}, u32[]{:S(2)}, u32[]{:S(2)}) async-start(bf16[8,128,128]{2,1,0:T(8,128)(2,1)} %factors.1), calls=%async_computation.8 | async-start | bytes 524288 | tf_op jit(solution)/shard_map/all_to_all | solution.py:1033
  172.9 10.1 %attendback.1 = (bf16[8,144,384]{2,1,0:T(8,128)(2,1)}, bf16[48,128]{1,0:T(8,128)(2,1)}) custom-call(s32[1]{0:T(128)S(6)} %copy.21.refs_0_, s32[1]{0:T(128)S(6)} %copy.22.refs_0_.refs_1_, bf16[1024,384]{1,0:T(8,128)(2,1)} %get-tuple-element.177.refs_2_, bf16[1024,128]{1,0:T(8,128)(2,1)S(1)} %bitcast.20, f32[8,1024]{1,0:T(8,128)} %get-tuple-element.190.refs_4_, ...), custom_call_target="tpu_custom_call" | custom-call | flops 4096 | bytes 4096 | tf_op jit(solution)/shard_map/attendback/pallas_call | solution.py:126
  183.0 4.1 %all-to-all-start.9 = ((bf16[8,144,384]{2,1,0:T(8,128)(2,1)}), bf16[8,144,384]{2,1,0:T(8,128)(2,1)S(1)}, u32[]{:S(2)}, u32[]{:S(2)}) async-start(bf16[8,144,384]{2,1,0:T(8,128)(2,1)} %get-tuple-element.195), calls=%async_computation.9 | async-start | bytes 1769472 | tf_op jit(solution)/shard_map/all_to_all | solution.py:1033
  191.5 3.2 %collective-permute-done.20.refs_2_ = bf16[128,128]{1,0:T(8,128)(2,1)S(1)} collective-permute-done((bf16[128,128]{1,0:T(8,128)(2,1)S(1)}, bf16[128,128]{1,0:T(8,128)(2,1)S(1)}, u32[]{:S(2)}, u32[]{:S(2)}) %collective-permute-start.20) | collective-permute-done | bytes 32800 | tf_op jit(solution)/shard_map/ppermute | solution.py:1016
  206.5 5.3 %entry.1 = bf16[128,1024]{1,0:T(8,128)(2,1)} custom-call(s32[1]{0:T(128)S(6)} %copy.22.refs_0_.refs_1_, bf16[8,144,384]{2,1,0:T(8,128)(2,1)S(1)} %all-to-all-done.9.refs_0_.refs_1_, bf16[128,1024]{1,0:T(8,128)(2,1)} %bitcast.34, bf16[1024]{0:T(1024)(128)(2,1)} %refs_3_.9, f32[128,1024]{1,0:T(8,128)} %get-tuple-element.180.refs_3_.refs_4_, ...), custom_call_target="tpu_custom_call" | custom-call | flops 4096 | bytes 4096 | tf_op jit(solution)/shard_map/entry/pallas_call | solution.py:126
  215.5 3.7 %spread.1 = (f32[7,8,16,1024]{3,2,1,0:T(8,128)}, f32[7,8,16,1024]{3,2,1,0:T(8,128)}) custom-call(s32[256,128]{1,0:T(8,128)} %get-tuple-element.160.refs_0_, bf16[4,4,128,128]{3,2,1,0:T(8,128)(2,1)S(1)} %pairsearly.1.refs_1_, bf16[4,4,128,128]{3,2,1,0:T(8,128)(2,1)S(1)} %collective-permute-done.28.refs_2_), custom_call_target="tpu_custom_call" | custom-call | flops 4096 | bytes 4096 | tf_op jit(solution)/shard_map/spread/pallas_call | solution.py:126
  221.5 3.0 %lastspread.1 = (f32[7,8,16,1024]{3,2,1,0:T(8,128)}, f32[7,8,16,1024]{3,2,1,0:T(8,128)}) custom-call(s32[256,128]{1,0:T(8,128)} %get-tuple-element.160.refs_0_, f32[7,8,16,1024]{3,2,1,0:T(8,128)} %get-tuple-element.206.refs_1_, f32[7,8,16,1024]{3,2,1,0:T(8,128)} %get-tuple-element.207.refs_2_, ...), custom_call_target="tpu_custom_call", output_to_operand_aliasing={{0}: (1, {}), {1}: (2, {})} | custom-call | flops 4096 | bytes 4096 | tf_op jit(solution)/shard_map/lastspread/pallas_call | solution.py:126
  (78 shorter events, 59.3 us)
Async XLA Ops:
  7.0 17.8 %all-to-all-start = ((bf16[8,128,384]{2,1,0:T(8,128)(2,1)}), bf16[8,128,384]{2,1,0:T(8,128)(2,1)S(1)}, u32[]{:S(2)}, u32[]{:S(2)}) async-start(bf16[8,128,384]{2,1,0:T(8,128)(2,1)} %get-tuple-element.109), calls=%async_computation | async-start | bytes 1572864 | tf_op jit(solution)/shard_map/all_to_all | solution.py:1033
  14.8 9.6 %collective-permute-start = (s32[72,128]{1,0:T(8,128)S(1)}, s32[72,128]{1,0:T(8,128)S(1)}, u32[]{:S(2)}, u32[]{:S(2)}) collective-permute-start(s32[72,128]{1,0:T(8,128)S(1)} %get-tuple-element.111), channel_id=1, source_target_pairs={{0,8},{8,16},{16,24},{24,0},{1,9},{9,17},{17,25},{25,1},{2,10},{10... | collective-permute-start | bytes 110600 | tf_op jit(solution)/shard_map/ppermute | solution.py:1016
  16.4 7.9 %collective-permute-start.1 = (s32[72,128]{1,0:T(8,128)S(1)}, s32[72,128]{1,0:T(8,128)S(1)}, u32[]{:S(2)}, u32[]{:S(2)}) collective-permute-start(s32[72,128]{1,0:T(8,128)S(1)} %get-tuple-element.112), channel_id=1, source_target_pairs={{0,16},{8,24},{16,0},{24,8},{1,17},{9,25},{17,1},{25,9},{2,18},{10... | collective-permute-start | bytes 110600 | tf_op jit(solution)/shard_map/ppermute | solution.py:1016
  29.8 12.7 %all-to-all-start.1 = ((bf16[8,192,128]{2,1,0:T(8,128)(2,1)}), bf16[8,192,128]{2,1,0:T(8,128)(2,1)S(1)}, u32[]{:S(2)}, u32[]{:S(2)}) async-start(bf16[8,192,128]{2,1,0:T(8,128)(2,1)} %get-tuple-element.120), calls=%async_computation.1 | async-start | bytes 786432 | tf_op jit(solution)/shard_map/all_to_all | solution.py:1033
  33.6 16.9 %collective-permute-start.11 = (bf16[128,1152]{1,0:T(8,128)(2,1)S(1)}, bf16[128,1152]{1,0:T(8,128)(2,1)S(1)}, u32[]{:S(2)}, u32[]{:S(2)}) collective-permute-start(bf16[128,1152]{1,0:T(8,128)(2,1)S(1)} %copy-done), channel_id=1, source_target_pairs={{0,6},{1,7},{2,4},{3,5},{4,2},{5,3},{6,0},{7,1},{8,14},{9,15},{10,... | collective-permute-start | bytes 884744 | tf_op jit(solution)/shard_map/ppermute | solution.py:1020
  36.5 19.2 %collective-permute-start.10 = (bf16[128,1152]{1,0:T(8,128)(2,1)S(1)}, bf16[128,1152]{1,0:T(8,128)(2,1)S(1)}, u32[]{:S(2)}, u32[]{:S(2)}) collective-permute-start(bf16[128,1152]{1,0:T(8,128)(2,1)S(1)} %copy-done), channel_id=1, source_target_pairs={{0,4},{1,5},{2,6},{3,7},{4,0},{5,1},{6,2},{7,3},{8,12},{9,13},{10,... | collective-permute-start | bytes 884744 | tf_op jit(solution)/shard_map/ppermute | solution.py:1020
  37.1 18.6 %collective-permute-start.9 = (bf16[128,1152]{1,0:T(8,128)(2,1)S(1)}, bf16[128,1152]{1,0:T(8,128)(2,1)S(1)}, u32[]{:S(2)}, u32[]{:S(2)}) collective-permute-start(bf16[128,1152]{1,0:T(8,128)(2,1)S(1)} %copy-done), channel_id=1, source_target_pairs={{0,2},{1,3},{2,0},{3,1},{4,6},{5,7},{6,4},{7,5},{8,10},{9,11},{10,... | collective-permute-start | bytes 884744 | tf_op jit(solution)/shard_map/ppermute | solution.py:1020
  47.2 12.1 %collective-permute-start.5 = (bf16[128,512]{1,0:T(8,128)(2,1)S(1)}, bf16[128,512]{1,0:T(8,128)(2,1)S(1)}, u32[]{:S(2)}, u32[]{:S(2)}) collective-permute-start(bf16[128,512]{1,0:T(8,128)(2,1)S(1)} %get-tuple-element.139.refs_1_), channel_id=1, source_target_pairs={{0,24},{8,0},{16,8},{24,16},{1,25},{9,1},{17,9},{25,17},{2,26},{10... | collective-permute-start | bytes 393224 | tf_op jit(solution)/shard_map/ppermute | solution.py:1016
  50.5 9.9 %collective-permute-start.4 = (bf16[128,512]{1,0:T(8,128)(2,1)S(1)}, bf16[128,512]{1,0:T(8,128)(2,1)S(1)}, u32[]{:S(2)}, u32[]{:S(2)}) collective-permute-start(bf16[128,512]{1,0:T(8,128)(2,1)S(1)} %get-tuple-element.139.refs_1_), channel_id=1, source_target_pairs={{0,16},{8,24},{16,0},{24,8},{1,17},{9,25},{17,1},{25,9},{2,18},{10... | collective-permute-start | bytes 393224 | tf_op jit(solution)/shard_map/ppermute | solution.py:1016
  50.5 9.9 %collective-permute-start.3 = (bf16[128,512]{1,0:T(8,128)(2,1)S(1)}, bf16[128,512]{1,0:T(8,128)(2,1)S(1)}, u32[]{:S(2)}, u32[]{:S(2)}) collective-permute-start(bf16[128,512]{1,0:T(8,128)(2,1)S(1)} %get-tuple-element.139.refs_1_), channel_id=1, source_target_pairs={{0,8},{8,16},{16,24},{24,0},{1,9},{9,17},{17,25},{25,1},{2,10},{10... | collective-permute-start | bytes 393224 | tf_op jit(solution)/shard_map/ppermute | solution.py:1016
  55.7 11.0 %all-to-all-start.2 = ((bf16[32,8,128]{2,1,0:T(8,128)(2,1)}), bf16[32,8,128]{2,1,0:T(8,128)(2,1)S(1)}, u32[]{:S(2)}, u32[]{:S(2)}) async-start(bf16[32,8,128]{2,1,0:T(8,128)(2,1)} %bitcast.6), calls=%async_computation.2 | async-start | bytes 131072 | tf_op jit(solution)/shard_map/all_to_all | solution.py:1033
  66.7 18.9 %all-to-all-start.3 = ((bf16[8,4,32,512]{3,2,1,0:T(8,128)(2,1)}), bf16[8,4,32,512]{3,2,1,0:T(8,128)(2,1)S(1)}, u32[]{:S(2)}, u32[]{:S(2)}) async-start(bf16[8,4,32,512]{3,2,1,0:T(8,128)(2,1)} %scatterleft.1), calls=%async_computation.3 | async-start | bytes 2097152 | tf_op jit(solution)/shard_map/all_to_all | solution.py:1033
  85.6 30.5 %all-to-all-start.4 = ((bf16[8,4,32,1024]{3,2,1,0:T(8,128)(2,1)}), bf16[8,4,32,1024]{3,2,1,0:T(8,128)(2,1)S(1)}, u32[]{:S(2)}, u32[]{:S(2)}) async-start(bf16[8,4,32,1024]{3,2,1,0:T(8,128)(2,1)} %recall.1), calls=%async_computation.4 | async-start | bytes 4194304 | tf_op jit(solution)/shard_map/all_to_all | solution.py:1033
  89.4 14.4 %collective-permute-start.12 = (bf16[4,128,1152]{2,1,0:T(8,128)(2,1)}, bf16[4,128,1152]{2,1,0:T(8,128)(2,1)}, u32[]{:S(2)}, u32[]{:S(2)}) collective-permute-start(bf16[4,128,1152]{2,1,0:T(8,128)(2,1)} %pairsnorm.1.refs_5_), channel_id=1, source_target_pairs={{0,1},{1,0},{2,3},{3,2},{4,5},{5,4},{6,7},{7,6},{8,9},{9,8},{10,11... | collective-permute-start | bytes 3538952 | tf_op jit(solution)/shard_map/ppermute | solution.py:1020
  90.0 8.9 %collective-permute-start.8 = (bf16[128,512]{1,0:T(8,128)(2,1)S(1)}, bf16[128,512]{1,0:T(8,128)(2,1)S(1)}, u32[]{:S(2)}, u32[]{:S(2)}) collective-permute-start(bf16[128,512]{1,0:T(8,128)(2,1)S(1)} %get-tuple-element.151.refs_1_), channel_id=1, source_target_pairs={{0,24},{8,0},{16,8},{24,16},{1,25},{9,1},{17,9},{25,17},{2,26},{10... | collective-permute-start | bytes 393224 | tf_op jit(solution)/shard_map/ppermute | solution.py:1016
  90.9 13.0 %collective-permute-start.7 = (bf16[128,512]{1,0:T(8,128)(2,1)S(1)}, bf16[128,512]{1,0:T(8,128)(2,1)S(1)}, u32[]{:S(2)}, u32[]{:S(2)}) collective-permute-start(bf16[128,512]{1,0:T(8,128)(2,1)S(1)} %get-tuple-element.151.refs_1_), channel_id=1, source_target_pairs={{0,16},{8,24},{16,0},{24,8},{1,17},{9,25},{17,1},{25,9},{2,18},{10... | collective-permute-start | bytes 393224 | tf_op jit(solution)/shard_map/ppermute | solution.py:1016
  92.0 11.8 %collective-permute-start.6 = (bf16[128,512]{1,0:T(8,128)(2,1)S(1)}, bf16[128,512]{1,0:T(8,128)(2,1)S(1)}, u32[]{:S(2)}, u32[]{:S(2)}) collective-permute-start(bf16[128,512]{1,0:T(8,128)(2,1)S(1)} %get-tuple-element.151.refs_1_), channel_id=1, source_target_pairs={{0,8},{8,16},{16,24},{24,0},{1,9},{9,17},{17,25},{25,1},{2,10},{10... | collective-permute-start | bytes 393224 | tf_op jit(solution)/shard_map/ppermute | solution.py:1016
  116.1 18.9 %all-to-all-start.5 = ((bf16[8,4,32,512]{3,2,1,0:T(8,128)(2,1)}), bf16[8,4,32,512]{3,2,1,0:T(8,128)(2,1)S(1)}, u32[]{:S(2)}, u32[]{:S(2)}) async-start(bf16[8,4,32,512]{3,2,1,0:T(8,128)(2,1)} %scatterright.1), calls=%async_computation.5 | async-start | bytes 2097152 | tf_op jit(solution)/shard_map/all_to_all | solution.py:1033
  121.7 22.1 %collective-permute-start.13 = (bf16[128,1024]{1,0:T(8,128)(2,1)}, bf16[128,1024]{1,0:T(8,128)(2,1)S(1)}, u32[]{:S(2)}, u32[]{:S(2)}) collective-permute-start(bf16[128,1024]{1,0:T(8,128)(2,1)} %get-tuple-element.164), channel_id=1, source_target_pairs={{0,24},{8,0},{16,8},{24,16},{1,25},{9,1},{17,9},{25,17},{2,26},{10... | collective-permute-start | bytes 786440 | tf_op jit(solution)/shard_map/ppermute | solution.py:1016
  122.6 24.9 %collective-permute-start.14 = (bf16[128,1024]{1,0:T(8,128)(2,1)}, bf16[128,1024]{1,0:T(8,128)(2,1)S(1)}, u32[]{:S(2)}, u32[]{:S(2)}) collective-permute-start(bf16[128,1024]{1,0:T(8,128)(2,1)} %get-tuple-element.165), channel_id=1, source_target_pairs={{0,16},{8,24},{16,0},{24,8},{1,17},{9,25},{17,1},{25,9},{2,18},{10... | collective-permute-start | bytes 786440 | tf_op jit(solution)/shard_map/ppermute | solution.py:1016
  123.8 23.8 %collective-permute-start.15 = (bf16[128,1024]{1,0:T(8,128)(2,1)}, bf16[128,1024]{1,0:T(8,128)(2,1)S(1)}, u32[]{:S(2)}, u32[]{:S(2)}) collective-permute-start(bf16[128,1024]{1,0:T(8,128)(2,1)} %get-tuple-element.166), channel_id=1, source_target_pairs={{0,8},{8,16},{16,24},{24,0},{1,9},{9,17},{17,25},{25,1},{2,10},{10... | collective-permute-start | bytes 786440 | tf_op jit(solution)/shard_map/ppermute | solution.py:1016
  141.2 10.0 %all-to-all-start.6 = ((bf16[32,8,128]{2,1,0:T(8,128)(2,1)}), bf16[32,8,128]{2,1,0:T(8,128)(2,1)S(1)}, u32[]{:S(2)}, u32[]{:S(2)}) async-start(bf16[32,8,128]{2,1,0:T(8,128)(2,1)} %bitcast.10), calls=%async_computation.6 | async-start | bytes 131072 | tf_op jit(solution)/shard_map/all_to_all | solution.py:1033
  159.2 10.3 %all-to-all-start.7 = ((bf16[8,128,128]{2,1,0:T(8,128)(2,1)}), bf16[8,128,128]{2,1,0:T(8,128)(2,1)S(1)}, u32[]{:S(2)}, u32[]{:S(2)}) async-start(bf16[8,128,128]{2,1,0:T(8,128)(2,1)} %get-tuple-element.174), calls=%async_computation.7 | async-start | bytes 524288 | tf_op jit(solution)/shard_map/all_to_all | solution.py:1033
  169.5 13.5 %all-to-all-start.8 = ((bf16[8,128,128]{2,1,0:T(8,128)(2,1)}), bf16[8,128,128]{2,1,0:T(8,128)(2,1)S(1)}, u32[]{:S(2)}, u32[]{:S(2)}) async-start(bf16[8,128,128]{2,1,0:T(8,128)(2,1)} %factors.1), calls=%async_computation.8 | async-start | bytes 524288 | tf_op jit(solution)/shard_map/all_to_all | solution.py:1033
  183.0 18.4 %all-to-all-start.9 = ((bf16[8,144,384]{2,1,0:T(8,128)(2,1)}), bf16[8,144,384]{2,1,0:T(8,128)(2,1)S(1)}, u32[]{:S(2)}, u32[]{:S(2)}) async-start(bf16[8,144,384]{2,1,0:T(8,128)(2,1)} %get-tuple-element.195), calls=%async_computation.9 | async-start | bytes 1769472 | tf_op jit(solution)/shard_map/all_to_all | solution.py:1033
  195.3 9.2 %collective-permute-start.24 = (bf16[4,128,128]{2,1,0:T(8,128)(2,1)S(1)}, bf16[4,128,128]{2,1,0:T(8,128)(2,1)S(1)}, u32[]{:S(2)}, u32[]{:S(2)}) collective-permute-start(bf16[4,128,128]{2,1,0:T(8,128)(2,1)S(1)} %stackearly.1.refs_0_), channel_id=1, source_target_pairs={{0,6},{1,7},{2,4},{3,5},{4,2},{5,3},{6,0},{7,1},{8,14},{9,15},{10,... | collective-permute-start | bytes 393224 | tf_op jit(solution)/shard_map/ppermute | solution.py:1020
  198.3 8.2 %collective-permute-start.23 = (bf16[4,128,128]{2,1,0:T(8,128)(2,1)S(1)}, bf16[4,128,128]{2,1,0:T(8,128)(2,1)S(1)}, u32[]{:S(2)}, u32[]{:S(2)}) collective-permute-start(bf16[4,128,128]{2,1,0:T(8,128)(2,1)S(1)} %stackearly.1.refs_0_), channel_id=1, source_target_pairs={{0,4},{1,5},{2,6},{3,7},{4,0},{5,1},{6,2},{7,3},{8,12},{9,13},{10,... | collective-permute-start | bytes 393224 | tf_op jit(solution)/shard_map/ppermute | solution.py:1020
  198.9 7.6 %collective-permute-start.22 = (bf16[4,128,128]{2,1,0:T(8,128)(2,1)S(1)}, bf16[4,128,128]{2,1,0:T(8,128)(2,1)S(1)}, u32[]{:S(2)}, u32[]{:S(2)}) collective-permute-start(bf16[4,128,128]{2,1,0:T(8,128)(2,1)S(1)} %stackearly.1.refs_0_), channel_id=1, source_target_pairs={{0,2},{1,3},{2,0},{3,1},{4,6},{5,7},{6,4},{7,5},{8,10},{9,11},{10,... | collective-permute-start | bytes 393224 | tf_op jit(solution)/shard_map/ppermute | solution.py:1020
  202.1 9.7 %collective-permute-start.18 = (bf16[96,128]{1,0:T(8,128)(2,1)S(1)}, bf16[96,128]{1,0:T(8,128)(2,1)S(1)}, u32[]{:S(2)}, u32[]{:S(2)}) collective-permute-start(bf16[96,128]{1,0:T(8,128)(2,1)S(1)} %late.1.refs_0_), channel_id=1, source_target_pairs={{0,24},{8,0},{16,8},{24,16},{1,25},{9,1},{17,9},{25,17},{2,26},{10... | collective-permute-start | bytes 73736 | tf_op jit(solution)/shard_map/ppermute | solution.py:1016
  204.5 7.4 %collective-permute-start.17 = (bf16[96,128]{1,0:T(8,128)(2,1)S(1)}, bf16[96,128]{1,0:T(8,128)(2,1)S(1)}, u32[]{:S(2)}, u32[]{:S(2)}) collective-permute-start(bf16[96,128]{1,0:T(8,128)(2,1)S(1)} %late.1.refs_0_), channel_id=1, source_target_pairs={{0,16},{8,24},{16,0},{24,8},{1,17},{9,25},{17,1},{25,9},{2,18},{10... | collective-permute-start | bytes 73736 | tf_op jit(solution)/shard_map/ppermute | solution.py:1016
  204.5 7.4 %collective-permute-start.16 = (bf16[96,128]{1,0:T(8,128)(2,1)S(1)}, bf16[96,128]{1,0:T(8,128)(2,1)S(1)}, u32[]{:S(2)}, u32[]{:S(2)}) collective-permute-start(bf16[96,128]{1,0:T(8,128)(2,1)S(1)} %late.1.refs_0_), channel_id=1, source_target_pairs={{0,8},{8,16},{16,24},{24,0},{1,9},{9,17},{17,25},{25,1},{2,10},{10... | collective-permute-start | bytes 73736 | tf_op jit(solution)/shard_map/ppermute | solution.py:1016
  212.0 7.3 %collective-permute-start.27 = (bf16[4,96,128]{2,1,0:T(8,128)(2,1)S(1)}, bf16[4,96,128]{2,1,0:T(8,128)(2,1)S(1)}, u32[]{:S(2)}, u32[]{:S(2)}) collective-permute-start(bf16[4,96,128]{2,1,0:T(8,128)(2,1)S(1)} %stacklate.1.refs_0_), channel_id=1, source_target_pairs={{0,6},{1,7},{2,4},{3,5},{4,2},{5,3},{6,0},{7,1},{8,14},{9,15},{10,... | collective-permute-start | bytes 294920 | tf_op jit(solution)/shard_map/ppermute | solution.py:1020
  (9 other events, 51.9 us)

commit v4 on v3

--- a/solution.py
+++ b/solution.py
@@ -171,10 +171,13 @@
     copies = fetch(
         [(dn_any.at[j, a], dn.at[pl.ds(RANK * j, RANK)]) for j in range(3)]
         + [(up_any.at[j, a], up.at[pl.ds(RANK * j, RANK)]) for j in range(3)]
-        + [(w_any.at[j], w.at[j]) for j in range(3)],
+        + [(w_any.at[0], w.at[0])],
         sems,
     )
-    ready()
+    copies += [pltpu.make_async_copy(w_any.at[j], w.at[j], sems.at[6 + j]) for j in (1, 2)]
+    ready()
+    copies[7].start()
+    copies[8].start()
     x = x_ref[...].astype(F32)
     normed = (x * inverse_norm(x) * gain_row(gain_ref)).astype(BF16)
     width = normed.shape[1]
@@ -411,7 +414,8 @@
     copies[0].wait()
 
     def whole(b, outer):
-        scores[...] = against(grad_ref[pl.ds(pl.multiple_of(b * block, block), block), :], mem[...])
+        scores[...] = against(grad_ref[pl.ds(pl.multiple_of(b * block, block), block), :], mem[...]).astype(BF16)
+        step = min(2, groups) * 8
 
         lane_group = iota((8, LANES), 1) // PICKS
         for local in range(per_block):
@@ -422,14 +426,18 @@
             low = ids & 127
             high = ids >> 7
             total = before_ref[pl.ds(start, 8), :] if part else jnp.zeros((8, LANES), F32)
-            for g in range(groups):
-                key = jnp.where(lane_group == g, high, -1)
-                here = jnp.zeros((8, LANES), F32)
+            for g in range(0, groups, 2):
+                key = jnp.concatenate([jnp.where(lane_group == g + i, high, -1) for i in range(step // 8)], axis=0)
+                index = jnp.concatenate([low] * (step // 8), axis=0)
+                key, index = key.astype(jnp.int16), index.astype(jnp.int16)
+                here = jnp.zeros((step, LANES), BF16)
                 row = local * capacity + g * 8
                 for c in range(chunks):
-                    found = scores[row : row + 8, c * LANES : (c + 1) * LANES]
-                    here = jnp.where(key == c, lane_pick(found, low), here)
-                total = total + here
+                    found = scores[row : row + step, c * LANES : (c + 1) * LANES]
+                    here = jnp.where(key == jnp.int16(c), short_pick(found, index), here)
+                here = here.astype(F32)
+                for i in range(step // 8):
+                    total = total + here[i * 8 : (i + 1) * 8]
             out_ref[pl.ds(start, 8), :] = total.astype(out_ref.dtype)
         return outer
 
@@ -571,7 +579,8 @@
             dq[:, first:last] = jnp.where(own, result, dq[:, first:last])
         return carry
 
-    lax.fori_loop(0, heads, one, 0)
+    for h in range(heads):
+        one(h, 0)
     grads_all[:, 0:cols] = (jnp.transpose(dq[...]) * scaling)[:, :cols].astype(BF16)
     grads_all[:, cols : 2 * cols] = dk[:, :cols].astype(BF16)
     grads_all[:, 2 * cols :] = dv[:, :cols].astype(BF16)
@@ -1144,7 +1153,7 @@
         return call(
             fixed(recall_back_kernel, part, batches, groups), name, "L" + "L" * part + "VH",
             [(kind, shaped((owners * 8, LANES), dtype))], (ids, *before, grads, memory_values),
-            [pltpu.VMEM((rows_dev, half), BF16), pltpu.VMEM((block, rows_dev), F32), sema(1)],
+            [pltpu.VMEM((rows_dev, half), BF16), pltpu.VMEM((block, rows_dev), BF16), sema(1)],
         )[0]
 
     rights, normed_all = lax.optimization_barrier((rights, normed_all))

time: 226 us -> 224 us (level)
  no operation moved by 1% of the time
where the time goes in v4:
time: 224 us; the launch traced here: 223 us
  Pallas kernels  98.3 us (44%)
  starting transfers between devices  72.9 us (33%)
  waiting for transfers between devices  49.3 us (22%)
  between operations  2.5 us (1%)
    pallas_call x28, Pallas kernels, call(): pl.pallas_call(wrapped, name=name, out_shape=[pltpu.HBM(out.shape, out.dt...  98.3 us
    all_to_all x10, starting transfers between devices, exchange(): return lax.all_to_all(values, axes, split_axis=0, concat_axis=0, tiled=True)  37.4 us
    all_to_all x10, waiting for transfers between devices, exchange(): return lax.all_to_all(values, axes, split_axis=0, concat_axis=0, tiled=True)  33.2 us
    ppermute x18, starting transfers between devices, along(): lax.ppermute(values, axis, [(i, (i + step) % size) for i in range(size)])  24.1 us
    ppermute x18, waiting for transfers between devices, along(): lax.ppermute(values, axis, [(i, (i + step) % size) for i in range(size)])  14.1 us
    ppermute x12, starting transfers between devices, across(): return lax.ppermute(values, axis, [(i, i ^ mask) for i in range(size)])  11.4 us
  transfers between devices with their start and end apart: 40, of which 16 were waited for; matrix products, arithmetic and copies ran while one was open for 0% of the time, Pallas kernels for 35%

profile of v4, /device:TPU:0, one launch (start us, length us, event | category | flops | bytes accessed | tf_op | source)
XLA Modules:
  0.0 223.1 jit_solution(11313554513817848922)
XLA Ops:
  1.3 5.3 %qkv.1 = (bf16[8,128,384]{2,1,0:T(8,128)(2,1)}, bf16[128,1152]{1,0:T(8,128)(2,1)}) custom-call(s32[1]{0:T(128)S(6)} %copy.22.refs_0_.refs_1_, bf16[128,1024]{1,0:T(8,128)(2,1)} %bitcast.32, bf16[1024]{0:T(1024)(128)(2,1)} %refs_3_.9, bf16[5,1024,1024]{2,1,0:T(8,128)(2,1)} %refs_5_.9, bf16[7,8,16,1024]{3,2,1,0:T(8,128)(2,1)} %bitcast.23, ...), custom_call_target="tpu_custom_call" | custom-call | flops 4096 | bytes 4096 | tf_op jit(solution)/shard_map/qkv/pallas_call | solution.py:126
  6.5 5.2 %all-to-all-start = ((bf16[8,128,384]{2,1,0:T(8,128)(2,1)}), bf16[8,128,384]{2,1,0:T(8,128)(2,1)S(1)}, u32[]{:S(2)}, u32[]{:S(2)}) async-start(bf16[8,128,384]{2,1,0:T(8,128)(2,1)} %get-tuple-element.109), calls=%async_computation | async-start | bytes 1572864 | tf_op jit(solution)/shard_map/all_to_all | solution.py:1042
  19.9 3.3 %mixback.1 = (bf16[128,1024]{1,0:T(8,128)(2,1)}, bf16[128,16]{1,0:T(8,128)(2,1)}) custom-call(s32[1]{0:T(128)S(6)} %copy.22.refs_0_.refs_1_, bf16[128,1024]{1,0:T(8,128)(2,1)} %bitcast.35, bf16[2,1024,1024]{2,1,0:T(8,128)(2,1)} %refs_3_.8, bf16[7,8,16,1024]{3,2,1,0:T(8,128)(2,1)} %bitcast.24, bf16[7,8,16,1024]{3,2,1,0:T(8,128)(2,1)} %refs_7_.7), custom_call_target="tpu_custom_call" | custom-call | flops 4096 | bytes 4096 | tf_op jit(solution)/shard_map/mixback/pallas_call | solution.py:126
  24.3 5.0 %attend.1 = (bf16[8,192,128]{2,1,0:T(8,128)(2,1)}, f32[8,1024]{1,0:T(8,128)}, s32[4,8,128]{2,1,0:T(8,128)}, bf16[1024,384]{1,0:T(8,128)(2,1)}) custom-call(s32[1]{0:T(128)S(6)} %copy.21.refs_0_, bf16[1024,384]{1,0:T(8,128)(2,1)S(1)} %bitcast.19, s32[72,128]{1,0:T(8,128)S(1)} %get-tuple-element.116.refs_2_, s32[72,128]{1,0:T(8,128)S(1)} %collective-permute-done.refs_3_, ...), custom_call_target="tpu_custom_call" | custom-call | flops 4096 | bytes 4096 | tf_op jit(solution)/shard_map/attend/pallas_call | solution.py:126
  29.4 3.8 %all-to-all-start.1 = ((bf16[8,192,128]{2,1,0:T(8,128)(2,1)}), bf16[8,192,128]{2,1,0:T(8,128)(2,1)S(1)}, u32[]{:S(2)}, u32[]{:S(2)}) async-start(bf16[8,192,128]{2,1,0:T(8,128)(2,1)} %get-tuple-element.120), calls=%async_computation.1 | async-start | bytes 786432 | tf_op jit(solution)/shard_map/all_to_all | solution.py:1042
  36.8 5.3 %all-to-all-done.1.refs_1_ = bf16[8,192,128]{2,1,0:T(8,128)(2,1)S(1)} async-done(((bf16[8,192,128]{2,1,0:T(8,128)(2,1)}), bf16[8,192,128]{2,1,0:T(8,128)(2,1)S(1)}, u32[]{:S(2)}, u32[]{:S(2)}) %all-to-all-start.1) | async-done | bytes 393248 | tf_op jit(solution)/shard_map/all_to_all | solution.py:1042
  42.1 4.8 %middle.1 = (bf16[128,512]{1,0:T(8,128)(2,1)S(1)}, bf16[128,512]{1,0:T(8,128)(2,1)S(1)}, bf16[128,1024]{1,0:T(8,128)(2,1)S(1)}, bf16[1024,1024]{1,0:T(8,128)(2,1...) custom-call(s32[1]{0:T(128)S(6)} %copy.22.refs_0_.refs_1_, ...), custom_call_target="tpu_custom_call" | custom-call | flops 4096 | bytes 4096 | tf_op jit(solution)/shard_map/middle/pallas_call | solution.py:126
  46.8 3.2 %collective-permute-start.5 = (bf16[128,512]{1,0:T(8,128)(2,1)S(1)}, bf16[128,512]{1,0:T(8,128)(2,1)S(1)}, u32[]{:S(2)}, u32[]{:S(2)}) collective-permute-start(bf16[128,512]{1,0:T(8,128)(2,1)S(1)} %get-tuple-element.139.refs_1_), channel_id=1, source_target_pairs={{0,24},{8,0},{16,8},{24,16},{1,25},{9,1},{17,9},{25,17},{2,26},{10... | collective-permute-start | bytes 393224 | tf_op jit(solution)/shard_map/ppermute | solution.py:1025
  51.1 4.2 %scores.1 = (bf16[256,128]{1,0:T(8,128)(2,1)}, bf16[128,16]{1,0:T(8,128)(2,1)}, f32[128,128]{1,0:T(8,128)}) custom-call(s32[1]{0:T(128)S(6)} %copy.22.refs_0_.refs_1_, bf16[128,1024]{1,0:T(8,128)(2,1)S(1)} %get-tuple-element.128.refs_1_, bf16[1024,1024]{1,0:T(8,128)(2,1)S(1)} %get-tuple-element.129.refs_2_, s32[128,128]{1,0:T(8,128)} %get-tuple-element.130.refs_3_, ...), custom_call_target="tpu_custom_call" | custom-call | flops 4096 | bytes 4096 | tf_op jit(solution)/shard_map/scores/pallas_call | solution.py:126
  55.3 3.6 %all-to-all-start.2 = ((bf16[32,8,128]{2,1,0:T(8,128)(2,1)}), bf16[32,8,128]{2,1,0:T(8,128)(2,1)S(1)}, u32[]{:S(2)}, u32[]{:S(2)}) async-start(bf16[32,8,128]{2,1,0:T(8,128)(2,1)} %bitcast.6), calls=%async_computation.2 | async-start | bytes 131072 | tf_op jit(solution)/shard_map/all_to_all | solution.py:1042
  63.3 3.0 %all-to-all-done.2 = bf16[32,8,128]{2,1,0:T(8,128)(2,1)S(1)} async-done(((bf16[32,8,128]{2,1,0:T(8,128)(2,1)}), bf16[32,8,128]{2,1,0:T(8,128)(2,1)S(1)}, u32[]{:S(2)}, u32[]{:S(2)}) %all-to-all-start.2) | async-done | bytes 65568 | tf_op jit(solution)/shard_map/all_to_all | solution.py:1042
  66.3 3.7 %all-to-all-start.3 = ((bf16[8,4,32,512]{3,2,1,0:T(8,128)(2,1)}), bf16[8,4,32,512]{3,2,1,0:T(8,128)(2,1)S(1)}, u32[]{:S(2)}, u32[]{:S(2)}) async-start(bf16[8,4,32,512]{3,2,1,0:T(8,128)(2,1)} %scatterleft.1), calls=%async_computation.3 | async-start | bytes 2097152 | tf_op jit(solution)/shard_map/all_to_all | solution.py:1042
  70.0 5.8 %prepare.1 = (s32[256,128]{1,0:T(8,128)}, s16[1024,2048]{1,0:T(8,128)(2,1)}) custom-call(bf16[8,64,128]{2,1,0:T(8,128)(2,1)} %get-tuple-element.156.refs_0_), custom_call_target="tpu_custom_call" | custom-call | flops 4096 | bytes 4096 | tf_op jit(solution)/shard_map/prepare/pallas_call | solution.py:126
  75.9 9.2 %recall.1 = bf16[8,4,32,1024]{3,2,1,0:T(8,128)(2,1)} custom-call(bf16[256,128]{1,0:T(8,128)(2,1)S(1)} %bitcast.22, s16[1024,2048]{1,0:T(8,128)(2,1)} %get-tuple-element.157.refs_1_, bf16[2048,1024]{1,0:T(8,128)(2,1)} %refs_3_.7), custom_call_target="tpu_custom_call" | custom-call | flops 4096 | bytes 4096 | tf_op jit(solution)/shard_map/recall/pallas_call | solution.py:126
  85.2 3.8 %all-to-all-start.4 = ((bf16[8,4,32,1024]{3,2,1,0:T(8,128)(2,1)}), bf16[8,4,32,1024]{3,2,1,0:T(8,128)(2,1)S(1)}, u32[]{:S(2)}, u32[]{:S(2)}) async-start(bf16[8,4,32,1024]{3,2,1,0:T(8,128)(2,1)} %recall.1), calls=%async_computation.4 | async-start | bytes 4194304 | tf_op jit(solution)/shard_map/all_to_all | solution.py:1042
  92.2 6.0 %recallleft.1.refs_1_ = f32[256,128]{1,0:T(8,128)} custom-call(s32[256,128]{1,0:T(8,128)} %get-tuple-element.160.refs_0_, bf16[1024,512]{1,0:T(8,128)(2,1)S(1)} %bitcast.17, bf16[2048,1024]{1,0:T(8,128)(2,1)} %refs_3_.7), custom_call_target="tpu_custom_call" | custom-call | flops 4096 | bytes 4096 | tf_op jit(solution)/shard_map/recallleft/pallas_call | solution.py:126
  98.2 5.2 %collective-permute-done.7.refs_3_ = bf16[128,512]{1,0:T(8,128)(2,1)S(1)} collective-permute-done((bf16[128,512]{1,0:T(8,128)(2,1)S(1)}, bf16[128,512]{1,0:T(8,128)(2,1)S(1)}, u32[]{:S(2)}, u32[]{:S(2)}) %collective-permute-start.7) | collective-permute-done | bytes 131104 | tf_op jit(solution)/shard_map/ppermute | solution.py:1025
  105.6 10.1 %all-to-all-done.4.refs_1_ = bf16[8,4,32,1024]{3,2,1,0:T(8,128)(2,1)S(1)} async-done(((bf16[8,4,32,1024]{3,2,1,0:T(8,128)(2,1)}), bf16[8,4,32,1024]{3,2,1,0:T(8,128)(2,1)S(1)}, u32[]{:S(2)}, u32[]{:S(2)}) %all-to-all-start.4) | async-done | bytes 2097184 | tf_op jit(solution)/shard_map/all_to_all | solution.py:1042
  115.7 3.6 %all-to-all-start.5 = ((bf16[8,4,32,512]{3,2,1,0:T(8,128)(2,1)}), bf16[8,4,32,512]{3,2,1,0:T(8,128)(2,1)S(1)}, u32[]{:S(2)}, u32[]{:S(2)}) async-start(bf16[8,4,32,512]{3,2,1,0:T(8,128)(2,1)} %scatterright.1), calls=%async_computation.5 | async-start | bytes 2097152 | tf_op jit(solution)/shard_map/all_to_all | solution.py:1042
  124.0 10.6 %all-to-all-done.5 = bf16[8,4,32,512]{3,2,1,0:T(8,128)(2,1)S(1)} async-done(((bf16[8,4,32,512]{3,2,1,0:T(8,128)(2,1)}), bf16[8,4,32,512]{3,2,1,0:T(8,128)(2,1)S(1)}, u32[]{:S(2)}, u32[]{:S(2)}) %all-to-all-start.5) | async-done | bytes 1048608 | tf_op jit(solution)/shard_map/all_to_all | solution.py:1042
  134.6 6.0 %recallright.1 = bf16[256,128]{1,0:T(8,128)(2,1)} custom-call(s32[256,128]{1,0:T(8,128)} %get-tuple-element.160.refs_0_, f32[256,128]{1,0:T(8,128)} %recallleft.1.refs_1_, bf16[1024,512]{1,0:T(8,128)(2,1)S(1)} %bitcast.18, bf16[2048,1024]{1,0:T(8,128)(2,1)} %refs_3_.7), custom_call_target="tpu_custom_call" | custom-call | flops 4096 | bytes 4096 | tf_op jit(solution)/shard_map/recallright/pallas_call | solution.py:126
  143.2 4.0 %collective-permute-done.14.refs_5_ = bf16[128,1024]{1,0:T(8,128)(2,1)S(1)} collective-permute-done((bf16[128,1024]{1,0:T(8,128)(2,1)}, bf16[128,1024]{1,0:T(8,128)(2,1)S(1)}, u32[]{:S(2)}, u32[]{:S(2)}) %collective-permute-start.14) | collective-permute-done | bytes 262176 | tf_op jit(solution)/shard_map/ppermute | solution.py:1025
  150.6 8.0 %query.1 = (bf16[8,128,128]{2,1,0:T(8,128)(2,1)}, bf16[128,1024]{1,0:T(8,128)(2,1)}, bf16[2,128,16]{2,1,0:T(8,128)(2,1)}, f32[128,1024]{1,0:T(8,128)}) custom-call(s32[1]{0:T(128)S(6)} %copy.21.refs_0_, s32[1]{0:T(128)S(6)} %copy.22.refs_0_.refs_1_, bf16[256,128]{1,0:T(8,128)(2,1)S(1)} %bitcast.21, s32[128,128]{1,0:T(8,128)} %get-tuple-element.170.refs_3_, ...), custom_call_target="tpu_custom_call" | custom-call | flops 4096 | bytes 4096 | tf_op jit(solution)/shard_map/query/pallas_call | solution.py:126
  158.6 3.6 %all-to-all-start.7 = ((bf16[8,128,128]{2,1,0:T(8,128)(2,1)}), bf16[8,128,128]{2,1,0:T(8,128)(2,1)S(1)}, u32[]{:S(2)}, u32[]{:S(2)}) async-start(bf16[8,128,128]{2,1,0:T(8,128)(2,1)} %get-tuple-element.174), calls=%async_computation.7 | async-start | bytes 524288 | tf_op jit(solution)/shard_map/all_to_all | solution.py:1042
  162.3 3.2 %output.1 = (bf16[128,1024]{1,0:T(8,128)(2,1)}, bf16[128,16]{1,0:T(8,128)(2,1)}) custom-call(s32[1]{0:T(128)S(6)} %copy.22.refs_0_.refs_1_, bf16[128,1024]{1,0:T(8,128)(2,1)} %get-tuple-element.175.refs_1_.refs_2_, f32[128,1024]{1,0:T(8,128)} %get-tuple-element.173.refs_7_.refs_2_, bf16[2,1024,1024]{2,1,0:T(8,128)(2,1)} %refs_3_.8, ...), custom_call_target="tpu_custom_call" | custom-call | flops 4096 | bytes 4096 | tf_op jit(solution)/shard_map/output/pallas_call | solution.py:126
  169.0 3.4 %all-to-all-start.8 = ((bf16[8,128,128]{2,1,0:T(8,128)(2,1)}), bf16[8,128,128]{2,1,0:T(8,128)(2,1)S(1)}, u32[]{:S(2)}, u32[]{:S(2)}) async-start(bf16[8,128,128]{2,1,0:T(8,128)(2,1)} %factors.1), calls=%async_computation.8 | async-start | bytes 524288 | tf_op jit(solution)/shard_map/all_to_all | solution.py:1042
  172.4 9.0 %attendback.1 = (bf16[8,144,384]{2,1,0:T(8,128)(2,1)}, bf16[48,128]{1,0:T(8,128)(2,1)}) custom-call(s32[1]{0:T(128)S(6)} %copy.21.refs_0_, s32[1]{0:T(128)S(6)} %copy.22.refs_0_.refs_1_, bf16[1024,384]{1,0:T(8,128)(2,1)} %get-tuple-element.177.refs_2_, bf16[1024,128]{1,0:T(8,128)(2,1)S(1)} %bitcast.20, f32[8,1024]{1,0:T(8,128)} %get-tuple-element.190.refs_4_, ...), custom_call_target="tpu_custom_call" | custom-call | flops 4096 | bytes 4096 | tf_op jit(solution)/shard_map/attendback/pallas_call | solution.py:126
  181.4 4.1 %all-to-all-start.9 = ((bf16[8,144,384]{2,1,0:T(8,128)(2,1)}), bf16[8,144,384]{2,1,0:T(8,128)(2,1)S(1)}, u32[]{:S(2)}, u32[]{:S(2)}) async-start(bf16[8,144,384]{2,1,0:T(8,128)(2,1)} %get-tuple-element.195), calls=%async_computation.9 | async-start | bytes 1769472 | tf_op jit(solution)/shard_map/all_to_all | solution.py:1042
  190.0 3.2 %collective-permute-done.20.refs_2_ = bf16[128,128]{1,0:T(8,128)(2,1)S(1)} collective-permute-done((bf16[128,128]{1,0:T(8,128)(2,1)S(1)}, bf16[128,128]{1,0:T(8,128)(2,1)S(1)}, u32[]{:S(2)}, u32[]{:S(2)}) %collective-permute-start.20) | collective-permute-done | bytes 32800 | tf_op jit(solution)/shard_map/ppermute | solution.py:1025
  205.0 5.3 %entry.1 = bf16[128,1024]{1,0:T(8,128)(2,1)} custom-call(s32[1]{0:T(128)S(6)} %copy.22.refs_0_.refs_1_, bf16[8,144,384]{2,1,0:T(8,128)(2,1)S(1)} %all-to-all-done.9.refs_0_.refs_1_, bf16[128,1024]{1,0:T(8,128)(2,1)} %bitcast.34, bf16[1024]{0:T(1024)(128)(2,1)} %refs_3_.9, f32[128,1024]{1,0:T(8,128)} %get-tuple-element.180.refs_3_.refs_4_, ...), custom_call_target="tpu_custom_call" | custom-call | flops 4096 | bytes 4096 | tf_op jit(solution)/shard_map/entry/pallas_call | solution.py:126
  214.0 3.7 %spread.1 = (f32[7,8,16,1024]{3,2,1,0:T(8,128)}, f32[7,8,16,1024]{3,2,1,0:T(8,128)}) custom-call(s32[256,128]{1,0:T(8,128)} %get-tuple-element.160.refs_0_, bf16[4,4,128,128]{3,2,1,0:T(8,128)(2,1)S(1)} %pairsearly.1.refs_1_, bf16[4,4,128,128]{3,2,1,0:T(8,128)(2,1)S(1)} %collective-permute-done.28.refs_2_), custom_call_target="tpu_custom_call" | custom-call | flops 4096 | bytes 4096 | tf_op jit(solution)/shard_map/spread/pallas_call | solution.py:126
  219.9 3.0 %lastspread.1 = (f32[7,8,16,1024]{3,2,1,0:T(8,128)}, f32[7,8,16,1024]{3,2,1,0:T(8,128)}) custom-call(s32[256,128]{1,0:T(8,128)} %get-tuple-element.160.refs_0_, f32[7,8,16,1024]{3,2,1,0:T(8,128)} %get-tuple-element.206.refs_1_, f32[7,8,16,1024]{3,2,1,0:T(8,128)} %get-tuple-element.207.refs_2_, ...), custom_call_target="tpu_custom_call", output_to_operand_aliasing={{0}: (1, {}), {1}: (2, {})} | custom-call | flops 4096 | bytes 4096 | tf_op jit(solution)/shard_map/lastspread/pallas_call | solution.py:126
  (78 shorter events, 59.2 us)
Async XLA Ops:
  6.5 17.8 %all-to-all-start = ((bf16[8,128,384]{2,1,0:T(8,128)(2,1)}), bf16[8,128,384]{2,1,0:T(8,128)(2,1)S(1)}, u32[]{:S(2)}, u32[]{:S(2)}) async-start(bf16[8,128,384]{2,1,0:T(8,128)(2,1)} %get-tuple-element.109), calls=%async_computation | async-start | bytes 1572864 | tf_op jit(solution)/shard_map/all_to_all | solution.py:1042
  14.4 9.6 %collective-permute-start = (s32[72,128]{1,0:T(8,128)S(1)}, s32[72,128]{1,0:T(8,128)S(1)}, u32[]{:S(2)}, u32[]{:S(2)}) collective-permute-start(s32[72,128]{1,0:T(8,128)S(1)} %get-tuple-element.111), channel_id=1, source_target_pairs={{0,8},{8,16},{16,24},{24,0},{1,9},{9,17},{17,25},{25,1},{2,10},{10... | collective-permute-start | bytes 110600 | tf_op jit(solution)/shard_map/ppermute | solution.py:1025
  16.0 7.9 %collective-permute-start.1 = (s32[72,128]{1,0:T(8,128)S(1)}, s32[72,128]{1,0:T(8,128)S(1)}, u32[]{:S(2)}, u32[]{:S(2)}) collective-permute-start(s32[72,128]{1,0:T(8,128)S(1)} %get-tuple-element.112), channel_id=1, source_target_pairs={{0,16},{8,24},{16,0},{24,8},{1,17},{9,25},{17,1},{25,9},{2,18},{10... | collective-permute-start | bytes 110600 | tf_op jit(solution)/shard_map/ppermute | solution.py:1025
  29.4 12.7 %all-to-all-start.1 = ((bf16[8,192,128]{2,1,0:T(8,128)(2,1)}), bf16[8,192,128]{2,1,0:T(8,128)(2,1)S(1)}, u32[]{:S(2)}, u32[]{:S(2)}) async-start(bf16[8,192,128]{2,1,0:T(8,128)(2,1)} %get-tuple-element.120), calls=%async_computation.1 | async-start | bytes 786432 | tf_op jit(solution)/shard_map/all_to_all | solution.py:1042
  33.2 16.9 %collective-permute-start.11 = (bf16[128,1152]{1,0:T(8,128)(2,1)S(1)}, bf16[128,1152]{1,0:T(8,128)(2,1)S(1)}, u32[]{:S(2)}, u32[]{:S(2)}) collective-permute-start(bf16[128,1152]{1,0:T(8,128)(2,1)S(1)} %copy-done), channel_id=1, source_target_pairs={{0,6},{1,7},{2,4},{3,5},{4,2},{5,3},{6,0},{7,1},{8,14},{9,15},{10,... | collective-permute-start | bytes 884744 | tf_op jit(solution)/shard_map/ppermute | solution.py:1029
  36.1 19.2 %collective-permute-start.10 = (bf16[128,1152]{1,0:T(8,128)(2,1)S(1)}, bf16[128,1152]{1,0:T(8,128)(2,1)S(1)}, u32[]{:S(2)}, u32[]{:S(2)}) collective-permute-start(bf16[128,1152]{1,0:T(8,128)(2,1)S(1)} %copy-done), channel_id=1, source_target_pairs={{0,4},{1,5},{2,6},{3,7},{4,0},{5,1},{6,2},{7,3},{8,12},{9,13},{10,... | collective-permute-start | bytes 884744 | tf_op jit(solution)/shard_map/ppermute | solution.py:1029
  36.7 18.6 %collective-permute-start.9 = (bf16[128,1152]{1,0:T(8,128)(2,1)S(1)}, bf16[128,1152]{1,0:T(8,128)(2,1)S(1)}, u32[]{:S(2)}, u32[]{:S(2)}) collective-permute-start(bf16[128,1152]{1,0:T(8,128)(2,1)S(1)} %copy-done), channel_id=1, source_target_pairs={{0,2},{1,3},{2,0},{3,1},{4,6},{5,7},{6,4},{7,5},{8,10},{9,11},{10,... | collective-permute-start | bytes 884744 | tf_op jit(solution)/shard_map/ppermute | solution.py:1029
  46.8 12.1 %collective-permute-start.5 = (bf16[128,512]{1,0:T(8,128)(2,1)S(1)}, bf16[128,512]{1,0:T(8,128)(2,1)S(1)}, u32[]{:S(2)}, u32[]{:S(2)}) collective-permute-start(bf16[128,512]{1,0:T(8,128)(2,1)S(1)} %get-tuple-element.139.refs_1_), channel_id=1, source_target_pairs={{0,24},{8,0},{16,8},{24,16},{1,25},{9,1},{17,9},{25,17},{2,26},{10... | collective-permute-start | bytes 393224 | tf_op jit(solution)/shard_map/ppermute | solution.py:1025
  50.1 9.9 %collective-permute-start.4 = (bf16[128,512]{1,0:T(8,128)(2,1)S(1)}, bf16[128,512]{1,0:T(8,128)(2,1)S(1)}, u32[]{:S(2)}, u32[]{:S(2)}) collective-permute-start(bf16[128,512]{1,0:T(8,128)(2,1)S(1)} %get-tuple-element.139.refs_1_), channel_id=1, source_target_pairs={{0,16},{8,24},{16,0},{24,8},{1,17},{9,25},{17,1},{25,9},{2,18},{10... | collective-permute-start | bytes 393224 | tf_op jit(solution)/shard_map/ppermute | solution.py:1025
  50.1 9.9 %collective-permute-start.3 = (bf16[128,512]{1,0:T(8,128)(2,1)S(1)}, bf16[128,512]{1,0:T(8,128)(2,1)S(1)}, u32[]{:S(2)}, u32[]{:S(2)}) collective-permute-start(bf16[128,512]{1,0:T(8,128)(2,1)S(1)} %get-tuple-element.139.refs_1_), channel_id=1, source_target_pairs={{0,8},{8,16},{16,24},{24,0},{1,9},{9,17},{17,25},{25,1},{2,10},{10... | collective-permute-start | bytes 393224 | tf_op jit(solution)/shard_map/ppermute | solution.py:1025
  55.3 11.0 %all-to-all-start.2 = ((bf16[32,8,128]{2,1,0:T(8,128)(2,1)}), bf16[32,8,128]{2,1,0:T(8,128)(2,1)S(1)}, u32[]{:S(2)}, u32[]{:S(2)}) async-start(bf16[32,8,128]{2,1,0:T(8,128)(2,1)} %bitcast.6), calls=%async_computation.2 | async-start | bytes 131072 | tf_op jit(solution)/shard_map/all_to_all | solution.py:1042
  66.3 18.9 %all-to-all-start.3 = ((bf16[8,4,32,512]{3,2,1,0:T(8,128)(2,1)}), bf16[8,4,32,512]{3,2,1,0:T(8,128)(2,1)S(1)}, u32[]{:S(2)}, u32[]{:S(2)}) async-start(bf16[8,4,32,512]{3,2,1,0:T(8,128)(2,1)} %scatterleft.1), calls=%async_computation.3 | async-start | bytes 2097152 | tf_op jit(solution)/shard_map/all_to_all | solution.py:1042
  85.2 30.5 %all-to-all-start.4 = ((bf16[8,4,32,1024]{3,2,1,0:T(8,128)(2,1)}), bf16[8,4,32,1024]{3,2,1,0:T(8,128)(2,1)S(1)}, u32[]{:S(2)}, u32[]{:S(2)}) async-start(bf16[8,4,32,1024]{3,2,1,0:T(8,128)(2,1)} %recall.1), calls=%async_computation.4 | async-start | bytes 4194304 | tf_op jit(solution)/shard_map/all_to_all | solution.py:1042
  89.0 14.4 %collective-permute-start.12 = (bf16[4,128,1152]{2,1,0:T(8,128)(2,1)}, bf16[4,128,1152]{2,1,0:T(8,128)(2,1)}, u32[]{:S(2)}, u32[]{:S(2)}) collective-permute-start(bf16[4,128,1152]{2,1,0:T(8,128)(2,1)} %pairsnorm.1.refs_5_), channel_id=1, source_target_pairs={{0,1},{1,0},{2,3},{3,2},{4,5},{5,4},{6,7},{7,6},{8,9},{9,8},{10,11... | collective-permute-start | bytes 3538952 | tf_op jit(solution)/shard_map/ppermute | solution.py:1029
  89.5 8.7 %collective-permute-start.8 = (bf16[128,512]{1,0:T(8,128)(2,1)S(1)}, bf16[128,512]{1,0:T(8,128)(2,1)S(1)}, u32[]{:S(2)}, u32[]{:S(2)}) collective-permute-start(bf16[128,512]{1,0:T(8,128)(2,1)S(1)} %get-tuple-element.151.refs_1_), channel_id=1, source_target_pairs={{0,24},{8,0},{16,8},{24,16},{1,25},{9,1},{17,9},{25,17},{2,26},{10... | collective-permute-start | bytes 393224 | tf_op jit(solution)/shard_map/ppermute | solution.py:1025
  90.5 13.0 %collective-permute-start.7 = (bf16[128,512]{1,0:T(8,128)(2,1)S(1)}, bf16[128,512]{1,0:T(8,128)(2,1)S(1)}, u32[]{:S(2)}, u32[]{:S(2)}) collective-permute-start(bf16[128,512]{1,0:T(8,128)(2,1)S(1)} %get-tuple-element.151.refs_1_), channel_id=1, source_target_pairs={{0,16},{8,24},{16,0},{24,8},{1,17},{9,25},{17,1},{25,9},{2,18},{10... | collective-permute-start | bytes 393224 | tf_op jit(solution)/shard_map/ppermute | solution.py:1025
  91.6 11.8 %collective-permute-start.6 = (bf16[128,512]{1,0:T(8,128)(2,1)S(1)}, bf16[128,512]{1,0:T(8,128)(2,1)S(1)}, u32[]{:S(2)}, u32[]{:S(2)}) collective-permute-start(bf16[128,512]{1,0:T(8,128)(2,1)S(1)} %get-tuple-element.151.refs_1_), channel_id=1, source_target_pairs={{0,8},{8,16},{16,24},{24,0},{1,9},{9,17},{17,25},{25,1},{2,10},{10... | collective-permute-start | bytes 393224 | tf_op jit(solution)/shard_map/ppermute | solution.py:1025
  115.7 18.9 %all-to-all-start.5 = ((bf16[8,4,32,512]{3,2,1,0:T(8,128)(2,1)}), bf16[8,4,32,512]{3,2,1,0:T(8,128)(2,1)S(1)}, u32[]{:S(2)}, u32[]{:S(2)}) async-start(bf16[8,4,32,512]{3,2,1,0:T(8,128)(2,1)} %scatterright.1), calls=%async_computation.5 | async-start | bytes 2097152 | tf_op jit(solution)/shard_map/all_to_all | solution.py:1042
  121.3 21.9 %collective-permute-start.13 = (bf16[128,1024]{1,0:T(8,128)(2,1)}, bf16[128,1024]{1,0:T(8,128)(2,1)S(1)}, u32[]{:S(2)}, u32[]{:S(2)}) collective-permute-start(bf16[128,1024]{1,0:T(8,128)(2,1)} %get-tuple-element.164), channel_id=1, source_target_pairs={{0,24},{8,0},{16,8},{24,16},{1,25},{9,1},{17,9},{25,17},{2,26},{10... | collective-permute-start | bytes 786440 | tf_op jit(solution)/shard_map/ppermute | solution.py:1025
  122.2 25.0 %collective-permute-start.14 = (bf16[128,1024]{1,0:T(8,128)(2,1)}, bf16[128,1024]{1,0:T(8,128)(2,1)S(1)}, u32[]{:S(2)}, u32[]{:S(2)}) collective-permute-start(bf16[128,1024]{1,0:T(8,128)(2,1)} %get-tuple-element.165), channel_id=1, source_target_pairs={{0,16},{8,24},{16,0},{24,8},{1,17},{9,25},{17,1},{25,9},{2,18},{10... | collective-permute-start | bytes 786440 | tf_op jit(solution)/shard_map/ppermute | solution.py:1025
  123.4 23.8 %collective-permute-start.15 = (bf16[128,1024]{1,0:T(8,128)(2,1)}, bf16[128,1024]{1,0:T(8,128)(2,1)S(1)}, u32[]{:S(2)}, u32[]{:S(2)}) collective-permute-start(bf16[128,1024]{1,0:T(8,128)(2,1)} %get-tuple-element.166), channel_id=1, source_target_pairs={{0,8},{8,16},{16,24},{24,0},{1,9},{9,17},{17,25},{25,1},{2,10},{10... | collective-permute-start | bytes 786440 | tf_op jit(solution)/shard_map/ppermute | solution.py:1025
  140.6 10.0 %all-to-all-start.6 = ((bf16[32,8,128]{2,1,0:T(8,128)(2,1)}), bf16[32,8,128]{2,1,0:T(8,128)(2,1)S(1)}, u32[]{:S(2)}, u32[]{:S(2)}) async-start(bf16[32,8,128]{2,1,0:T(8,128)(2,1)} %bitcast.10), calls=%async_computation.6 | async-start | bytes 131072 | tf_op jit(solution)/shard_map/all_to_all | solution.py:1042
  158.6 10.4 %all-to-all-start.7 = ((bf16[8,128,128]{2,1,0:T(8,128)(2,1)}), bf16[8,128,128]{2,1,0:T(8,128)(2,1)S(1)}, u32[]{:S(2)}, u32[]{:S(2)}) async-start(bf16[8,128,128]{2,1,0:T(8,128)(2,1)} %get-tuple-element.174), calls=%async_computation.7 | async-start | bytes 524288 | tf_op jit(solution)/shard_map/all_to_all | solution.py:1042
  169.0 12.4 %all-to-all-start.8 = ((bf16[8,128,128]{2,1,0:T(8,128)(2,1)}), bf16[8,128,128]{2,1,0:T(8,128)(2,1)S(1)}, u32[]{:S(2)}, u32[]{:S(2)}) async-start(bf16[8,128,128]{2,1,0:T(8,128)(2,1)} %factors.1), calls=%async_computation.8 | async-start | bytes 524288 | tf_op jit(solution)/shard_map/all_to_all | solution.py:1042
  181.4 18.4 %all-to-all-start.9 = ((bf16[8,144,384]{2,1,0:T(8,128)(2,1)}), bf16[8,144,384]{2,1,0:T(8,128)(2,1)S(1)}, u32[]{:S(2)}, u32[]{:S(2)}) async-start(bf16[8,144,384]{2,1,0:T(8,128)(2,1)} %get-tuple-element.195), calls=%async_computation.9 | async-start | bytes 1769472 | tf_op jit(solution)/shard_map/all_to_all | solution.py:1042
  193.8 9.2 %collective-permute-start.24 = (bf16[4,128,128]{2,1,0:T(8,128)(2,1)S(1)}, bf16[4,128,128]{2,1,0:T(8,128)(2,1)S(1)}, u32[]{:S(2)}, u32[]{:S(2)}) collective-permute-start(bf16[4,128,128]{2,1,0:T(8,128)(2,1)S(1)} %stackearly.1.refs_0_), channel_id=1, source_target_pairs={{0,6},{1,7},{2,4},{3,5},{4,2},{5,3},{6,0},{7,1},{8,14},{9,15},{10,... | collective-permute-start | bytes 393224 | tf_op jit(solution)/shard_map/ppermute | solution.py:1029
  196.8 8.2 %collective-permute-start.23 = (bf16[4,128,128]{2,1,0:T(8,128)(2,1)S(1)}, bf16[4,128,128]{2,1,0:T(8,128)(2,1)S(1)}, u32[]{:S(2)}, u32[]{:S(2)}) collective-permute-start(bf16[4,128,128]{2,1,0:T(8,128)(2,1)S(1)} %stackearly.1.refs_0_), channel_id=1, source_target_pairs={{0,4},{1,5},{2,6},{3,7},{4,0},{5,1},{6,2},{7,3},{8,12},{9,13},{10,... | collective-permute-start | bytes 393224 | tf_op jit(solution)/shard_map/ppermute | solution.py:1029
  197.3 7.6 %collective-permute-start.22 = (bf16[4,128,128]{2,1,0:T(8,128)(2,1)S(1)}, bf16[4,128,128]{2,1,0:T(8,128)(2,1)S(1)}, u32[]{:S(2)}, u32[]{:S(2)}) collective-permute-start(bf16[4,128,128]{2,1,0:T(8,128)(2,1)S(1)} %stackearly.1.refs_0_), channel_id=1, source_target_pairs={{0,2},{1,3},{2,0},{3,1},{4,6},{5,7},{6,4},{7,5},{8,10},{9,11},{10,... | collective-permute-start | bytes 393224 | tf_op jit(solution)/shard_map/ppermute | solution.py:1029
  200.5 9.8 %collective-permute-start.18 = (bf16[96,128]{1,0:T(8,128)(2,1)S(1)}, bf16[96,128]{1,0:T(8,128)(2,1)S(1)}, u32[]{:S(2)}, u32[]{:S(2)}) collective-permute-start(bf16[96,128]{1,0:T(8,128)(2,1)S(1)} %late.1.refs_0_), channel_id=1, source_target_pairs={{0,24},{8,0},{16,8},{24,16},{1,25},{9,1},{17,9},{25,17},{2,26},{10... | collective-permute-start | bytes 73736 | tf_op jit(solution)/shard_map/ppermute | solution.py:1025
  203.0 7.4 %collective-permute-start.17 = (bf16[96,128]{1,0:T(8,128)(2,1)S(1)}, bf16[96,128]{1,0:T(8,128)(2,1)S(1)}, u32[]{:S(2)}, u32[]{:S(2)}) collective-permute-start(bf16[96,128]{1,0:T(8,128)(2,1)S(1)} %late.1.refs_0_), channel_id=1, source_target_pairs={{0,16},{8,24},{16,0},{24,8},{1,17},{9,25},{17,1},{25,9},{2,18},{10... | collective-permute-start | bytes 73736 | tf_op jit(solution)/shard_map/ppermute | solution.py:1025
  203.0 7.4 %collective-permute-start.16 = (bf16[96,128]{1,0:T(8,128)(2,1)S(1)}, bf16[96,128]{1,0:T(8,128)(2,1)S(1)}, u32[]{:S(2)}, u32[]{:S(2)}) collective-permute-start(bf16[96,128]{1,0:T(8,128)(2,1)S(1)} %late.1.refs_0_), channel_id=1, source_target_pairs={{0,8},{8,16},{16,24},{24,0},{1,9},{9,17},{17,25},{25,1},{2,10},{10... | collective-permute-start | bytes 73736 | tf_op jit(solution)/shard_map/ppermute | solution.py:1025
  210.5 7.3 %collective-permute-start.27 = (bf16[4,96,128]{2,1,0:T(8,128)(2,1)S(1)}, bf16[4,96,128]{2,1,0:T(8,128)(2,1)S(1)}, u32[]{:S(2)}, u32[]{:S(2)}) collective-permute-start(bf16[4,96,128]{2,1,0:T(8,128)(2,1)S(1)} %stacklate.1.refs_0_), channel_id=1, source_target_pairs={{0,6},{1,7},{2,4},{3,5},{4,2},{5,3},{6,0},{7,1},{8,14},{9,15},{10,... | collective-permute-start | bytes 294920 | tf_op jit(solution)/shard_map/ppermute | solution.py:1029
  (9 other events, 52.1 us)

commit v5 on v4

--- a/solution.py
+++ b/solution.py
@@ -970,8 +970,17 @@
     return [ids_ref[b * step : b * step + 1, 0:1] // ADAPTER_STEP for b in range(batches)]
 
 
-def spread_rows(parts, marks, runs, stage, sems):
-    seq, batches = parts.shape[:2]
+def spread_rows(even, odd, marks, runs, stage, sems):
+    pairs, batches = even.shape[:2]
+    seq = 2 * pairs
+    me = lax.axis_index("seq")
+
+    def part(s, k, start):
+        place = me ^ s
+        at = place // 2
+        rows = even[at, k, pl.ds(start, RANK), :].astype(F32), odd[at, k, pl.ds(start, RANK), :].astype(F32)
+        return jnp.where(lax.rem(place, 2) == 0, rows[0], rows[1])
+
     for target, origin, base, count in runs:
 
         def put(i, target=target, origin=origin, base=base):
@@ -980,7 +989,7 @@
         def one(i, carry, put=put, base=base):
             start = pl.multiple_of((base + i) * RANK, RANK)
             rows = [
-                jnp.concatenate([parts[s, k, pl.ds(start, RANK), :] for s in range(seq)], axis=1).astype(F32)
+                jnp.concatenate([part(s, k, start) for s in range(seq)], axis=1)
                 for k in range(batches)
             ]
             for k in range(ADAPTERS):
@@ -997,28 +1006,16 @@
             pltpu.make_async_copy(stage.at[base + i], target.at[origin + i], sems.at[base + i]).wait()
 
 
-def spread_kernel(batches, ready, ids_ref, *refs):
-    down_any, up_any, parts, stage, load_sems, sems = refs[-6:]
-    seq = parts.shape[0]
-    me = lax.axis_index("seq")
-    copies = fetch([(refs[m % 2].at[m // 2], parts.at[me ^ m]) for m in range(seq)], load_sems)
+def spread_kernel(batches, ready, ids_ref, even, odd, down_any, up_any, stage, sems):
     ready()
     marks = relative_marks(ids_ref, batches)
-    for copy in copies:
-        copy.wait()
-    spread_rows(parts, marks, ((down_any, 3, 0, 4), (up_any, 3, 4, 4)), stage, sems)
-
-
-def last_spread_kernel(batches, ready, ids_ref, down_in, up_in, *refs):
-    down_any, up_any, parts, stage, load_sems, sems = refs[-6:]
-    seq = parts.shape[0]
-    me = lax.axis_index("seq")
-    copies = fetch([(refs[m % 2].at[m // 2], parts.at[me ^ m]) for m in range(seq)], load_sems)
+    spread_rows(even, odd, marks, ((down_any, 3, 0, 4), (up_any, 3, 4, 4)), stage, sems)
+
+
+def last_spread_kernel(batches, ready, ids_ref, down_in, up_in, even, odd, down_any, up_any, stage, sems):
     ready()
     marks = relative_marks(ids_ref, batches)
-    for copy in copies:
-        copy.wait()
-    spread_rows(parts, marks, ((down_any, 0, 0, 3), (up_any, 0, 3, 3)), stage, sems)
+    spread_rows(even, odd, marks, ((down_any, 0, 0, 3), (up_any, 0, 3, 3)), stage, sems)
 
 
 def along(values, axis, step, size):
@@ -1222,7 +1219,7 @@
     full = shaped((7, ADAPTERS, RANK, width), F32)
     grad_down, grad_up = call(
         fixed(spread_kernel, batches), "spread", "LVV", [("H", full), ("H", full)], (ids, *some),
-        [pltpu.VMEM((seq, batches, 8 * RANK, cols), BF16), pltpu.VMEM((8, ADAPTERS, RANK, width), F32), sema(seq), sema(8)],
+        [pltpu.VMEM((8, ADAPTERS, RANK, width), F32), sema(8)],
     )
     late_all, grad_down, grad_up = lax.optimization_barrier((late_all, grad_down, grad_up))
     late_all = stacked(late_all, "pairslate")
@@ -1230,7 +1227,7 @@
     grad_down, grad_up = call(
         fixed(last_spread_kernel, batches), "lastspread", "LHHVV", [("H", full), ("H", full)],
         (ids, grad_down, grad_up, *late_all),
-        [pltpu.VMEM((seq, batches, 6 * RANK, cols), BF16), pltpu.VMEM((6, ADAPTERS, RANK, width), F32), sema(seq), sema(6)],
+        [pltpu.VMEM((6, ADAPTERS, RANK, width), F32), sema(6)],
         aliases={1: 0, 2: 1},
     )
     return (output[None], grad_input[None], jnp.swapaxes(grad_down, 2, 3), grad_up)

time: 224 us -> 224 us (level)
  transfers between devices with their start and end apart: 40 -> 40, of which waited for: 16 -> 16; matrix products, arithmetic and copies ran while one was open for 0% -> 0% of each run, Pallas kernels for 35% -> 34%
where the time goes in v5:
time: 224 us; the launch traced here: 223 us
  Pallas kernels  97.8 us (44%)
  starting transfers between devices  72.9 us (33%)
  waiting for transfers between devices  49.7 us (22%)
  between operations  2.5 us (1%)
    pallas_call x28, Pallas kernels, call(): pl.pallas_call(wrapped, name=name, out_shape=[pltpu.HBM(out.shape, out.dt...  97.8 us
    all_to_all x10, starting transfers between devices, exchange(): return lax.all_to_all(values, axes, split_axis=0, concat_axis=0, tiled=True)  37.4 us
    all_to_all x10, waiting for transfers between devices, exchange(): return lax.all_to_all(values, axes, split_axis=0, concat_axis=0, tiled=True)  33.2 us
    ppermute x18, starting transfers between devices, along(): lax.ppermute(values, axis, [(i, (i + step) % size) for i in range(size)])  24.1 us
    ppermute x18, waiting for transfers between devices, along(): lax.ppermute(values, axis, [(i, (i + step) % size) for i in range(size)])  14.1 us
    ppermute x12, starting transfers between devices, across(): return lax.ppermute(values, axis, [(i, i ^ mask) for i in range(size)])  11.4 us
  transfers between devices with their start and end apart: 40, of which 16 were waited for; matrix products, arithmetic and copies ran while one was open for 0% of the time, Pallas kernels for 34%

profile of v5, /device:TPU:0, one launch (start us, length us, event | category | flops | bytes accessed | tf_op | source)
XLA Modules:
  0.0 223.0 jit_solution(12973600049067090433)
XLA Ops:
  1.3 5.3 %qkv.1 = (bf16[8,128,384]{2,1,0:T(8,128)(2,1)}, bf16[128,1152]{1,0:T(8,128)(2,1)}) custom-call(s32[1]{0:T(128)S(6)} %copy.22.refs_0_.refs_1_, bf16[128,1024]{1,0:T(8,128)(2,1)} %bitcast.32, bf16[1024]{0:T(1024)(128)(2,1)} %refs_3_.9, bf16[5,1024,1024]{2,1,0:T(8,128)(2,1)} %refs_5_.9, bf16[7,8,16,1024]{3,2,1,0:T(8,128)(2,1)} %bitcast.23, ...), custom_call_target="tpu_custom_call" | custom-call | flops 4096 | bytes 4096 | tf_op jit(solution)/shard_map/qkv/pallas_call | solution.py:126
  6.5 5.2 %all-to-all-start = ((bf16[8,128,384]{2,1,0:T(8,128)(2,1)}), bf16[8,128,384]{2,1,0:T(8,128)(2,1)S(1)}, u32[]{:S(2)}, u32[]{:S(2)}) async-start(bf16[8,128,384]{2,1,0:T(8,128)(2,1)} %get-tuple-element.109), calls=%async_computation | async-start | bytes 1572864 | tf_op jit(solution)/shard_map/all_to_all | solution.py:1039
  19.9 3.3 %mixback.1 = (bf16[128,1024]{1,0:T(8,128)(2,1)}, bf16[128,16]{1,0:T(8,128)(2,1)}) custom-call(s32[1]{0:T(128)S(6)} %copy.22.refs_0_.refs_1_, bf16[128,1024]{1,0:T(8,128)(2,1)} %bitcast.35, bf16[2,1024,1024]{2,1,0:T(8,128)(2,1)} %refs_3_.8, bf16[7,8,16,1024]{3,2,1,0:T(8,128)(2,1)} %bitcast.24, bf16[7,8,16,1024]{3,2,1,0:T(8,128)(2,1)} %refs_7_.7), custom_call_target="tpu_custom_call" | custom-call | flops 4096 | bytes 4096 | tf_op jit(solution)/shard_map/mixback/pallas_call | solution.py:126
  24.3 5.0 %attend.1 = (bf16[8,192,128]{2,1,0:T(8,128)(2,1)}, f32[8,1024]{1,0:T(8,128)}, s32[4,8,128]{2,1,0:T(8,128)}, bf16[1024,384]{1,0:T(8,128)(2,1)}) custom-call(s32[1]{0:T(128)S(6)} %copy.21.refs_0_, bf16[1024,384]{1,0:T(8,128)(2,1)S(1)} %bitcast.19, s32[72,128]{1,0:T(8,128)S(1)} %get-tuple-element.116.refs_2_, s32[72,128]{1,0:T(8,128)S(1)} %collective-permute-done.refs_3_, ...), custom_call_target="tpu_custom_call" | custom-call | flops 4096 | bytes 4096 | tf_op jit(solution)/shard_map/attend/pallas_call | solution.py:126
  29.4 3.8 %all-to-all-start.1 = ((bf16[8,192,128]{2,1,0:T(8,128)(2,1)}), bf16[8,192,128]{2,1,0:T(8,128)(2,1)S(1)}, u32[]{:S(2)}, u32[]{:S(2)}) async-start(bf16[8,192,128]{2,1,0:T(8,128)(2,1)} %get-tuple-element.120), calls=%async_computation.1 | async-start | bytes 786432 | tf_op jit(solution)/shard_map/all_to_all | solution.py:1039
  36.8 5.3 %all-to-all-done.1.refs_1_ = bf16[8,192,128]{2,1,0:T(8,128)(2,1)S(1)} async-done(((bf16[8,192,128]{2,1,0:T(8,128)(2,1)}), bf16[8,192,128]{2,1,0:T(8,128)(2,1)S(1)}, u32[]{:S(2)}, u32[]{:S(2)}) %all-to-all-start.1) | async-done | bytes 393248 | tf_op jit(solution)/shard_map/all_to_all | solution.py:1039
  42.1 4.8 %middle.1 = (bf16[128,512]{1,0:T(8,128)(2,1)S(1)}, bf16[128,512]{1,0:T(8,128)(2,1)S(1)}, bf16[128,1024]{1,0:T(8,128)(2,1)S(1)}, bf16[1024,1024]{1,0:T(8,128)(2,1...) custom-call(s32[1]{0:T(128)S(6)} %copy.22.refs_0_.refs_1_, ...), custom_call_target="tpu_custom_call" | custom-call | flops 4096 | bytes 4096 | tf_op jit(solution)/shard_map/middle/pallas_call | solution.py:126
  46.8 3.2 %collective-permute-start.5 = (bf16[128,512]{1,0:T(8,128)(2,1)S(1)}, bf16[128,512]{1,0:T(8,128)(2,1)S(1)}, u32[]{:S(2)}, u32[]{:S(2)}) collective-permute-start(bf16[128,512]{1,0:T(8,128)(2,1)S(1)} %get-tuple-element.139.refs_1_), channel_id=1, source_target_pairs={{0,24},{8,0},{16,8},{24,16},{1,25},{9,1},{17,9},{25,17},{2,26},{10... | collective-permute-start | bytes 393224 | tf_op jit(solution)/shard_map/ppermute | solution.py:1022
  51.1 4.2 %scores.1 = (bf16[256,128]{1,0:T(8,128)(2,1)}, bf16[128,16]{1,0:T(8,128)(2,1)}, f32[128,128]{1,0:T(8,128)}) custom-call(s32[1]{0:T(128)S(6)} %copy.22.refs_0_.refs_1_, bf16[128,1024]{1,0:T(8,128)(2,1)S(1)} %get-tuple-element.128.refs_1_, bf16[1024,1024]{1,0:T(8,128)(2,1)S(1)} %get-tuple-element.129.refs_2_, s32[128,128]{1,0:T(8,128)} %get-tuple-element.130.refs_3_, ...), custom_call_target="tpu_custom_call" | custom-call | flops 4096 | bytes 4096 | tf_op jit(solution)/shard_map/scores/pallas_call | solution.py:126
  55.3 3.6 %all-to-all-start.2 = ((bf16[32,8,128]{2,1,0:T(8,128)(2,1)}), bf16[32,8,128]{2,1,0:T(8,128)(2,1)S(1)}, u32[]{:S(2)}, u32[]{:S(2)}) async-start(bf16[32,8,128]{2,1,0:T(8,128)(2,1)} %bitcast.6), calls=%async_computation.2 | async-start | bytes 131072 | tf_op jit(solution)/shard_map/all_to_all | solution.py:1039
  63.3 3.0 %all-to-all-done.2 = bf16[32,8,128]{2,1,0:T(8,128)(2,1)S(1)} async-done(((bf16[32,8,128]{2,1,0:T(8,128)(2,1)}), bf16[32,8,128]{2,1,0:T(8,128)(2,1)S(1)}, u32[]{:S(2)}, u32[]{:S(2)}) %all-to-all-start.2) | async-done | bytes 65568 | tf_op jit(solution)/shard_map/all_to_all | solution.py:1039
  66.3 3.7 %all-to-all-start.3 = ((bf16[8,4,32,512]{3,2,1,0:T(8,128)(2,1)}), bf16[8,4,32,512]{3,2,1,0:T(8,128)(2,1)S(1)}, u32[]{:S(2)}, u32[]{:S(2)}) async-start(bf16[8,4,32,512]{3,2,1,0:T(8,128)(2,1)} %scatterleft.1), calls=%async_computation.3 | async-start | bytes 2097152 | tf_op jit(solution)/shard_map/all_to_all | solution.py:1039
  70.0 5.8 %prepare.1 = (s32[256,128]{1,0:T(8,128)}, s16[1024,2048]{1,0:T(8,128)(2,1)}) custom-call(bf16[8,64,128]{2,1,0:T(8,128)(2,1)} %get-tuple-element.156.refs_0_), custom_call_target="tpu_custom_call" | custom-call | flops 4096 | bytes 4096 | tf_op jit(solution)/shard_map/prepare/pallas_call | solution.py:126
  75.9 9.2 %recall.1 = bf16[8,4,32,1024]{3,2,1,0:T(8,128)(2,1)} custom-call(bf16[256,128]{1,0:T(8,128)(2,1)S(1)} %bitcast.22, s16[1024,2048]{1,0:T(8,128)(2,1)} %get-tuple-element.157.refs_1_, bf16[2048,1024]{1,0:T(8,128)(2,1)} %refs_3_.7), custom_call_target="tpu_custom_call" | custom-call | flops 4096 | bytes 4096 | tf_op jit(solution)/shard_map/recall/pallas_call | solution.py:126
  85.2 3.8 %all-to-all-start.4 = ((bf16[8,4,32,1024]{3,2,1,0:T(8,128)(2,1)}), bf16[8,4,32,1024]{3,2,1,0:T(8,128)(2,1)S(1)}, u32[]{:S(2)}, u32[]{:S(2)}) async-start(bf16[8,4,32,1024]{3,2,1,0:T(8,128)(2,1)} %recall.1), calls=%async_computation.4 | async-start | bytes 4194304 | tf_op jit(solution)/shard_map/all_to_all | solution.py:1039
  92.2 6.0 %recallleft.1.refs_1_ = f32[256,128]{1,0:T(8,128)} custom-call(s32[256,128]{1,0:T(8,128)} %get-tuple-element.160.refs_0_, bf16[1024,512]{1,0:T(8,128)(2,1)S(1)} %bitcast.17, bf16[2048,1024]{1,0:T(8,128)(2,1)} %refs_3_.7), custom_call_target="tpu_custom_call" | custom-call | flops 4096 | bytes 4096 | tf_op jit(solution)/shard_map/recallleft/pallas_call | solution.py:126
  98.2 5.2 %collective-permute-done.7.refs_3_ = bf16[128,512]{1,0:T(8,128)(2,1)S(1)} collective-permute-done((bf16[128,512]{1,0:T(8,128)(2,1)S(1)}, bf16[128,512]{1,0:T(8,128)(2,1)S(1)}, u32[]{:S(2)}, u32[]{:S(2)}) %collective-permute-start.7) | collective-permute-done | bytes 131104 | tf_op jit(solution)/shard_map/ppermute | solution.py:1022
  105.6 10.1 %all-to-all-done.4.refs_1_ = bf16[8,4,32,1024]{3,2,1,0:T(8,128)(2,1)S(1)} async-done(((bf16[8,4,32,1024]{3,2,1,0:T(8,128)(2,1)}), bf16[8,4,32,1024]{3,2,1,0:T(8,128)(2,1)S(1)}, u32[]{:S(2)}, u32[]{:S(2)}) %all-to-all-start.4) | async-done | bytes 2097184 | tf_op jit(solution)/shard_map/all_to_all | solution.py:1039
  115.7 3.6 %all-to-all-start.5 = ((bf16[8,4,32,512]{3,2,1,0:T(8,128)(2,1)}), bf16[8,4,32,512]{3,2,1,0:T(8,128)(2,1)S(1)}, u32[]{:S(2)}, u32[]{:S(2)}) async-start(bf16[8,4,32,512]{3,2,1,0:T(8,128)(2,1)} %scatterright.1), calls=%async_computation.5 | async-start | bytes 2097152 | tf_op jit(solution)/shard_map/all_to_all | solution.py:1039
  124.0 10.6 %all-to-all-done.5 = bf16[8,4,32,512]{3,2,1,0:T(8,128)(2,1)S(1)} async-done(((bf16[8,4,32,512]{3,2,1,0:T(8,128)(2,1)}), bf16[8,4,32,512]{3,2,1,0:T(8,128)(2,1)S(1)}, u32[]{:S(2)}, u32[]{:S(2)}) %all-to-all-start.5) | async-done | bytes 1048608 | tf_op jit(solution)/shard_map/all_to_all | solution.py:1039
  134.6 6.0 %recallright.1 = bf16[256,128]{1,0:T(8,128)(2,1)} custom-call(s32[256,128]{1,0:T(8,128)} %get-tuple-element.160.refs_0_, f32[256,128]{1,0:T(8,128)} %recallleft.1.refs_1_, bf16[1024,512]{1,0:T(8,128)(2,1)S(1)} %bitcast.18, bf16[2048,1024]{1,0:T(8,128)(2,1)} %refs_3_.7), custom_call_target="tpu_custom_call" | custom-call | flops 4096 | bytes 4096 | tf_op jit(solution)/shard_map/recallright/pallas_call | solution.py:126
  143.2 4.0 %collective-permute-done.14.refs_5_ = bf16[128,1024]{1,0:T(8,128)(2,1)S(1)} collective-permute-done((bf16[128,1024]{1,0:T(8,128)(2,1)}, bf16[128,1024]{1,0:T(8,128)(2,1)S(1)}, u32[]{:S(2)}, u32[]{:S(2)}) %collective-permute-start.14) | collective-permute-done | bytes 262176 | tf_op jit(solution)/shard_map/ppermute | solution.py:1022
  150.6 8.0 %query.1 = (bf16[8,128,128]{2,1,0:T(8,128)(2,1)}, bf16[128,1024]{1,0:T(8,128)(2,1)}, bf16[2,128,16]{2,1,0:T(8,128)(2,1)}, f32[128,1024]{1,0:T(8,128)}) custom-call(s32[1]{0:T(128)S(6)} %copy.21.refs_0_, s32[1]{0:T(128)S(6)} %copy.22.refs_0_.refs_1_, bf16[256,128]{1,0:T(8,128)(2,1)S(1)} %bitcast.21, s32[128,128]{1,0:T(8,128)} %get-tuple-element.170.refs_3_, ...), custom_call_target="tpu_custom_call" | custom-call | flops 4096 | bytes 4096 | tf_op jit(solution)/shard_map/query/pallas_call | solution.py:126
  158.6 3.6 %all-to-all-start.7 = ((bf16[8,128,128]{2,1,0:T(8,128)(2,1)}), bf16[8,128,128]{2,1,0:T(8,128)(2,1)S(1)}, u32[]{:S(2)}, u32[]{:S(2)}) async-start(bf16[8,128,128]{2,1,0:T(8,128)(2,1)} %get-tuple-element.174), calls=%async_computation.7 | async-start | bytes 524288 | tf_op jit(solution)/shard_map/all_to_all | solution.py:1039
  162.3 3.2 %output.1 = (bf16[128,1024]{1,0:T(8,128)(2,1)}, bf16[128,16]{1,0:T(8,128)(2,1)}) custom-call(s32[1]{0:T(128)S(6)} %copy.22.refs_0_.refs_1_, bf16[128,1024]{1,0:T(8,128)(2,1)} %get-tuple-element.175.refs_1_.refs_2_, f32[128,1024]{1,0:T(8,128)} %get-tuple-element.173.refs_7_.refs_2_, bf16[2,1024,1024]{2,1,0:T(8,128)(2,1)} %refs_3_.8, ...), custom_call_target="tpu_custom_call" | custom-call | flops 4096 | bytes 4096 | tf_op jit(solution)/shard_map/output/pallas_call | solution.py:126
  169.0 3.4 %all-to-all-start.8 = ((bf16[8,128,128]{2,1,0:T(8,128)(2,1)}), bf16[8,128,128]{2,1,0:T(8,128)(2,1)S(1)}, u32[]{:S(2)}, u32[]{:S(2)}) async-start(bf16[8,128,128]{2,1,0:T(8,128)(2,1)} %factors.1), calls=%async_computation.8 | async-start | bytes 524288 | tf_op jit(solution)/shard_map/all_to_all | solution.py:1039
  172.4 9.0 %attendback.1 = (bf16[8,144,384]{2,1,0:T(8,128)(2,1)}, bf16[48,128]{1,0:T(8,128)(2,1)}) custom-call(s32[1]{0:T(128)S(6)} %copy.21.refs_0_, s32[1]{0:T(128)S(6)} %copy.22.refs_0_.refs_1_, bf16[1024,384]{1,0:T(8,128)(2,1)} %get-tuple-element.177.refs_2_, bf16[1024,128]{1,0:T(8,128)(2,1)S(1)} %bitcast.20, f32[8,1024]{1,0:T(8,128)} %get-tuple-element.190.refs_4_, ...), custom_call_target="tpu_custom_call" | custom-call | flops 4096 | bytes 4096 | tf_op jit(solution)/shard_map/attendback/pallas_call | solution.py:126
  181.4 4.1 %all-to-all-start.9 = ((bf16[8,144,384]{2,1,0:T(8,128)(2,1)}), bf16[8,144,384]{2,1,0:T(8,128)(2,1)S(1)}, u32[]{:S(2)}, u32[]{:S(2)}) async-start(bf16[8,144,384]{2,1,0:T(8,128)(2,1)} %get-tuple-element.195), calls=%async_computation.9 | async-start | bytes 1769472 | tf_op jit(solution)/shard_map/all_to_all | solution.py:1039
  190.0 3.2 %collective-permute-done.20.refs_2_ = bf16[128,128]{1,0:T(8,128)(2,1)S(1)} collective-permute-done((bf16[128,128]{1,0:T(8,128)(2,1)S(1)}, bf16[128,128]{1,0:T(8,128)(2,1)S(1)}, u32[]{:S(2)}, u32[]{:S(2)}) %collective-permute-start.20) | collective-permute-done | bytes 32800 | tf_op jit(solution)/shard_map/ppermute | solution.py:1022
  193.8 3.0 %collective-permute-start.24 = (bf16[4,128,128]{2,1,0:T(8,128)(2,1)S(1)}, bf16[4,128,128]{2,1,0:T(8,128)(2,1)S(1)}, u32[]{:S(2)}, u32[]{:S(2)}) collective-permute-start(bf16[4,128,128]{2,1,0:T(8,128)(2,1)S(1)} %stackearly.1.refs_0_), channel_id=1, source_target_pairs={{0,6},{1,7},{2,4},{3,5},{4,2},{5,3},{6,0},{7,1},{8,14},{9,15},{10,... | collective-permute-start | bytes 393224 | tf_op jit(solution)/shard_map/ppermute | solution.py:1026
  205.0 5.3 %entry.1 = bf16[128,1024]{1,0:T(8,128)(2,1)} custom-call(s32[1]{0:T(128)S(6)} %copy.22.refs_0_.refs_1_, bf16[8,144,384]{2,1,0:T(8,128)(2,1)S(1)} %all-to-all-done.9.refs_0_.refs_1_, bf16[128,1024]{1,0:T(8,128)(2,1)} %bitcast.34, bf16[1024]{0:T(1024)(128)(2,1)} %refs_3_.9, f32[128,1024]{1,0:T(8,128)} %get-tuple-element.180.refs_3_.refs_4_, ...), custom_call_target="tpu_custom_call" | custom-call | flops 4096 | bytes 4096 | tf_op jit(solution)/shard_map/entry/pallas_call | solution.py:126
  214.0 3.3 %spread.1 = (f32[7,8,16,1024]{3,2,1,0:T(8,128)}, f32[7,8,16,1024]{3,2,1,0:T(8,128)}) custom-call(s32[256,128]{1,0:T(8,128)} %get-tuple-element.160.refs_0_, bf16[4,4,128,128]{3,2,1,0:T(8,128)(2,1)S(1)} %pairsearly.1.refs_1_, bf16[4,4,128,128]{3,2,1,0:T(8,128)(2,1)S(1)} %collective-permute-done.28.refs_2_), custom_call_target="tpu_custom_call" | custom-call | flops 4096 | bytes 4096 | tf_op jit(solution)/shard_map/spread/pallas_call | solution.py:126
  (78 shorter events, 59.5 us)
Async XLA Ops:
  6.5 17.8 %all-to-all-start = ((bf16[8,128,384]{2,1,0:T(8,128)(2,1)}), bf16[8,128,384]{2,1,0:T(8,128)(2,1)S(1)}, u32[]{:S(2)}, u32[]{:S(2)}) async-start(bf16[8,128,384]{2,1,0:T(8,128)(2,1)} %get-tuple-element.109), calls=%async_computation | async-start | bytes 1572864 | tf_op jit(solution)/shard_map/all_to_all | solution.py:1039
  14.4 9.6 %collective-permute-start = (s32[72,128]{1,0:T(8,128)S(1)}, s32[72,128]{1,0:T(8,128)S(1)}, u32[]{:S(2)}, u32[]{:S(2)}) collective-permute-start(s32[72,128]{1,0:T(8,128)S(1)} %get-tuple-element.111), channel_id=1, source_target_pairs={{0,8},{8,16},{16,24},{24,0},{1,9},{9,17},{17,25},{25,1},{2,10},{10... | collective-permute-start | bytes 110600 | tf_op jit(solution)/shard_map/ppermute | solution.py:1022
  16.0 7.9 %collective-permute-start.1 = (s32[72,128]{1,0:T(8,128)S(1)}, s32[72,128]{1,0:T(8,128)S(1)}, u32[]{:S(2)}, u32[]{:S(2)}) collective-permute-start(s32[72,128]{1,0:T(8,128)S(1)} %get-tuple-element.112), channel_id=1, source_target_pairs={{0,16},{8,24},{16,0},{24,8},{1,17},{9,25},{17,1},{25,9},{2,18},{10... | collective-permute-start | bytes 110600 | tf_op jit(solution)/shard_map/ppermute | solution.py:1022
  29.4 12.7 %all-to-all-start.1 = ((bf16[8,192,128]{2,1,0:T(8,128)(2,1)}), bf16[8,192,128]{2,1,0:T(8,128)(2,1)S(1)}, u32[]{:S(2)}, u32[]{:S(2)}) async-start(bf16[8,192,128]{2,1,0:T(8,128)(2,1)} %get-tuple-element.120), calls=%async_computation.1 | async-start | bytes 786432 | tf_op jit(solution)/shard_map/all_to_all | solution.py:1039
  33.2 16.9 %collective-permute-start.11 = (bf16[128,1152]{1,0:T(8,128)(2,1)S(1)}, bf16[128,1152]{1,0:T(8,128)(2,1)S(1)}, u32[]{:S(2)}, u32[]{:S(2)}) collective-permute-start(bf16[128,1152]{1,0:T(8,128)(2,1)S(1)} %copy-done), channel_id=1, source_target_pairs={{0,6},{1,7},{2,4},{3,5},{4,2},{5,3},{6,0},{7,1},{8,14},{9,15},{10,... | collective-permute-start | bytes 884744 | tf_op jit(solution)/shard_map/ppermute | solution.py:1026
  36.1 19.2 %collective-permute-start.10 = (bf16[128,1152]{1,0:T(8,128)(2,1)S(1)}, bf16[128,1152]{1,0:T(8,128)(2,1)S(1)}, u32[]{:S(2)}, u32[]{:S(2)}) collective-permute-start(bf16[128,1152]{1,0:T(8,128)(2,1)S(1)} %copy-done), channel_id=1, source_target_pairs={{0,4},{1,5},{2,6},{3,7},{4,0},{5,1},{6,2},{7,3},{8,12},{9,13},{10,... | collective-permute-start | bytes 884744 | tf_op jit(solution)/shard_map/ppermute | solution.py:1026
  36.7 18.6 %collective-permute-start.9 = (bf16[128,1152]{1,0:T(8,128)(2,1)S(1)}, bf16[128,1152]{1,0:T(8,128)(2,1)S(1)}, u32[]{:S(2)}, u32[]{:S(2)}) collective-permute-start(bf16[128,1152]{1,0:T(8,128)(2,1)S(1)} %copy-done), channel_id=1, source_target_pairs={{0,2},{1,3},{2,0},{3,1},{4,6},{5,7},{6,4},{7,5},{8,10},{9,11},{10,... | collective-permute-start | bytes 884744 | tf_op jit(solution)/shard_map/ppermute | solution.py:1026
  46.8 12.1 %collective-permute-start.5 = (bf16[128,512]{1,0:T(8,128)(2,1)S(1)}, bf16[128,512]{1,0:T(8,128)(2,1)S(1)}, u32[]{:S(2)}, u32[]{:S(2)}) collective-permute-start(bf16[128,512]{1,0:T(8,128)(2,1)S(1)} %get-tuple-element.139.refs_1_), channel_id=1, source_target_pairs={{0,24},{8,0},{16,8},{24,16},{1,25},{9,1},{17,9},{25,17},{2,26},{10... | collective-permute-start | bytes 393224 | tf_op jit(solution)/shard_map/ppermute | solution.py:1022
  50.1 9.9 %collective-permute-start.4 = (bf16[128,512]{1,0:T(8,128)(2,1)S(1)}, bf16[128,512]{1,0:T(8,128)(2,1)S(1)}, u32[]{:S(2)}, u32[]{:S(2)}) collective-permute-start(bf16[128,512]{1,0:T(8,128)(2,1)S(1)} %get-tuple-element.139.refs_1_), channel_id=1, source_target_pairs={{0,16},{8,24},{16,0},{24,8},{1,17},{9,25},{17,1},{25,9},{2,18},{10... | collective-permute-start | bytes 393224 | tf_op jit(solution)/shard_map/ppermute | solution.py:1022
  50.1 9.9 %collective-permute-start.3 = (bf16[128,512]{1,0:T(8,128)(2,1)S(1)}, bf16[128,512]{1,0:T(8,128)(2,1)S(1)}, u32[]{:S(2)}, u32[]{:S(2)}) collective-permute-start(bf16[128,512]{1,0:T(8,128)(2,1)S(1)} %get-tuple-element.139.refs_1_), channel_id=1, source_target_pairs={{0,8},{8,16},{16,24},{24,0},{1,9},{9,17},{17,25},{25,1},{2,10},{10... | collective-permute-start | bytes 393224 | tf_op jit(solution)/shard_map/ppermute | solution.py:1022
  55.3 11.0 %all-to-all-start.2 = ((bf16[32,8,128]{2,1,0:T(8,128)(2,1)}), bf16[32,8,128]{2,1,0:T(8,128)(2,1)S(1)}, u32[]{:S(2)}, u32[]{:S(2)}) async-start(bf16[32,8,128]{2,1,0:T(8,128)(2,1)} %bitcast.6), calls=%async_computation.2 | async-start | bytes 131072 | tf_op jit(solution)/shard_map/all_to_all | solution.py:1039
  66.3 18.9 %all-to-all-start.3 = ((bf16[8,4,32,512]{3,2,1,0:T(8,128)(2,1)}), bf16[8,4,32,512]{3,2,1,0:T(8,128)(2,1)S(1)}, u32[]{:S(2)}, u32[]{:S(2)}) async-start(bf16[8,4,32,512]{3,2,1,0:T(8,128)(2,1)} %scatterleft.1), calls=%async_computation.3 | async-start | bytes 2097152 | tf_op jit(solution)/shard_map/all_to_all | solution.py:1039
  85.2 30.5 %all-to-all-start.4 = ((bf16[8,4,32,1024]{3,2,1,0:T(8,128)(2,1)}), bf16[8,4,32,1024]{3,2,1,0:T(8,128)(2,1)S(1)}, u32[]{:S(2)}, u32[]{:S(2)}) async-start(bf16[8,4,32,1024]{3,2,1,0:T(8,128)(2,1)} %recall.1), calls=%async_computation.4 | async-start | bytes 4194304 | tf_op jit(solution)/shard_map/all_to_all | solution.py:1039
  89.0 14.4 %collective-permute-start.12 = (bf16[4,128,1152]{2,1,0:T(8,128)(2,1)}, bf16[4,128,1152]{2,1,0:T(8,128)(2,1)}, u32[]{:S(2)}, u32[]{:S(2)}) collective-permute-start(bf16[4,128,1152]{2,1,0:T(8,128)(2,1)} %pairsnorm.1.refs_5_), channel_id=1, source_target_pairs={{0,1},{1,0},{2,3},{3,2},{4,5},{5,4},{6,7},{7,6},{8,9},{9,8},{10,11... | collective-permute-start | bytes 3538952 | tf_op jit(solution)/shard_map/ppermute | solution.py:1026
  89.5 8.7 %collective-permute-start.8 = (bf16[128,512]{1,0:T(8,128)(2,1)S(1)}, bf16[128,512]{1,0:T(8,128)(2,1)S(1)}, u32[]{:S(2)}, u32[]{:S(2)}) collective-permute-start(bf16[128,512]{1,0:T(8,128)(2,1)S(1)} %get-tuple-element.151.refs_1_), channel_id=1, source_target_pairs={{0,24},{8,0},{16,8},{24,16},{1,25},{9,1},{17,9},{25,17},{2,26},{10... | collective-permute-start | bytes 393224 | tf_op jit(solution)/shard_map/ppermute | solution.py:1022
  90.5 13.0 %collective-permute-start.7 = (bf16[128,512]{1,0:T(8,128)(2,1)S(1)}, bf16[128,512]{1,0:T(8,128)(2,1)S(1)}, u32[]{:S(2)}, u32[]{:S(2)}) collective-permute-start(bf16[128,512]{1,0:T(8,128)(2,1)S(1)} %get-tuple-element.151.refs_1_), channel_id=1, source_target_pairs={{0,16},{8,24},{16,0},{24,8},{1,17},{9,25},{17,1},{25,9},{2,18},{10... | collective-permute-start | bytes 393224 | tf_op jit(solution)/shard_map/ppermute | solution.py:1022
  91.6 11.8 %collective-permute-start.6 = (bf16[128,512]{1,0:T(8,128)(2,1)S(1)}, bf16[128,512]{1,0:T(8,128)(2,1)S(1)}, u32[]{:S(2)}, u32[]{:S(2)}) collective-permute-start(bf16[128,512]{1,0:T(8,128)(2,1)S(1)} %get-tuple-element.151.refs_1_), channel_id=1, source_target_pairs={{0,8},{8,16},{16,24},{24,0},{1,9},{9,17},{17,25},{25,1},{2,10},{10... | collective-permute-start | bytes 393224 | tf_op jit(solution)/shard_map/ppermute | solution.py:1022
  115.7 18.9 %all-to-all-start.5 = ((bf16[8,4,32,512]{3,2,1,0:T(8,128)(2,1)}), bf16[8,4,32,512]{3,2,1,0:T(8,128)(2,1)S(1)}, u32[]{:S(2)}, u32[]{:S(2)}) async-start(bf16[8,4,32,512]{3,2,1,0:T(8,128)(2,1)} %scatterright.1), calls=%async_computation.5 | async-start | bytes 2097152 | tf_op jit(solution)/shard_map/all_to_all | solution.py:1039
  121.3 21.9 %collective-permute-start.13 = (bf16[128,1024]{1,0:T(8,128)(2,1)}, bf16[128,1024]{1,0:T(8,128)(2,1)S(1)}, u32[]{:S(2)}, u32[]{:S(2)}) collective-permute-start(bf16[128,1024]{1,0:T(8,128)(2,1)} %get-tuple-element.164), channel_id=1, source_target_pairs={{0,24},{8,0},{16,8},{24,16},{1,25},{9,1},{17,9},{25,17},{2,26},{10... | collective-permute-start | bytes 786440 | tf_op jit(solution)/shard_map/ppermute | solution.py:1022
  122.2 25.0 %collective-permute-start.14 = (bf16[128,1024]{1,0:T(8,128)(2,1)}, bf16[128,1024]{1,0:T(8,128)(2,1)S(1)}, u32[]{:S(2)}, u32[]{:S(2)}) collective-permute-start(bf16[128,1024]{1,0:T(8,128)(2,1)} %get-tuple-element.165), channel_id=1, source_target_pairs={{0,16},{8,24},{16,0},{24,8},{1,17},{9,25},{17,1},{25,9},{2,18},{10... | collective-permute-start | bytes 786440 | tf_op jit(solution)/shard_map/ppermute | solution.py:1022
  123.4 23.8 %collective-permute-start.15 = (bf16[128,1024]{1,0:T(8,128)(2,1)}, bf16[128,1024]{1,0:T(8,128)(2,1)S(1)}, u32[]{:S(2)}, u32[]{:S(2)}) collective-permute-start(bf16[128,1024]{1,0:T(8,128)(2,1)} %get-tuple-element.166), channel_id=1, source_target_pairs={{0,8},{8,16},{16,24},{24,0},{1,9},{9,17},{17,25},{25,1},{2,10},{10... | collective-permute-start | bytes 786440 | tf_op jit(solution)/shard_map/ppermute | solution.py:1022
  140.6 10.0 %all-to-all-start.6 = ((bf16[32,8,128]{2,1,0:T(8,128)(2,1)}), bf16[32,8,128]{2,1,0:T(8,128)(2,1)S(1)}, u32[]{:S(2)}, u32[]{:S(2)}) async-start(bf16[32,8,128]{2,1,0:T(8,128)(2,1)} %bitcast.10), calls=%async_computation.6 | async-start | bytes 131072 | tf_op jit(solution)/shard_map/all_to_all | solution.py:1039
  158.6 10.4 %all-to-all-start.7 = ((bf16[8,128,128]{2,1,0:T(8,128)(2,1)}), bf16[8,128,128]{2,1,0:T(8,128)(2,1)S(1)}, u32[]{:S(2)}, u32[]{:S(2)}) async-start(bf16[8,128,128]{2,1,0:T(8,128)(2,1)} %get-tuple-element.174), calls=%async_computation.7 | async-start | bytes 524288 | tf_op jit(solution)/shard_map/all_to_all | solution.py:1039
  169.0 12.4 %all-to-all-start.8 = ((bf16[8,128,128]{2,1,0:T(8,128)(2,1)}), bf16[8,128,128]{2,1,0:T(8,128)(2,1)S(1)}, u32[]{:S(2)}, u32[]{:S(2)}) async-start(bf16[8,128,128]{2,1,0:T(8,128)(2,1)} %factors.1), calls=%async_computation.8 | async-start | bytes 524288 | tf_op jit(solution)/shard_map/all_to_all | solution.py:1039
  181.4 18.4 %all-to-all-start.9 = ((bf16[8,144,384]{2,1,0:T(8,128)(2,1)}), bf16[8,144,384]{2,1,0:T(8,128)(2,1)S(1)}, u32[]{:S(2)}, u32[]{:S(2)}) async-start(bf16[8,144,384]{2,1,0:T(8,128)(2,1)} %get-tuple-element.195), calls=%async_computation.9 | async-start | bytes 1769472 | tf_op jit(solution)/shard_map/all_to_all | solution.py:1039
  193.8 9.2 %collective-permute-start.24 = (bf16[4,128,128]{2,1,0:T(8,128)(2,1)S(1)}, bf16[4,128,128]{2,1,0:T(8,128)(2,1)S(1)}, u32[]{:S(2)}, u32[]{:S(2)}) collective-permute-start(bf16[4,128,128]{2,1,0:T(8,128)(2,1)S(1)} %stackearly.1.refs_0_), channel_id=1, source_target_pairs={{0,6},{1,7},{2,4},{3,5},{4,2},{5,3},{6,0},{7,1},{8,14},{9,15},{10,... | collective-permute-start | bytes 393224 | tf_op jit(solution)/shard_map/ppermute | solution.py:1026
  196.8 8.2 %collective-permute-start.23 = (bf16[4,128,128]{2,1,0:T(8,128)(2,1)S(1)}, bf16[4,128,128]{2,1,0:T(8,128)(2,1)S(1)}, u32[]{:S(2)}, u32[]{:S(2)}) collective-permute-start(bf16[4,128,128]{2,1,0:T(8,128)(2,1)S(1)} %stackearly.1.refs_0_), channel_id=1, source_target_pairs={{0,4},{1,5},{2,6},{3,7},{4,0},{5,1},{6,2},{7,3},{8,12},{9,13},{10,... | collective-permute-start | bytes 393224 | tf_op jit(solution)/shard_map/ppermute | solution.py:1026
  197.3 7.6 %collective-permute-start.22 = (bf16[4,128,128]{2,1,0:T(8,128)(2,1)S(1)}, bf16[4,128,128]{2,1,0:T(8,128)(2,1)S(1)}, u32[]{:S(2)}, u32[]{:S(2)}) collective-permute-start(bf16[4,128,128]{2,1,0:T(8,128)(2,1)S(1)} %stackearly.1.refs_0_), channel_id=1, source_target_pairs={{0,2},{1,3},{2,0},{3,1},{4,6},{5,7},{6,4},{7,5},{8,10},{9,11},{10,... | collective-permute-start | bytes 393224 | tf_op jit(solution)/shard_map/ppermute | solution.py:1026
  200.5 9.8 %collective-permute-start.18 = (bf16[96,128]{1,0:T(8,128)(2,1)S(1)}, bf16[96,128]{1,0:T(8,128)(2,1)S(1)}, u32[]{:S(2)}, u32[]{:S(2)}) collective-permute-start(bf16[96,128]{1,0:T(8,128)(2,1)S(1)} %late.1.refs_0_), channel_id=1, source_target_pairs={{0,24},{8,0},{16,8},{24,16},{1,25},{9,1},{17,9},{25,17},{2,26},{10... | collective-permute-start | bytes 73736 | tf_op jit(solution)/shard_map/ppermute | solution.py:1022
  203.0 7.4 %collective-permute-start.17 = (bf16[96,128]{1,0:T(8,128)(2,1)S(1)}, bf16[96,128]{1,0:T(8,128)(2,1)S(1)}, u32[]{:S(2)}, u32[]{:S(2)}) collective-permute-start(bf16[96,128]{1,0:T(8,128)(2,1)S(1)} %late.1.refs_0_), channel_id=1, source_target_pairs={{0,16},{8,24},{16,0},{24,8},{1,17},{9,25},{17,1},{25,9},{2,18},{10... | collective-permute-start | bytes 73736 | tf_op jit(solution)/shard_map/ppermute | solution.py:1022
  203.0 7.4 %collective-permute-start.16 = (bf16[96,128]{1,0:T(8,128)(2,1)S(1)}, bf16[96,128]{1,0:T(8,128)(2,1)S(1)}, u32[]{:S(2)}, u32[]{:S(2)}) collective-permute-start(bf16[96,128]{1,0:T(8,128)(2,1)S(1)} %late.1.refs_0_), channel_id=1, source_target_pairs={{0,8},{8,16},{16,24},{24,0},{1,9},{9,17},{17,25},{25,1},{2,10},{10... | collective-permute-start | bytes 73736 | tf_op jit(solution)/shard_map/ppermute | solution.py:1022
  211.1 7.0 %collective-permute-start.26 = (bf16[4,96,128]{2,1,0:T(8,128)(2,1)S(1)}, bf16[4,96,128]{2,1,0:T(8,128)(2,1)S(1)}, u32[]{:S(2)}, u32[]{:S(2)}) collective-permute-start(bf16[4,96,128]{2,1,0:T(8,128)(2,1)S(1)} %stacklate.1.refs_0_), channel_id=1, source_target_pairs={{0,4},{1,5},{2,6},{3,7},{4,0},{5,1},{6,2},{7,3},{8,12},{9,13},{10,... | collective-permute-start | bytes 294920 | tf_op jit(solution)/shard_map/ppermute | solution.py:1026
  (9 other events, 51.9 us)
